TPU v7x, 32 devices: a whole 2x2x4 slice. The times are simulated.
32 devices in a mesh: ctx: 8 (over y, x, core), wshard: 4 (over z).
Axes of the slice: x: 2, y: 2, z: 4, core: 2. Of those that a mesh axis runs over, the one named last changes fastest.
Arguments:
- byte_feats: bfloat16 [8, 2048, 768], P('wshard', 'ctx'), may hold values from -6 to 6
- lengths: int32 [8], P('wshard'), may hold values from 512 to 2048, as said below
- latent_array: bfloat16 [256, 1280], P('wshard'), may hold values from -6 to 6
- lat_gain: bfloat16 [1280], P('wshard'), may hold values from 0.5 to 1.5
- lat_bias: bfloat16 [1280], P('wshard'), may hold values from -4 to 4
- in_gain: bfloat16 [768], P('wshard'), may hold values from 0.5 to 1.5
- in_bias: bfloat16 [768], P('wshard'), may hold values from -4 to 4
- w_query: bfloat16 [1280, 256], P('wshard'), may hold values from -0.25 to 0.25
- w_key: bfloat16 [768, 256], P('wshard'), may hold values from -0.3125 to 0.3125
- w_value: bfloat16 [768, 1280], P('wshard'), may hold values from -0.21875 to 0.21875
- w_output: bfloat16 [1280, 1280], P('wshard'), may hold values from -2 to 2
- mlp_gain: bfloat16 [1280], P('wshard'), may hold values from 0.5 to 1.5
- mlp_bias: bfloat16 [1280], P('wshard'), may hold values from -4 to 4
- w_up: bfloat16 [1280, 1280], P('wshard'), may hold values from -0.15625 to 0.15625
- w_down: bfloat16 [1280, 1280], P('wshard'), may hold values from -0.15625 to 0.15625
- cotangent: bfloat16 [8, 256, 1280], P('wshard'), may hold values from -6 to 6
Outputs:
- latents_out: bfloat16 [8, 256, 1280], P('wshard')
- byte_grad: bfloat16 [8, 2048, 768], P('wshard', 'ctx')
- grad_latent: float32 [256, 1280], P('wshard')
- grad_lat_gain: float32 [1280], P('wshard')
- grad_lat_bias: float32 [1280], P('wshard')
- grad_in_gain: float32 [768], P('wshard')
- grad_in_bias: float32 [768], P('wshard')
- grad_query: float32 [1280, 256], P('wshard')
- grad_key: float32 [768, 256], P('wshard')
- grad_value: float32 [768, 1280], P('wshard')
- grad_output: float32 [1280, 1280], P('wshard')
- grad_mlp_gain: float32 [1280], P('wshard')
- grad_mlp_bias: float32 [1280], P('wshard')
- grad_up: float32 [1280, 1280], P('wshard')
- grad_down: float32 [1280, 1280], P('wshard')
Inputs may be any that keep to these rules, and one draw needn't show every extreme that they name: The first lengths[s] slots of sequence s hold bytes, the rest are padding; some sequence fills all 2048 slots.
All inputs are finite; a program needn't handle non-finite values.
Results may differ from a plain program's by a relative error of at most 0.019.
Values may be sent and summed in bfloat16 or wider, within the bound.
A program may use at most 256 MiB of HBM per device.

v0:
```python
import math

import jax
import jax.numpy as jnp
from jax import lax
from jax.sharding import PartitionSpec as P

H = 8


def layer_norm(values, gain, offset):
    center = jnp.mean(values, axis=-1, keepdims=True)
    centred = values - center
    variance = jnp.mean(centred * centred, axis=-1, keepdims=True)
    return centred * lax.rsqrt(variance + 1e-05) * gain + offset


def exact_gelu(values):
    return jax.nn.gelu(values, approximate=False)


def matmul(left, right):
    return jnp.dot(left, right, preferred_element_type=jnp.float32)


def combine(first, second):
    top_first, sum_first, num_first = first
    top_second, sum_second, num_second = second
    highest = jnp.maximum(top_first, top_second)
    weight_first = jnp.exp(top_first - highest)
    weight_second = jnp.exp(top_second - highest)
    return (
        highest,
        sum_first * weight_first + sum_second * weight_second,
        num_first * weight_first[..., None] + num_second * weight_second[..., None],
    )


def block_stats(queries, keys, values, start, length, score_scale):
    row_count = keys.shape[0]
    head_count = queries.shape[1]
    kheads = keys.reshape(row_count, head_count, -1)
    vheads = values.reshape(row_count, head_count, -1)
    scores = (
        jnp.einsum("lhd,khd->hlk", queries, kheads, preferred_element_type=jnp.float32)
        * score_scale
    )
    valid = start + lax.iota(jnp.int32, row_count) < length
    masked = jnp.where(valid, scores, -1e30)
    highest = jnp.max(masked, axis=-1)
    weights = jnp.where(valid, jnp.exp(masked - highest[..., None]), 0.0)
    numer = jnp.einsum(
        "hlk,khe->hle", weights.astype(jnp.bfloat16), vheads, preferred_element_type=jnp.float32
    )
    return (highest, jnp.sum(weights, axis=-1), numer)


def query_part(queries, grad_heads, log_total, delta, keys, values, start, length, score_scale):
    row_count = keys.shape[0]
    head_count = queries.shape[1]
    kheads = keys.reshape(row_count, head_count, -1)
    vheads = values.reshape(row_count, head_count, -1)
    scores = (
        jnp.einsum("lhd,khd->hlk", queries, kheads, preferred_element_type=jnp.float32)
        * score_scale
    )
    valid = start + lax.iota(jnp.int32, row_count) < length
    probs = jnp.where(valid, jnp.exp(scores - log_total[..., None]), 0.0)
    dprobs = jnp.einsum("lhe,khe->hlk", grad_heads, vheads, preferred_element_type=jnp.float32)
    dscores = (probs * (dprobs - delta[..., None])).astype(jnp.bfloat16)
    dquery = (
        jnp.einsum("hlk,khd->lhd", dscores, kheads, preferred_element_type=jnp.float32)
        * score_scale
    )
    return (dquery, dscores, probs)


def blocked(block_fn, carry, keys, values):
    row_count = keys.shape[0]
    block_size = math.gcd(row_count, 1024)
    block_count = row_count // block_size
    key_blocks = keys.reshape(block_count, block_size, keys.shape[1])
    value_blocks = values.reshape(block_count, block_size, values.shape[1])

    def scan_step(carried, block_item):
        key_block, value_block, offset = block_item
        return (block_fn(carried, key_block, value_block, offset * block_size), None)

    result, _ = lax.scan(
        scan_step, carry, (key_blocks, value_blocks, jnp.arange(block_count, dtype=jnp.int32))
    )
    return result


def shards(
    byte_feats,
    lengths,
    latent_array,
    lat_gain,
    lat_bias,
    in_gain,
    in_bias,
    w_query,
    w_key,
    w_value,
    w_output,
    mlp_gain,
    mlp_bias,
    w_up,
    w_down,
    cotangent,
):
    head_count = H
    micro_count = byte_feats.shape[0]
    slot_count = byte_feats.shape[1]
    key_start = lax.axis_index("ctx") * slot_count
    latent_outs = []
    byte_grads = []
    totals = None
    for micro_step in range(micro_count):
        gathered = (
            lax.all_gather(latent_array, "wshard", axis=0, tiled=True),
            lax.all_gather(lat_gain, "wshard", axis=0, tiled=True),
            lax.all_gather(lat_bias, "wshard", axis=0, tiled=True),
            lax.all_gather(in_gain, "wshard", axis=0, tiled=True),
            lax.all_gather(in_bias, "wshard", axis=0, tiled=True),
            lax.all_gather(w_query, "wshard", axis=0, tiled=True),
            lax.all_gather(w_key, "wshard", axis=0, tiled=True),
            lax.all_gather(w_value, "wshard", axis=0, tiled=True),
            lax.all_gather(w_output, "wshard", axis=0, tiled=True),
            lax.all_gather(mlp_gain, "wshard", axis=0, tiled=True),
            lax.all_gather(mlp_bias, "wshard", axis=0, tiled=True),
            lax.all_gather(w_up, "wshard", axis=0, tiled=True),
            lax.all_gather(w_down, "wshard", axis=0, tiled=True),
        )
        (
            latent,
            gain_lat,
            bias_lat,
            gain_in,
            bias_in,
            query_w,
            key_w,
            value_w,
            output_w,
            gain_mlp,
            bias_mlp,
            up_w,
            down_w,
        ) = gathered
        length = lengths[micro_step]
        features = byte_feats[micro_step].astype(jnp.float32)
        normed_in, in_back = jax.vjp(
            layer_norm, features, gain_in.astype(jnp.float32), bias_in.astype(jnp.float32)
        )
        input_low = normed_in.astype(jnp.bfloat16)
        keys = matmul(input_low, key_w).astype(jnp.bfloat16)
        values = matmul(input_low, value_w).astype(jnp.bfloat16)
        latent_full = latent.astype(jnp.float32)
        normed_lat, lat_back = jax.vjp(
            layer_norm, latent_full, gain_lat.astype(jnp.float32), bias_lat.astype(jnp.float32)
        )
        lat_low = normed_lat.astype(jnp.bfloat16)
        head_size = query_w.shape[1] // head_count
        score_scale = 1.0 / math.sqrt(head_size)
        queries = matmul(lat_low, query_w).astype(jnp.bfloat16).reshape(-1, head_count, head_size)
        lat_rows = queries.shape[0]
        value_head = values.shape[1] // head_count
        empty = (
            jnp.full((head_count, lat_rows), -1e30, jnp.float32),
            jnp.zeros((head_count, lat_rows), jnp.float32),
            jnp.zeros((head_count, lat_rows, value_head), jnp.float32),
        )

        def add_block(carried, key_block, value_block, block_start):
            return combine(
                carried,
                block_stats(queries, key_block, value_block, block_start, length, score_scale),
            )

        highest, total, numer = blocked(
            add_block,
            empty,
            lax.all_gather(keys, "ctx", axis=0, tiled=True),
            lax.all_gather(values, "ctx", axis=0, tiled=True),
        )
        attended = numer / total[..., None]
        log_total = highest + jnp.log(total)
        att_low = jnp.transpose(attended, (1, 0, 2)).reshape(lat_rows, -1).astype(jnp.bfloat16)
        hidden = latent_full + matmul(att_low, output_w)
        normed_mid, mid_back = jax.vjp(
            layer_norm, hidden, gain_mlp.astype(jnp.float32), bias_mlp.astype(jnp.float32)
        )
        mid_low = normed_mid.astype(jnp.bfloat16)
        upward = matmul(mid_low, up_w)
        activated, gelu_back = jax.vjp(exact_gelu, upward)
        act_low = activated.astype(jnp.bfloat16)
        result = hidden + matmul(act_low, down_w)
        latent_outs.append(result.astype(jnp.bfloat16))
        dout = cotangent[micro_step].astype(jnp.float32)
        dout_low = dout.astype(jnp.bfloat16)
        grad_down = matmul(act_low.T, dout_low)
        grad_act = matmul(dout_low, down_w.T)
        (grad_upward,) = gelu_back(grad_act)
        up_low = grad_upward.astype(jnp.bfloat16)
        grad_upw = matmul(mid_low.T, up_low)
        grad_mid = matmul(up_low, up_w.T)
        dhid_norm, grad_gmlp, grad_bmlp = mid_back(grad_mid)
        dhidden = dout + dhid_norm
        dhid_low = dhidden.astype(jnp.bfloat16)
        grad_outw = matmul(att_low.T, dhid_low)
        grad_att = matmul(dhid_low, output_w.T).astype(jnp.bfloat16)
        grad_heads = grad_att.reshape(lat_rows, head_count, value_head)
        delta = jnp.sum(
            jnp.transpose(grad_heads.astype(jnp.float32), (1, 0, 2)) * attended, axis=-1
        )
        dquery_local, dscores, probs = query_part(
            queries, grad_heads, log_total, delta, keys, values, key_start, length, score_scale
        )
        dkeys = (
            (
                jnp.einsum("hlk,lhd->khd", dscores, queries, preferred_element_type=jnp.float32)
                * score_scale
            )
            .astype(jnp.bfloat16)
            .reshape(slot_count, -1)
        )
        dvalues = (
            jnp.einsum(
                "hlk,lhe->khe",
                probs.astype(jnp.bfloat16),
                grad_heads,
                preferred_element_type=jnp.float32,
            )
            .astype(jnp.bfloat16)
            .reshape(slot_count, -1)
        )

        def fold_add_block(carried, key_block, value_block, block_start):
            return (
                carried
                + query_part(
                    queries,
                    grad_heads,
                    log_total,
                    delta,
                    key_block,
                    value_block,
                    block_start,
                    length,
                    score_scale,
                )[0]
            )

        dquery = blocked(
            fold_add_block,
            jnp.zeros((lat_rows, head_count, head_size), jnp.float32),
            lax.all_gather(keys, "ctx", axis=0, tiled=True),
            lax.all_gather(values, "ctx", axis=0, tiled=True),
        )
        dquery_low = dquery.reshape(lat_rows, -1).astype(jnp.bfloat16)
        grad_qw = matmul(lat_low.T, dquery_low)
        dnorm_lat = matmul(dquery_low, query_w.T)
        dlat_norm, grad_glat, grad_blat = lat_back(dnorm_lat)
        grad_lat = dhidden + dlat_norm
        grad_kw = matmul(input_low.T, dkeys)
        grad_vw = matmul(input_low.T, dvalues)
        dnorm_in = matmul(dkeys, key_w.T) + matmul(dvalues, value_w.T)
        dfeatures, grad_gin, grad_bin = in_back(dnorm_in)
        byte_grads.append(dfeatures.astype(jnp.bfloat16))
        step_grads = [
            grad_lat,
            grad_glat,
            grad_blat,
            grad_gin,
            grad_bin,
            grad_qw,
            grad_kw,
            grad_vw,
            grad_outw,
            grad_gmlp,
            grad_bmlp,
            grad_upw,
            grad_down,
        ]
        if totals is None:
            totals = step_grads
        else:
            totals = [older + newer for older, newer in zip(totals, step_grads)]
    shares = (
        lax.psum_scatter(
            totals[0].astype(jnp.bfloat16), "wshard", scatter_dimension=0, tiled=True
        ).astype(jnp.float32),
        lax.psum_scatter(
            totals[1].astype(jnp.bfloat16), "wshard", scatter_dimension=0, tiled=True
        ).astype(jnp.float32),
        lax.psum_scatter(
            totals[2].astype(jnp.bfloat16), "wshard", scatter_dimension=0, tiled=True
        ).astype(jnp.float32),
        lax.psum_scatter(
            totals[3].astype(jnp.bfloat16), "wshard", scatter_dimension=0, tiled=True
        ).astype(jnp.float32),
        lax.psum_scatter(
            totals[4].astype(jnp.bfloat16), "wshard", scatter_dimension=0, tiled=True
        ).astype(jnp.float32),
        lax.psum_scatter(
            totals[5].astype(jnp.bfloat16), "wshard", scatter_dimension=0, tiled=True
        ).astype(jnp.float32),
        lax.psum_scatter(
            totals[6].astype(jnp.bfloat16), "wshard", scatter_dimension=0, tiled=True
        ).astype(jnp.float32),
        lax.psum_scatter(
            totals[7].astype(jnp.bfloat16), "wshard", scatter_dimension=0, tiled=True
        ).astype(jnp.float32),
        lax.psum_scatter(
            totals[8].astype(jnp.bfloat16), "wshard", scatter_dimension=0, tiled=True
        ).astype(jnp.float32),
        lax.psum_scatter(
            totals[9].astype(jnp.bfloat16), "wshard", scatter_dimension=0, tiled=True
        ).astype(jnp.float32),
        lax.psum_scatter(
            totals[10].astype(jnp.bfloat16), "wshard", scatter_dimension=0, tiled=True
        ).astype(jnp.float32),
        lax.psum_scatter(
            totals[11].astype(jnp.bfloat16), "wshard", scatter_dimension=0, tiled=True
        ).astype(jnp.float32),
        lax.psum_scatter(
            totals[12].astype(jnp.bfloat16), "wshard", scatter_dimension=0, tiled=True
        ).astype(jnp.float32),
    )
    summed = (
        lax.psum(shares[3].astype(jnp.bfloat16), "ctx").astype(jnp.float32),
        lax.psum(shares[4].astype(jnp.bfloat16), "ctx").astype(jnp.float32),
        lax.psum(shares[6].astype(jnp.bfloat16), "ctx").astype(jnp.float32),
        lax.psum(shares[7].astype(jnp.bfloat16), "ctx").astype(jnp.float32),
    )
    return (
        jnp.stack(latent_outs),
        jnp.stack(byte_grads),
        shares[0],
        shares[1],
        shares[2],
        summed[0],
        summed[1],
        shares[5],
        summed[2],
        summed[3],
        shares[8],
        shares[9],
        shares[10],
        shares[11],
        shares[12],
    )


def solution(mesh):
    placed = (
        P("wshard", "ctx", None),
        P("wshard"),
        P("wshard", None),
        P("wshard"),
        P("wshard"),
        P("wshard"),
        P("wshard"),
        P("wshard", None),
        P("wshard", None),
        P("wshard", None),
        P("wshard", None),
        P("wshard"),
        P("wshard"),
        P("wshard", None),
        P("wshard", None),
        P("wshard", None, None),
    )
    return jax.shard_map(
        shards,
        mesh=mesh,
        in_specs=placed,
        out_specs=(
            P("wshard", None, None),
            P("wshard", "ctx", None),
            P("wshard", None),
            P("wshard"),
            P("wshard"),
            P("wshard"),
            P("wshard"),
            P("wshard", None),
            P("wshard", None),
            P("wshard", None),
            P("wshard", None),
            P("wshard"),
            P("wshard"),
            P("wshard", None),
            P("wshard", None),
        ),
        check_vma=False,
    )
```

profile of v0, /device:TPU:0, one launch (start us, length us, event | category | flops | bytes accessed | tf_op | source)
XLA Modules:
  0.0 846.3 jit_solution(12040518271220998177)
XLA Ops:
  15.8 21.7 %all-reduce.15 = (bf16[768]{0:T(1024)(128)(2,1)S(1)}, bf16[768]{0:T(1024)(128)(2,1)S(1)}, bf16[1280]{0:T(1024)(128)(2,1)S(1)}, bf16[1280]{0:T(1024)(128)(2,1)S(1...) all-reduce(bf16[768]{0:T(1024)(128)(2,1)S(1)} %dynamic-update-slice, ...), channel_id=1, replica_groups=mesh['ctx'=8,'wshard'=4] {'wshard'}, use_global_device_ids=true, to_apply=%add.1 | all-reduce | flops 6656 | bytes 26624
  38.8 17.7 %all_gather.71 = bf16[768,256]{1,0:T(8,128)(2,1)S(1)} all-gather(bf16[192,256]{1,0:T(8,128)(2,1)S(1)} %copy-done.57), channel_id=1, replica_groups=mesh['ctx'=8,'wshard'=4] {'wshard'}, dimensions={0}, use_global_device_ids=true | all-gather | bytes 491520 | tf_op jit(solution)/shard_map/all_gather | solution.py:128
  59.3 3.7 all-gather.11.cloned.1.call-done
  63.1 3.3 convolution_convert_fusion
  71.0 17.1 %all_gather.68 = bf16[256,1280]{1,0:T(8,128)(2,1)S(1)} all-gather(bf16[64,1280]{1,0:T(8,128)(2,1)S(1)} %copy-done.53), channel_id=1, replica_groups=mesh['ctx'=8,'wshard'=4] {'wshard'}, dimensions={0}, use_global_device_ids=true | all-gather | bytes 819200 | tf_op jit(solution)/shard_map/all_gather | solution.py:122
  88.6 15.9 %all_gather.75 = bf16[1280,256]{1,0:T(8,128)(2,1)S(1)} all-gather(bf16[320,256]{1,0:T(8,128)(2,1)S(1)} %copy-done.54), channel_id=1, replica_groups=mesh['ctx'=8,'wshard'=4] {'wshard'}, dimensions={0}, use_global_device_ids=true | all-gather | bytes 819200 | tf_op jit(solution)/shard_map/all_gather | solution.py:127
  108.4 5.1 all-gather.9.cloned.1.call-done
  119.2 37.8 %all-gather.23.cloned.1.call-done = bf16[2048,1280]{1,0:T(8,128)(2,1)} async-done(((bf16[256,1280]{1,0:T(8,128)(2,1)}), bf16[2048,1280]{1,0:T(8,128)(2,1)}) %all-gather.23.cloned.1.call-update) | async-done | bytes 5242896 | tf_op jit(solution)/shard_map/all_gather | solution.py:185
  157.0 8.1 copy.70
  165.1 35.3 %all-gather.13.cloned.1.call-done = bf16[2048,1280]{1,0:T(8,128)(2,1)} async-done(((bf16[256,1280]{1,0:T(8,128)(2,1)}), bf16[2048,1280]{1,0:T(8,128)(2,1)}) %all-gather.13.cloned.1.call-update) | async-done | bytes 5242896 | tf_op jit(solution)/shard_map/all_gather | solution.py:185
  200.4 8.0 copy.68
  208.4 25.4 %while.53 = (s32[]{:T(128)}, f32[8,256]{1,0:T(8,128)S(1)}, f32[8,256]{1,0:T(8,128)S(1)}, f32[8,256,160]{1,2,0:T(8,128)}, s32[2]{0:T(128)S(1)}, /*index=5*/s32[]{...) while((s32[]{:T(128)}, f32[8,256]{1,0:T(8,128)S(1)}, ...), condition=%wide.region_15.16_spmd.clone, body=%wide.region_12.15_spmd.clone.sunk | while | flops 833894400 | bytes 47960292 | solution.py:89
  210.3 2.2 constant_dynamic-slice_fusion.19
  212.5 2.3 bitcast_reduce_fusion.5
  214.9 2.6 fusion.322
  217.5 2.6 fusion.324
  225.1 2.3 bitcast_reduce_fusion.5
  227.5 2.6 fusion.322
  230.1 2.6 fusion.324
  234.8 25.6 %while.52 = (s32[]{:T(128)}, f32[8,256]{1,0:T(8,128)S(1)}, f32[8,256]{1,0:T(8,128)S(1)}, f32[8,256,160]{1,2,0:T(8,128)}, s32[2]{0:T(128)S(1)}, /*index=5*/s32[]{...) while((s32[]{:T(128)}, f32[8,256]{1,0:T(8,128)S(1)}, ...), condition=%wide.region_7.8_spmd.clone, body=%wide.region_4.7_spmd.clone.sunk | while | flops 833894400 | bytes 47960292 | solution.py:89
  238.8 2.3 bitcast_reduce_fusion.4
  241.1 2.6 fusion.315
  243.7 2.6 fusion.317
  251.5 2.3 bitcast_reduce_fusion.4
  253.8 2.6 fusion.315
  256.4 2.6 fusion.317
  260.4 2.3 fusion.149
  262.7 4.9 all-gather.15.cloned.1.call-done
  267.5 3.4 fusion.196
  275.5 58.0 %all-gather.17.cloned.1.call-done = bf16[1280,1280]{1,0:T(8,128)(2,1)} async-done(((bf16[320,1280]{1,0:T(8,128)(2,1)}), bf16[1280,1280]{1,0:T(8,128)(2,1)}) %all-gather.17.cloned.1.call-update) | async-done | bytes 3276816 | tf_op jit(solution)/shard_map/all_gather | solution.py:133
  333.4 7.7 multiply_convert_fusion.18
  341.2 5.4 multiply_convert_fusion.19
  346.6 52.8 %all-gather.19.cloned.1.call-done = bf16[1280,1280]{1,0:T(8,128)(2,1)} async-done(((bf16[320,1280]{1,0:T(8,128)(2,1)}), bf16[1280,1280]{1,0:T(8,128)(2,1)}) %all-gather.19.cloned.1.call-update) | async-done | bytes 3276816 | tf_op jit(solution)/shard_map/all_gather | solution.py:134
  399.3 4.2 add_convert_fusion.2
  427.6 34.5 %while.55 = (s32[]{:T(128)}, f32[256,8,32]{0,2,1:T(8,128)S(1)}, bf16[2,1024,256]{1,2,0:T(8,128)(2,1)}, s32[2]{0:T(128)S(1)}, s32[]{:T(128)}, /*index=5*/bf16[256...) while((s32[]{:T(128)}, f32[256,8,32]{0,2,1:T(8,128)S(1)}, ...), condition=%wide.region_33.34_spmd.clone, body=%wide.region_32.33_spmd.clone.sunk | while | flops 952305664 | bytes 27543732 | solution.py:89
  433.5 4.7 fusion.337
  438.3 6.7 fusion.338
  450.7 4.7 fusion.337
  455.5 6.7 fusion.338
  464.1 2.6 fusion.98
  466.8 2.3 fusion.174
  471.2 2.6 fusion.99
  473.9 2.5 fusion.95
  479.4 2.2 fusion.57
  482.6 30.5 %while.54 = (s32[]{:T(128)}, f32[256,8,32]{0,2,1:T(8,128)S(1)}, bf16[2,1024,256]{1,2,0:T(8,128)(2,1)S(1)}, s32[2]{0:T(128)S(1)}, s32[]{:T(128)}, /*index=5*/bf16...) while((s32[]{:T(128)}, f32[256,8,32]{0,2,1:T(8,128)S(1)}, ...), condition=%wide.region_29.30_spmd.clone, body=%wide.region_28.29_spmd.clone.sunk | while | flops 952305664 | bytes 27543732 | solution.py:89
  486.8 4.8 fusion.330
  491.6 6.4 fusion.331
  501.9 4.8 fusion.330
  506.7 6.4 fusion.331
  523.0 5.2 fusion.178
  528.2 9.5 %reduce-scatter.14.cloned.1.call-done = bf16[192,1280]{1,0:T(8,128)(2,1)} async-done(((bf16[768,1280]{1,0:T(8,128)(2,1)}), bf16[192,1280]{1,0:T(8,128)(2,1)}) %reduce-scatter.14.cloned.1.call-update) | async-done | bytes 491536 | tf_op jit(solution)/shard_map/reduce_scatter | solution.py:312
  537.9 5.7 fusion.55
  546.9 2.8 fusion.54
  550.8 2.3 fusion.143
  553.1 2.8 fusion.56
  562.5 17.7 %all-reduce.14 = (bf16[1280]{0:T(1024)(128)(2,1)S(1)}, bf16[1280]{0:T(1024)(128)(2,1)S(1)}, bf16[768]{0:T(1024)(128)(2,1)S(1)}, bf16[768]{0:T(1024)(128)(2,1)S(1...) all-reduce(bf16[1280]{0:T(1024)(128)(2,1)S(1)} %add_convert_fusion., ...), channel_id=3, replica_groups=mesh['ctx'=8,'wshard'=4] {'wshard'}, use_global_device_ids=true, to_apply=%region_39.40.clone | all-reduce | flops 6656 | bytes 26624
  580.4 12.0 %all-reduce.12 = (bf16[192]{0:T(256)(128)(2,1)S(1)}, bf16[192]{0:T(256)(128)(2,1)S(1)}) all-reduce(bf16[192]{0:T(256)(128)(2,1)S(1)} %dynamic-slice.11, bf16[192]{0:T(256)(128)(2,1)S(1)} %dynamic-slice.13), channel_id=1, replica_groups=mesh['ctx'=8,'wshard'=4] {'ctx'}, use_global_device_ids=true, to_apply=%region_46.47 | all-reduce | flops 384 | bytes 1536 | tf_op jit(solution)/shard_map/psum | solution.py:332
  607.2 36.8 %all-reduce.18.cloned.1.call-done = (bf16[192,256]{1,0:T(8,128)(2,1)}, bf16[192,1280]{1,0:T(8,128)(2,1)}) async-done(((bf16[192,256]{1,0:T(8,128)(2,1)}, bf16[192,1280]{1,0:T(8,128)(2,1)}), (bf16[192,256]{1,0:T(8,128)(2,1)}, bf16[192,1280]{1,0:T(8,128)(2,1)})) %all-reduce.18.cloned.1.call-update) | async-done | bytes 589840 | tf_op jit(solution)/shard_map/psum | solution.py:334
  647.6 60.1 %reduce-scatter.18.cloned.1.call-done = bf16[320,1280]{1,0:T(8,128)(2,1)} async-done(((bf16[1280,1280]{1,0:T(8,128)(2,1)}), bf16[320,1280]{1,0:T(8,128)(2,1)}) %reduce-scatter.18.cloned.1.call-update) | async-done | bytes 819216 | tf_op jit(solution)/shard_map/reduce_scatter | solution.py:324
  707.7 2.4 convert_element_type.382
  710.1 62.2 %reduce-scatter.16.cloned.1.call-done = bf16[320,1280]{1,0:T(8,128)(2,1)} async-done(((bf16[1280,1280]{1,0:T(8,128)(2,1)}), bf16[320,1280]{1,0:T(8,128)(2,1)}) %reduce-scatter.16.cloned.1.call-update) | async-done | bytes 819216 | tf_op jit(solution)/shard_map/reduce_scatter | solution.py:315
  772.3 2.4 convert_element_type.376
  774.8 62.2 %reduce-scatter.20.cloned.1.call-done = bf16[320,1280]{1,0:T(8,128)(2,1)} async-done(((bf16[1280,1280]{1,0:T(8,128)(2,1)}), bf16[320,1280]{1,0:T(8,128)(2,1)}) %reduce-scatter.20.cloned.1.call-update) | async-done | bytes 819216 | tf_op jit(solution)/shard_map/reduce_scatter | solution.py:327
  836.9 2.4 convert_element_type.384
  (455 shorter events, 132.5 us)
Async XLA Ops:
  7.2 49.4 %copy-start.3 = (bf16[2,256,768]{2,1,0:T(8,128)(2,1)S(1)}, bf16[2,256,768]{2,1,0:T(8,128)(2,1)}, u32[]{:S(2)}) copy-start(bf16[2,256,768]{2,1,0:T(8,128)(2,1)} %param.24) | copy-start | bytes 2359300
  7.2 31.6 %copy-start.57 = (bf16[192,256]{1,0:T(8,128)(2,1)S(1)}, bf16[192,256]{1,0:T(8,128)(2,1)}, u32[]{:S(2)}) copy-start(bf16[192,256]{1,0:T(8,128)(2,1)} %param.32) | copy-start | bytes 294916
  7.2 55.9 %all-gather.11.cloned.1.call-start = ((), (), s32[]{:S(2)}) async-start(), calls=%async_computation.8 | async-start | bytes 2457600 | tf_op jit(solution)/shard_map/all_gather | solution.py:129
  7.9 99.1 %all-gather.21.cloned.1.call-start = ((), (), s32[]{:S(2)}) async-start(), calls=%async_computation.13 | async-start | bytes 1179648 | tf_op jit(solution)/shard_map/all_gather | solution.py:184
  37.5 28.9 %copy-start.65 = (f32[768]{0:T(1024)}, f32[768]{0:T(1024)S(1)}, u32[]{:S(2)}) copy-start(f32[768]{0:T(1024)S(1)} %convert_element_type.302) | copy-start | bytes 9220
  37.5 28.9 %copy-start.60 = (f32[768]{0:T(1024)}, f32[768]{0:T(1024)S(1)}, u32[]{:S(2)}) copy-start(f32[768]{0:T(1024)S(1)} %convert_element_type.301) | copy-start | bytes 9220
  56.5 6.6 copy-start.78
  56.5 9.9 %copy-start.81 = (f32[256]{0:T(256)}, f32[256]{0:T(256)S(1)}, u32[]{:S(2)}) copy-start(f32[256]{0:T(256)S(1)} %get-tuple-element.636) | copy-start | bytes 3076
  56.9 6.1 copy-start.87
  58.1 55.4 %all-gather.9.cloned.1.call-start = ((), (), s32[]{:S(2)}) async-start(), calls=%async_computation.7 | async-start | bytes 1179648 | tf_op jit(solution)/shard_map/all_gather | solution.py:184
  58.1 8.3 copy-start.90
  59.3 97.7 %all-gather.23.cloned.1.call-start = ((), (), s32[]{:S(2)}) async-start(), calls=%async_computation.14 | async-start | bytes 5898240 | tf_op jit(solution)/shard_map/all_gather | solution.py:185
  63.1 3.4 copy-start.37
  66.4 134.0 %all-gather.13.cloned.1.call-start = ((), (), s32[]{:S(2)}) async-start(), calls=%async_computation.9 | async-start | bytes 5898240 | tf_op jit(solution)/shard_map/all_gather | solution.py:185
  68.1 2.9 copy-start.53
  68.1 199.4 %all-gather.15.cloned.1.call-start = ((), (), s32[]{:S(2)}) async-start(), calls=%async_computation.10 | async-start | bytes 4096000 | tf_op jit(solution)/shard_map/all_gather | solution.py:130
  68.7 264.7 %all-gather.17.cloned.1.call-start = ((), (), s32[]{:S(2)}) async-start(), calls=%async_computation.11 | async-start | bytes 4096000 | tf_op jit(solution)/shard_map/all_gather | solution.py:133
  69.5 329.9 %all-gather.19.cloned.1.call-start = ((), (), s32[]{:S(2)}) async-start(), calls=%async_computation.12 | async-start | bytes 4096000 | tf_op jit(solution)/shard_map/all_gather | solution.py:134
  70.2 18.4 %copy-start.54 = (bf16[320,256]{1,0:T(8,128)(2,1)S(1)}, bf16[320,256]{1,0:T(8,128)(2,1)}, u32[]{:S(2)}) copy-start(bf16[320,256]{1,0:T(8,128)(2,1)} %param.31) | copy-start | bytes 491524
  70.2 458.0 %reduce-scatter.12.cloned.1.call-start = ((), (), s32[]{:S(2)}) async-start(), calls=%async_computation.17 | async-start | bytes 491520 | tf_op jit(solution)/shard_map/reduce_scatter | solution.py:309
  71.0 35.5 %copy-start.48 = (f32[1280]{0:T(1024)}, f32[1280]{0:T(1024)S(1)}, u32[]{:S(2)}) copy-start(f32[1280]{0:T(1024)S(1)} %convert_element_type.305) | copy-start | bytes 15364
  71.0 35.5 %copy-start.58 = (f32[1280]{0:T(1024)}, f32[1280]{0:T(1024)S(1)}, u32[]{:S(2)}) copy-start(f32[1280]{0:T(1024)S(1)} %convert_element_type.306) | copy-start | bytes 15364
  88.3 18.8 %copy-start.63 = (f32[256]{0:T(256)}, f32[256]{0:T(256)S(1)}, u32[]{:S(2)}) copy-start(f32[256]{0:T(256)S(1)} %broadcast_multiply_fusion.2) | copy-start | bytes 3076
  88.6 18.4 %copy-start.97 = (f32[256]{0:T(256)}, f32[256]{0:T(256)S(1)}, u32[]{:S(2)}) copy-start(f32[256]{0:T(256)S(1)} %fusion.80) | copy-start | bytes 3076
  88.6 18.4 %copy-start.75 = (f32[256]{0:T(256)}, f32[256]{0:T(256)S(1)}, u32[]{:S(2)}) copy-start(f32[256]{0:T(256)S(1)} %fusion.162) | copy-start | bytes 3076
  104.6 3.8 copy-start.17
  214.9 2.6 copy-start.23
  267.5 5.3 copy-start.118
  270.9 138.7 %copy-start.1 = (f32[256,1280]{1,0:T(8,128)}, f32[256,1280]{1,0:T(8,128)S(1)}, u32[]{:S(2)}) copy-start(f32[256,1280]{1,0:T(8,128)S(1)} %get-tuple-element.630) | copy-start | bytes 3932164
  271.0 138.7 %copy-start.77 = (f32[256]{0:T(256)}, f32[256]{0:T(256)S(1)}, u32[]{:S(2)}) copy-start(f32[256]{0:T(256)S(1)} %broadcast_multiply_fusion.1) | copy-start | bytes 3076
  274.1 135.6 %copy-start.84 = (f32[256]{0:T(256)}, f32[256]{0:T(256)S(1)}, u32[]{:S(2)}) copy-start(f32[256]{0:T(256)S(1)} %broadcast_multiply_fusion) | copy-start | bytes 3076
  275.4 134.3 %copy-start.86 = (f32[256]{0:T(256)}, f32[256]{0:T(256)S(1)}, u32[]{:S(2)}) copy-start(f32[256]{0:T(256)S(1)} %fusion.163) | copy-start | bytes 3076
  275.4 134.3 %copy-start.99 = (f32[256]{0:T(256)}, f32[256]{0:T(256)S(1)}, u32[]{:S(2)}) copy-start(f32[256]{0:T(256)S(1)} %fusion.165) | copy-start | bytes 3076
  275.4 143.7 %copy-start.105 = (f32[8,256]{1,0:T(8,128)}, f32[8,256]{1,0:T(8,128)S(1)}, u32[]{:S(2)}) copy-start(f32[8,256]{1,0:T(8,128)S(1)} %log_add_fusion.1) | copy-start | bytes 24580
  333.4 7.7 copy-start.121
  399.3 4.2 copy-start.122
  399.3 5.3 copy-start.123
  399.3 5.3 copy-start.124
  403.6 2.6 copy-start.116
  410.5 3.3 copy-start.119
  411.9 9.4 %copy-start.32 = (bf16[256,1280]{1,0:T(8,128)(2,1)}, bf16[256,1280]{1,0:T(8,128)(2,1)S(1)}, u32[]{:S(2)}) copy-start(bf16[256,1280]{1,0:T(8,128)(2,1)S(1)} %get-tuple-element.611) | copy-start | bytes 1966084
  419.9 2.9 copy-start.120
  427.6 36.5 %copy-start.67 = (f32[8,256]{1,0:T(8,128)S(1)}, f32[8,256]{1,0:T(8,128)}, u32[]{:S(2)}) copy-start(f32[8,256]{1,0:T(8,128)} %fusion.84) | copy-start | bytes 24580
  464.1 2.7 copy-start.61
  464.1 2.7 copy-start.66
  464.1 2.7 copy-start.82
  464.1 2.7 copy-start.91
  471.2 2.6 copy-start.79
  471.2 2.7 copy-start.88
  473.8 4.7 copy-start.46
  476.4 61.4 %reduce-scatter.14.cloned.1.call-start = ((), (), s32[]{:S(2)}) async-start(), calls=%async_computation.18 | async-start | bytes 2457600 | tf_op jit(solution)/shard_map/reduce_scatter | solution.py:312
  481.7 122.2 %reduce-scatter.8.cloned.1.call-start = ((), (), s32[]{:S(2)}) async-start(), calls=%async_computation.15 | async-start | bytes 819200 | tf_op jit(solution)/shard_map/reduce_scatter | solution.py:291
  515.8 3.1 copy-start.15
  520.9 84.6 %reduce-scatter.10.cloned.1.call-start = ((), (), s32[]{:S(2)}) async-start(), calls=%async_computation.16 | async-start | bytes 819200 | tf_op jit(solution)/shard_map/reduce_scatter | solution.py:306
  522.9 14.9 %copy-start.42 = (bf16[256,1280]{1,0:T(8,128)(2,1)S(1)}, bf16[256,1280]{1,0:T(8,128)(2,1)}, u32[]{:S(2)}) copy-start(bf16[256,1280]{1,0:T(8,128)(2,1)} %copy-done.41) | copy-start | bytes 1966084
  522.9 14.9 %copy-start.85 = (f32[256]{0:T(256)S(1)}, f32[256]{0:T(256)}, u32[]{:S(2)}) copy-start(f32[256]{0:T(256)} %copy-done.84) | copy-start | bytes 3076
  522.9 14.9 %copy-start.100 = (f32[256]{0:T(256)S(1)}, f32[256]{0:T(256)}, u32[]{:S(2)}) copy-start(f32[256]{0:T(256)} %copy-done.99) | copy-start | bytes 3076
  522.9 121.0 %all-reduce.18.cloned.1.call-start = ((), (), s32[]{:S(2)}) async-start(), calls=%async_computation.22 | async-start | bytes 1179648 | tf_op jit(solution)/shard_map/psum | solution.py:334
  523.0 14.9 %copy-start.8 = (f32[256,1280]{1,0:T(8,128)S(1)}, f32[256,1280]{1,0:T(8,128)}, u32[]{:S(2)}) copy-start(f32[256,1280]{1,0:T(8,128)} %copy-done.6) | copy-start | bytes 3932164
  537.8 169.9 %reduce-scatter.18.cloned.1.call-start = ((), (), s32[]{:S(2)}) async-start(), calls=%async_computation.20 | async-start | bytes 4096000 | tf_op jit(solution)/shard_map/reduce_scatter | solution.py:324
  543.6 228.7 %reduce-scatter.16.cloned.1.call-start = ((), (), s32[]{:S(2)}) async-start(), calls=%async_computation.19 | async-start | bytes 4096000 | tf_op jit(solution)/shard_map/reduce_scatter | solution.py:315
  549.7 287.2 %reduce-scatter.20.cloned.1.call-start = ((), (), s32[]{:S(2)}) async-start(), calls=%async_computation.21 | async-start | bytes 4096000 | tf_op jit(solution)/shard_map/reduce_scatter | solution.py:327
  560.4 35.7 %copy-start.96 = (f32[256]{0:T(256)S(1)}, f32[256]{0:T(256)}, u32[]{:S(2)}) copy-start(f32[256]{0:T(256)} %copy-done.95) | copy-start | bytes 3076
  560.4 35.7 %copy-start.94 = (f32[256]{0:T(256)S(1)}, f32[256]{0:T(256)}, u32[]{:S(2)}) copy-start(f32[256]{0:T(256)} %copy-done.93) | copy-start | bytes 3076
  (81 other events, 132.1 us)
Sparse Core Ops, SparseCore 0:
  9.6 53.4 all-gather.10
  65.5 22.4 all-gather.20
  89.9 23.5 all-gather.8
  115.8 41.1 all-gather.22
  159.3 41.1 all-gather.12
  201.8 65.6 all-gather.14
  269.1 64.2 all-gather.16
  335.0 64.2 all-gather.18
  476.5 19.2 reduce-scatter.11
  498.0 39.6 reduce-scatter.13
  540.7 21.3 reduce-scatter.7
  565.0 21.3 reduce-scatter.9
  589.9 54.0 all-reduce.17
  646.1 61.5 reduce-scatter.17
  709.9 62.4 reduce-scatter.15
  774.5 62.3 reduce-scatter.19
where the time goes:
time: 854 us; the launch traced here: 846 us
  waiting for transfers between devices  431 us (50%)
  matrix products  153 us (18%)
  blocking collectives  102 us (12%)
  local copies, waits for them, and re-layouts  79.7 us (9%)
  other arithmetic  54.5 us (6%)
  between operations  18.7 us (2%)
    dot_general x35, matrix products, matmul(): return jnp.dot(left, right, preferred_element_type=jnp.float32)  76.7 us
    all_gather x2, waiting for transfers between devices, shards(): lax.all_gather(values, 'ctx', axis=0, tiled=True)  73.1 us
    reduce_scatter x1, waiting for transfers between devices, shards(): lax.psum_scatter(totals[8].astype(jnp.bfloat16), 'wshard', scatter_dimens...  62.2 us
    reduce_scatter x1, waiting for transfers between devices, shards(): lax.psum_scatter(totals[12].astype(jnp.bfloat16), 'wshard', scatter_dimen...  62.2 us
    reduce_scatter x1, waiting for transfers between devices, shards(): lax.psum_scatter(totals[11].astype(jnp.bfloat16), 'wshard', scatter_dimen...  60.1 us
    all_gather x1, waiting for transfers between devices, shards(): lax.all_gather(w_up, 'wshard', axis=0, tiled=True)  58 us
    all_gather x1, waiting for transfers between devices, shards(): lax.all_gather(w_down, 'wshard', axis=0, tiled=True)  52.8 us
    unnamed x259, local copies, waits for them, and re-layouts  40.3 us
  transfers between devices with their start and end apart: 16, of which 12 were waited for; matrix products, arithmetic and copies ran while one was open for 23% of the time, Pallas kernels for 0%

commit v1 on v0

v1 whole, which is shorter than its diff:
```python
import math

import jax
import jax.numpy as jnp
from jax import lax
from jax.sharding import PartitionSpec as P

H = 8
LOW = jnp.bfloat16
FULL = jnp.float32


def layer_norm(values, gain, offset):
    center = jnp.mean(values, axis=-1, keepdims=True)
    centred = values - center
    variance = jnp.mean(centred * centred, axis=-1, keepdims=True)
    return centred * lax.rsqrt(variance + 1e-05) * gain + offset


def exact_gelu(values):
    return jax.nn.gelu(values, approximate=False)


def matmul(left, right):
    return jnp.dot(left, right, preferred_element_type=FULL)


def matmul_tn(left, right):
    return lax.dot_general(left, right, (((0,), (0,)), ((), ())), preferred_element_type=FULL)


def matmul_nt(left, right):
    return lax.dot_general(left, right, (((1,), (1,)), ((), ())), preferred_element_type=FULL)


def gather(shard):
    return lax.all_gather(shard, "wshard", axis=0, tiled=True)


def scatter(total):
    return lax.psum_scatter(
        total.astype(LOW), "wshard", scatter_dimension=0, tiled=True
    ).astype(FULL)


def own_part(total, shard):
    size = shard.shape[0]
    return lax.dynamic_slice_in_dim(total, lax.axis_index("wshard") * size, size, 0)


def shards(
    byte_feats,
    lengths,
    latent_array,
    lat_gain,
    lat_bias,
    in_gain,
    in_bias,
    w_query,
    w_key,
    w_value,
    w_output,
    mlp_gain,
    mlp_bias,
    w_up,
    w_down,
    cotangent,
):
    seqs, slots, width = byte_feats.shape
    gain_in, bias_in = gather(in_gain).astype(FULL), gather(in_bias).astype(FULL)
    key_w, value_w = gather(w_key), gather(w_value)
    latent = gather(latent_array).astype(FULL)
    gain_lat, bias_lat = gather(lat_gain).astype(FULL), gather(lat_bias).astype(FULL)
    query_w = gather(w_query)
    gain_mlp, bias_mlp = gather(mlp_gain).astype(FULL), gather(mlp_bias).astype(FULL)
    output_w, up_w, down_w = gather(w_output), gather(w_up), gather(w_down)

    features = byte_feats.reshape(seqs * slots, width).astype(FULL)
    normed_in, in_back = jax.vjp(layer_norm, features, gain_in, bias_in)
    input_low = normed_in.astype(LOW)
    keys = matmul(input_low, key_w).astype(LOW)
    values = matmul(input_low, value_w).astype(LOW)
    normed_lat, lat_back = jax.vjp(layer_norm, latent, gain_lat, bias_lat)
    lat_low = normed_lat.astype(LOW)
    rows = lat_low.shape[0]
    queries = matmul(lat_low, query_w).astype(LOW)
    score_scale = 1.0 / math.sqrt(queries.shape[1] // H)
    qheads = queries.reshape(rows, H, -1)
    kheads = keys.reshape(seqs, slots, H, -1)
    vheads = values.reshape(seqs, slots, H, -1)

    scores = jnp.einsum("lhd,mkhd->mhlk", qheads, kheads, preferred_element_type=FULL) * score_scale
    slot_ids = lax.axis_index("ctx") * slots + lax.iota(jnp.int32, slots)
    valid = (slot_ids[None, :] < lengths[:, None])[:, None, None, :]
    scores = jnp.where(valid, scores, -1e30)
    highest = lax.pmax(jnp.max(scores, axis=-1), "ctx")
    weights = jnp.where(valid, jnp.exp(scores - highest[..., None]), 0.0)
    total = lax.psum(jnp.sum(weights, axis=-1), "ctx")
    numer = jnp.einsum("mhlk,mkhe->mlhe", weights.astype(LOW), vheads, preferred_element_type=FULL)
    numer = lax.psum(numer.astype(LOW), "ctx").astype(FULL)
    attended = numer / jnp.transpose(total, (0, 2, 1))[..., None]
    attended = attended.reshape(seqs * rows, -1)

    att_low = attended.astype(LOW)
    hidden = jnp.tile(latent, (seqs, 1)) + matmul(att_low, output_w)
    normed_mid, mid_back = jax.vjp(layer_norm, hidden, gain_mlp, bias_mlp)
    mid_low = normed_mid.astype(LOW)
    upward = matmul(mid_low, up_w)
    activated, gelu_back = jax.vjp(exact_gelu, upward)
    act_low = activated.astype(LOW)
    result = hidden + matmul(act_low, down_w)
    dout_low = cotangent.reshape(seqs * rows, -1)
    grad_down = scatter(matmul_tn(act_low, dout_low))
    (grad_upward,) = gelu_back(matmul_nt(dout_low, down_w))
    up_low = grad_upward.astype(LOW)
    grad_up = scatter(matmul_tn(mid_low, up_low))
    dhid_norm, grad_gmlp, grad_bmlp = mid_back(matmul_nt(up_low, up_w))
    dhidden = dout_low.astype(FULL) + dhid_norm
    dhid_low = dhidden.astype(LOW)
    grad_output = scatter(matmul_tn(att_low, dhid_low))
    grad_hidden = scatter(jnp.sum(dhidden.reshape(seqs, rows, -1), axis=0))
    grad_att = matmul_nt(dhid_low, output_w).astype(LOW)

    grad_heads = grad_att.reshape(seqs, rows, H, -1)
    delta = jnp.sum(
        grad_heads.astype(FULL) * attended.reshape(seqs, rows, H, -1), axis=-1
    ).transpose(0, 2, 1)
    probs = weights / total[..., None]
    dprobs = jnp.einsum("mlhe,mkhe->mhlk", grad_heads, vheads, preferred_element_type=FULL)
    dscores = (probs * (dprobs - delta[..., None])).astype(LOW)
    dquery = jnp.einsum("mhlk,mkhd->lhd", dscores, kheads, preferred_element_type=FULL) * score_scale
    dkeys = jnp.einsum("mhlk,lhd->mkhd", dscores, qheads, preferred_element_type=FULL) * score_scale
    dvalues = jnp.einsum("mhlk,mlhe->mkhe", probs.astype(LOW), grad_heads, preferred_element_type=FULL)
    dkeys = dkeys.astype(LOW).reshape(seqs * slots, -1)
    dvalues = dvalues.astype(LOW).reshape(seqs * slots, -1)

    dquery = lax.psum(dquery.reshape(rows, -1).astype(LOW), ("ctx", "wshard"))
    grad_query = matmul_tn(
        lax.dynamic_slice_in_dim(
            lat_low, lax.axis_index("wshard") * w_query.shape[0], w_query.shape[0], 1
        ),
        dquery,
    )
    dlat_norm, grad_glat, grad_blat = lat_back(matmul_nt(dquery, query_w))
    grad_latent = grad_hidden + own_part(dlat_norm, latent_array)

    dnorm_in = matmul_nt(dkeys, key_w) + matmul_nt(dvalues, value_w)
    dfeatures, grad_gin, grad_bin = in_back(dnorm_in)
    grad_key = lax.psum(scatter(matmul_tn(input_low, dkeys)).astype(LOW), "ctx").astype(FULL)
    grad_value = lax.psum(scatter(matmul_tn(input_low, dvalues)).astype(LOW), "ctx").astype(FULL)
    in_sums = lax.psum(jnp.concatenate([grad_gin, grad_bin]), ("ctx", "wshard"))
    grad_gin, grad_bin = jnp.split(in_sums, 2)
    mlp_sums = lax.psum(jnp.concatenate([grad_gmlp, grad_bmlp]), "wshard")
    grad_gmlp, grad_bmlp = jnp.split(mlp_sums, 2)
    return (
        result.astype(LOW).reshape(seqs, rows, -1),
        dfeatures.astype(LOW).reshape(seqs, slots, width),
        grad_latent,
        own_part(grad_glat, lat_gain),
        own_part(grad_blat, lat_bias),
        own_part(grad_gin, in_gain),
        own_part(grad_bin, in_bias),
        grad_query,
        grad_key,
        grad_value,
        grad_output,
        own_part(grad_gmlp, mlp_gain),
        own_part(grad_bmlp, mlp_bias),
        grad_up,
        grad_down,
    )


def solution(mesh):
    sharded, plain = P("wshard", None), P("wshard")
    return jax.shard_map(
        shards,
        mesh=mesh,
        in_specs=(
            P("wshard", "ctx", None),
            plain,
            sharded,
            plain,
            plain,
            plain,
            plain,
            sharded,
            sharded,
            sharded,
            sharded,
            plain,
            plain,
            sharded,
            sharded,
            P("wshard", None, None),
        ),
        out_specs=(
            P("wshard", None, None),
            P("wshard", "ctx", None),
            sharded,
            plain,
            plain,
            plain,
            plain,
            sharded,
            sharded,
            sharded,
            sharded,
            plain,
            plain,
            sharded,
            sharded,
        ),
        check_vma=False,
    )
```

time: 854 us -> 929 us (1.088)
  waiting for transfers between devices: 431 us -> 580 us
  matrix products: 153 us -> 76.5 us
  blocking collectives: 102 us -> 175 us
  local copies, waits for them, and re-layouts: 79.7 us -> 34.6 us
  other arithmetic: 54.5 us -> 36.8 us
    psum x1 -> x3, waiting for transfers between devices: 36.8 us -> 143 us  [the longest x1 55.3 us: shards(): lax.psum(scatter(matmul_tn(input_low, dkeys)).astype(LOW), 'ctx')]
    dot_general x57 -> x24, matrix products: 153 us -> 76.5 us  [the longest x6 22.2 us: matmul_nt(): lax.dot_general(left, right, (((1,), (1,)), ((), ())), preferred_element_...]
    psum x1 -> x3, blocking collectives: 12 us -> 79.5 us  [the longest x1 39.6 us: shards(): in_sums = lax.psum(jnp.concatenate([grad_gin, grad_bin]), ('ctx', 'wshard'))]
    reduce_scatter x7 -> x6, waiting for transfers between devices: 194 us -> 252 us  [scatter(): lax.psum_scatter(total.astype(LOW), 'wshard', scatter_dimension=0, tiled=...]
    unnamed x259 -> x164, local copies, waits for them, and re-layouts: 40.3 us -> 17.9 us
    pmax x0 -> x1, blocking collectives: none -> 22.3 us  [shards(): highest = lax.pmax(jnp.max(scores, axis=-1), 'ctx')]
    dynamic_slice x24 -> x7, local copies, waits for them, and re-layouts: 24.8 us -> 3.96 us  [own_part(): lax.dynamic_slice_in_dim(total, lax.axis_index('wshard') * size, size, 0)]
    unnamed x2 -> x1, blocking collectives: 39.5 us -> 19.8 us
  transfers between devices with their start and end apart: 16 -> 13, of which waited for: 12 -> 12; matrix products, arithmetic and copies ran while one was open for 23% -> 10% of each run, Pallas kernels for 0% -> 0%
where the time goes in v1:
time: 929 us; the launch traced here: 920 us
  waiting for transfers between devices  580 us (62%)
  blocking collectives  175 us (19%)
  matrix products  76.5 us (8%)
  other arithmetic  36.8 us (4%)
  local copies, waits for them, and re-layouts  34.6 us (4%)
  between operations  16.6 us (2%)
    reduce_scatter x6, waiting for transfers between devices, scatter(): lax.psum_scatter(total.astype(LOW), 'wshard', scatter_dimension=0, tiled=...  252 us
    all_gather x4, waiting for transfers between devices, gather(): return lax.all_gather(shard, 'wshard', axis=0, tiled=True)  183 us
    psum x1, waiting for transfers between devices, shards(): lax.psum(scatter(matmul_tn(input_low, dkeys)).astype(LOW), 'ctx')  55.3 us
    all_gather x3, blocking collectives, gather(): return lax.all_gather(shard, 'wshard', axis=0, tiled=True)  53 us
    psum x1, waiting for transfers between devices, shards(): numer = lax.psum(numer.astype(LOW), 'ctx').astype(FULL)  52.8 us
    psum x1, blocking collectives, shards(): in_sums = lax.psum(jnp.concatenate([grad_gin, grad_bin]), ('ctx', 'wshard'))  39.6 us
    psum x1, waiting for transfers between devices, shards(): dquery = lax.psum(dquery.reshape(rows, -1).astype(LOW), ('ctx', 'wshard'))  34.9 us
    psum x1, blocking collectives, shards(): total = lax.psum(jnp.sum(weights, axis=-1), 'ctx')  22.3 us
  transfers between devices with their start and end apart: 13, of which 12 were waited for; matrix products, arithmetic and copies ran while one was open for 10% of the time, Pallas kernels for 0%

profile of v1, /device:TPU:0, one launch (start us, length us, event | category | flops | bytes accessed | tf_op | source)
XLA Modules:
  0.0 920.4 jit_solution(9357087982869084946)
XLA Ops:
  8.1 22.5 %all_gather.39 = bf16[256,1280]{1,0:T(8,128)(2,1)S(1)} all-gather(bf16[64,1280]{1,0:T(8,128)(2,1)} %param.18), channel_id=1, replica_groups=mesh['ctx'=8,'wshard'=4] {'wshard'}, dimensions={0}, use_global_device_ids=true | all-gather | bytes 819200 | tf_op jit(solution)/shard_map/all_gather | solution.py:37
  30.5 1.2 dynamic-slice.4
  35.1 19.8 %all-reduce.7 = (bf16[1280]{0:T(1024)(128)(2,1)S(1)}, bf16[1280]{0:T(1024)(128)(2,1)S(1)}, bf16[768]{0:T(1024)(128)(2,1)S(1)}, bf16[768]{0:T(1024)(128)(2,1)S(1)...) all-reduce(bf16[1280]{0:T(1024)(128)(2,1)S(1)} %dynamic-update-slic, ...), channel_id=1, replica_groups=mesh['ctx'=8,'wshard'=4] {'wshard'}, use_global_device_ids=true, to_apply=%add.3 | all-reduce | flops 6656 | bytes 26624
  56.1 15.5 %all_gather.43 = bf16[768,256]{1,0:T(8,128)(2,1)S(1)} all-gather(bf16[192,256]{1,0:T(8,128)(2,1)S(1)} %copy-done.36), channel_id=1, replica_groups=mesh['ctx'=8,'wshard'=4] {'wshard'}, dimensions={0}, use_global_device_ids=true | all-gather | bytes 491520 | tf_op jit(solution)/shard_map/all_gather | solution.py:37
  73.1 15.1 %all_gather.46 = bf16[1280,256]{1,0:T(8,128)(2,1)S(1)} all-gather(bf16[320,256]{1,0:T(8,128)(2,1)S(1)} %copy-done.30), channel_id=1, replica_groups=mesh['ctx'=8,'wshard'=4] {'wshard'}, dimensions={0}, use_global_device_ids=true | all-gather | bytes 819200 | tf_op jit(solution)/shard_map/all_gather | solution.py:37
  90.5 3.0 bitcast_reduce_fusion
  93.5 22.3 %pmax.7 = f32[2,8,256]{2,0,1:T(2,128)S(1)} all-reduce(f32[2,8,256]{2,0,1:T(2,128)S(1)} %get-tuple-element.50), channel_id=1, replica_groups=mesh['ctx'=8,'wshard'=4] {'ctx'}, use_global_device_ids=true, to_apply=%region_5.6 | all-reduce | flops 4096 | bytes 32768 | tf_op jit(solution)/shard_map/pmax | solution.py:96
  115.8 3.4 fusion.37
  119.2 22.3 %psum.50 = f32[2,8,256]{2,0,1:T(2,128)S(1)} all-reduce(f32[2,8,256]{2,0,1:T(2,128)S(1)} %fusion.37), channel_id=1, replica_groups=mesh['ctx'=8,'wshard'=4] {'ctx'}, use_global_device_ids=true, to_apply=%region_8.9 | all-reduce | flops 4096 | bytes 32768 | tf_op jit(solution)/shard_map/psum | solution.py:98
  141.6 4.4 fusion.14
  146.0 3.8 convolution_convert_fusion.4
  149.8 1.6 copy.60
  151.4 1.2 reshape.259
  152.6 3.6 fusion.24
  158.7 1.2 add_convert_fusion.2
  160.0 52.8 %all-reduce.12.cloned.1.call-done = bf16[2,256,8,160]{1,3,2,0:T(8,128)(2,1)} async-done(((bf16[2,256,8,160]{1,3,2,0:T(8,128)(2,1)}), bf16[2,256,8,160]{1,3,2,0:T(8,128)(2,1)}) %all-reduce.12.cloned.1.call-update) | async-done | bytes 1310736 | tf_op jit(solution)/shard_map/psum | solution.py:100
  212.7 1.6 fusion.13
  214.3 1.4 copy.66
  216.0 63.3 %all-gather.7.cloned.1.call-done = bf16[1280,1280]{1,0:T(8,128)(2,1)} async-done(((bf16[320,1280]{1,0:T(8,128)(2,1)}), bf16[1280,1280]{1,0:T(8,128)(2,1)}) %all-gather.7.cloned.1.call-update) | async-done | bytes 3276816 | tf_op jit(solution)/shard_map/all_gather | solution.py:37
  279.5 1.8 copy-done.12
  281.2 2.1 fusion.58
  283.3 1.4 copy-done.1
  285.2 60.0 %all-gather.9.cloned.1.call-done = bf16[1280,1280]{1,0:T(8,128)(2,1)} async-done(((bf16[320,1280]{1,0:T(8,128)(2,1)}), bf16[1280,1280]{1,0:T(8,128)(2,1)}) %all-gather.9.cloned.1.call-update) | async-done | bytes 3276816 | tf_op jit(solution)/shard_map/all_gather | solution.py:37
  345.1 6.2 fusion.51
  351.4 59.6 %all-gather.11.cloned.1.call-done = bf16[1280,1280]{1,0:T(8,128)(2,1)} async-done(((bf16[320,1280]{1,0:T(8,128)(2,1)}), bf16[1280,1280]{1,0:T(8,128)(2,1)}) %all-gather.11.cloned.1.call-update) | async-done | bytes 3276816 | tf_op jit(solution)/shard_map/all_gather | solution.py:37
  411.0 11.0 %add_convert_fusion = (bf16[512,1280]{1,0:T(8,128)(2,1)S(1)}, f32[512,1280]{1,0:T(8,128)}) fusion(f32[512,1280]{1,0:T(8,128)} %fusion.51, bf16[512,1280]{1,0:T(8,128)(2,1)S(1)} %bitcast.132, bf16[1280,1280]{1,0:T(8,128)(2,1)} %all-gather.11.cloned.1.call-done), kind=kOutput, calls=%fused_computation.22 | convolution fusion | flops 1724907520 | bytes 11141120 | tf_op jit(solution)/shard_map/dot_general | solution.py:33
  421.9 2.8 multiply_reduce_fusion
  425.9 1.6 copy-done.4
  428.4 3.0 convolution_convert_fusion.5
  431.3 2.5 copy.67
  433.9 4.0 reshape.264
  437.9 1.9 multiply_reduce_fusion.1
  440.0 4.0 multiply_convert_fusion
  445.8 1.2 convolution_convert_fusion.6
  447.0 2.8 fusion.21
  449.9 1.4 copy.77
  452.6 2.6 convolution_convert_fusion.3
  455.2 2.0 fusion.34
  457.3 3.1 reduce_sum.204
  460.5 5.9 reduce-scatter.9.cloned.1.call-done
  466.4 42.1 %reduce-scatter.11.cloned.1.call-done = bf16[192,1280]{1,0:T(8,128)(2,1)} async-done(((bf16[768,1280]{1,0:T(8,128)(2,1)}), bf16[192,1280]{1,0:T(8,128)(2,1)}) %reduce-scatter.11.cloned.1.call-update) | async-done | bytes 491536 | tf_op jit(solution)/shard_map/reduce_scatter | solution.py:41
  508.5 5.3 convolution_convert_fusion.2
  515.2 5.7 convolution_convert_fusion.1
  521.2 3.0 multiply_convert_fusion.1
  525.2 3.7 convolution_convert_fusion
  528.9 1.3 copy-done.22
  530.2 2.8 fusion.59
  534.1 39.6 %psum.52 = f32[1536]{0:T(1024)S(1)} all-reduce(f32[1536]{0:T(1024)S(1)} %pad_maximum_fusion.1), channel_id=1, replica_groups=mesh['ctx'=8,'wshard'=4] {'ctx','wshard'}, use_global_device_ids=true, to_apply=%region_25.26 | all-reduce | flops 1536 | bytes 12288 | tf_op jit(solution)/shard_map/psum | solution.py:151
  575.0 17.6 %psum.55 = f32[2560]{0:T(1024)S(1)} all-reduce(f32[2560]{0:T(1024)S(1)} %pad_maximum_fusion), channel_id=1, replica_groups=mesh['ctx'=8,'wshard'=4] {'wshard'}, use_global_device_ids=true, to_apply=%region_33.34 | all-reduce | flops 2560 | bytes 20480 | tf_op jit(solution)/shard_map/psum | solution.py:153
  596.3 5.0 fusion.2
  601.3 34.9 %all-reduce.14.cloned.1.call-done = bf16[256,256]{0,1:T(8,128)(2,1)} async-done(((bf16[256,256]{0,1:T(8,128)(2,1)}), bf16[256,256]{0,1:T(8,128)(2,1)}) %all-reduce.14.cloned.1.call-update) | async-done | bytes 131088 | tf_op jit(solution)/shard_map/psum | solution.py:137
  636.3 1.7 multiply_reduce_fusion.7
  639.9 2.0 fusion.43
  641.9 18.4 %reduce-scatter.7.cloned.1.call-done = bf16[64,1280]{1,0:T(8,128)(2,1)} async-done(((bf16[256,1280]{1,0:T(8,128)(2,1)}), bf16[64,1280]{1,0:T(8,128)(2,1)}) %reduce-scatter.7.cloned.1.call-update) | async-done | bytes 163856 | tf_op jit(solution)/shard_map/reduce_scatter | solution.py:41
  660.3 1.7 fusion.39
  662.1 55.3 %all-reduce.16.cloned.1.call-done = (bf16[192,256]{1,0:T(8,128)(2,1)}, bf16[192,1280]{1,0:T(8,128)(2,1)}) async-done(((bf16[192,256]{1,0:T(8,128)(2,1)}, bf16[192,1280]{1,0:T(8,128)(2,1)}), (bf16[192,256]{1,0:T(8,128)(2,1)}, bf16[192,1280]{1,0:T(8,128)(2,1)})) %all-reduce.16.cloned.1.call-update) | async-done | bytes 589840 | tf_op jit(solution)/shard_map/psum | solution.py:149
  717.4 1.6 convert_element_type.210
  719.0 2.0 convert_element_type.212
  721.0 60.4 %reduce-scatter.13.cloned.1.call-done = bf16[320,1280]{1,0:T(8,128)(2,1)} async-done(((bf16[1280,1280]{1,0:T(8,128)(2,1)}), bf16[320,1280]{1,0:T(8,128)(2,1)}) %reduce-scatter.13.cloned.1.call-update) | async-done | bytes 819216 | tf_op jit(solution)/shard_map/reduce_scatter | solution.py:41
  781.4 2.4 convert_element_type.214
  783.8 62.3 %reduce-scatter.15.cloned.1.call-done = bf16[320,1280]{1,0:T(8,128)(2,1)} async-done(((bf16[1280,1280]{1,0:T(8,128)(2,1)}), bf16[320,1280]{1,0:T(8,128)(2,1)}) %reduce-scatter.15.cloned.1.call-update) | async-done | bytes 819216 | tf_op jit(solution)/shard_map/reduce_scatter | solution.py:41
  846.1 2.4 convert_element_type.216
  848.5 62.4 %reduce-scatter.17.cloned.1.call-done = bf16[320,1280]{1,0:T(8,128)(2,1)} async-done(((bf16[1280,1280]{1,0:T(8,128)(2,1)}), bf16[320,1280]{1,0:T(8,128)(2,1)}) %reduce-scatter.17.cloned.1.call-update) | async-done | bytes 819216 | tf_op jit(solution)/shard_map/reduce_scatter | solution.py:41
  911.0 2.4 convert_element_type.218
  (240 shorter events, 27.1 us)
Async XLA Ops:
  7.2 26.4 %copy-start.63 = (bf16[320]{0:T(512)(128)(2,1)S(1)}, bf16[320]{0:T(512)(128)(2,1)}, u32[]{:S(2)}) copy-start(bf16[320]{0:T(512)(128)(2,1)} %param.20) | copy-start | bytes 1924
  7.2 26.7 %copy-start.64 = (bf16[320]{0:T(512)(128)(2,1)S(1)}, bf16[320]{0:T(512)(128)(2,1)}, u32[]{:S(2)}) copy-start(bf16[320]{0:T(512)(128)(2,1)} %param.19) | copy-start | bytes 1924
  7.2 26.9 %copy-start.69 = (bf16[192]{0:T(256)(128)(2,1)S(1)}, bf16[192]{0:T(256)(128)(2,1)}, u32[]{:S(2)}) copy-start(bf16[192]{0:T(256)(128)(2,1)} %param.22) | copy-start | bytes 1156
  7.2 27.2 %copy-start.70 = (bf16[192]{0:T(256)(128)(2,1)S(1)}, bf16[192]{0:T(256)(128)(2,1)}, u32[]{:S(2)}) copy-start(bf16[192]{0:T(256)(128)(2,1)} %param.21) | copy-start | bytes 1156
  7.2 27.4 %copy-start.65 = (bf16[320]{0:T(512)(128)(2,1)S(1)}, bf16[320]{0:T(512)(128)(2,1)}, u32[]{:S(2)}) copy-start(bf16[320]{0:T(512)(128)(2,1)} %param.28) | copy-start | bytes 1924
  7.2 27.6 %copy-start.66 = (bf16[320]{0:T(512)(128)(2,1)S(1)}, bf16[320]{0:T(512)(128)(2,1)}, u32[]{:S(2)}) copy-start(bf16[320]{0:T(512)(128)(2,1)} %param.27) | copy-start | bytes 1924
  7.2 47.6 %copy-start = (bf16[2,256,768]{2,1,0:T(8,128)(2,1)S(1)}, bf16[2,256,768]{2,1,0:T(8,128)(2,1)}, u32[]{:S(2)}) copy-start(bf16[2,256,768]{2,1,0:T(8,128)(2,1)} %param.16) | copy-start | bytes 2359300
  7.3 48.8 %copy-start.36 = (bf16[192,256]{1,0:T(8,128)(2,1)S(1)}, bf16[192,256]{1,0:T(8,128)(2,1)}, u32[]{:S(2)}) copy-start(bf16[192,256]{1,0:T(8,128)(2,1)} %param.24) | copy-start | bytes 294916
  7.3 138.7 %all-gather.5.cloned.1.call-start = ((), (), s32[]{:S(2)}) async-start(), calls=%async_computation.6 | async-start | bytes 2457600 | tf_op jit(solution)/shard_map/all_gather | solution.py:37
  8.0 204.7 %all-reduce.12.cloned.1.call-start = ((), (), s32[]{:S(2)}) async-start(), calls=%async_computation.7 | async-start | bytes 2621440 | tf_op jit(solution)/shard_map/psum | solution.py:100
  33.3 55.0 %copy-start.51 = (f32[256]{0:T(256)}, f32[256]{0:T(256)S(1)}, u32[]{:S(2)}) copy-start(f32[256]{0:T(256)S(1)} %broadcast_multiply_fusion.2) | copy-start | bytes 3076
  33.6 39.1 %copy-start.55 = (f32[256]{0:T(256)}, f32[256]{0:T(256)S(1)}, u32[]{:S(2)}) copy-start(f32[256]{0:T(256)S(1)} %multiply_reduce_fusion.9) | copy-start | bytes 3076
  54.9 103.8 %copy-start.34 = (f32[768]{0:T(1024)}, f32[768]{0:T(1024)S(1)}, u32[]{:S(2)}) copy-start(f32[768]{0:T(1024)S(1)} %convert_element_type.170) | copy-start | bytes 9220
  55.1 18.0 %copy-start.67 = (s32[2]{0:T(128)S(1)}, s32[2]{0:T(128)}, u32[]{:S(2)}) copy-start(s32[2]{0:T(128)} %param.17) | copy-start | bytes 28
  55.1 18.0 %copy-start.30 = (bf16[320,256]{1,0:T(8,128)(2,1)S(1)}, bf16[320,256]{1,0:T(8,128)(2,1)}, u32[]{:S(2)}) copy-start(bf16[320,256]{1,0:T(8,128)(2,1)} %param.23) | copy-start | bytes 491524
  56.1 16.7 %copy-start.41 = (f32[512]{0:T(512)}, f32[512]{0:T(512)S(1)}, u32[]{:S(2)}) copy-start(f32[512]{0:T(512)S(1)} %rsqrt.33) | copy-start | bytes 6148
  56.1 16.7 %copy-start.43 = (f32[1,2,2,128]{3,1,2,0:T(2,128)}, f32[1,2,2,128]{3,1,2,0:T(2,128)S(1)}, u32[]{:S(2)}) copy-start(f32[1,2,2,128]{3,1,2,0:T(2,128)S(1)} %copy.93) | copy-start | bytes 6148
  72.7 20.7 %copy-start.53 = (f32[256]{0:T(256)}, f32[256]{0:T(256)S(1)}, u32[]{:S(2)}) copy-start(f32[256]{0:T(256)S(1)} %fusion.48) | copy-start | bytes 3076
  72.8 20.7 %copy-start.37 = (f32[1280]{0:T(1024)}, f32[1280]{0:T(1024)S(1)}, u32[]{:S(2)}) copy-start(f32[1280]{0:T(1024)S(1)} %convert_element_type.175) | copy-start | bytes 15364
  73.0 20.5 %copy-start.18 = (bf16[2,256,8,32]{1,0,3,2:T(2,128)(2,1)}, bf16[2,256,8,32]{1,0,3,2:T(2,128)(2,1)S(1)}, u32[]{:S(2)}) copy-start(bf16[2,256,8,32]{1,0,3,2:T(2,128)(2,1)S(1)} %reshape.260) | copy-start | bytes 786436
  73.1 68.5 %copy-start.39 = (pred[2,256]{1,0:T(4,128)(4,1)}, pred[2,256]{1,0:T(4,128)(4,1)S(1)}, u32[]{:S(2)}) copy-start(pred[2,256]{1,0:T(4,128)(4,1)S(1)} %broadcast_compare_fusion) | copy-start | bytes 1540
  141.6 17.1 %copy-start.31 = (f32[2,8,256]{2,0,1:T(2,128)}, f32[2,8,256]{2,0,1:T(2,128)S(1)}, u32[]{:S(2)}) copy-start(f32[2,8,256]{2,0,1:T(2,128)S(1)} %psum.50) | copy-start | bytes 49156
  156.2 123.1 %all-gather.7.cloned.1.call-start = ((), (), s32[]{:S(2)}) async-start(), calls=%async_computation.8 | async-start | bytes 4096000 | tf_op jit(solution)/shard_map/all_gather | solution.py:37
  157.0 188.2 %all-gather.9.cloned.1.call-start = ((), (), s32[]{:S(2)}) async-start(), calls=%async_computation.9 | async-start | bytes 4096000 | tf_op jit(solution)/shard_map/all_gather | solution.py:37
  157.5 253.4 %all-gather.11.cloned.1.call-start = ((), (), s32[]{:S(2)}) async-start(), calls=%async_computation.10 | async-start | bytes 4096000 | tf_op jit(solution)/shard_map/all_gather | solution.py:37
  158.1 308.2 %reduce-scatter.9.cloned.1.call-start = ((), (), s32[]{:S(2)}) async-start(), calls=%async_computation.13 | async-start | bytes 491520 | tf_op jit(solution)/shard_map/reduce_scatter | solution.py:41
  158.7 186.4 %copy-start.59 = (f32[1280]{0:T(1024)}, f32[1280]{0:T(1024)S(1)}, u32[]{:S(2)}) copy-start(f32[1280]{0:T(1024)S(1)} %convert_element_type.186) | copy-start | bytes 15364
  158.7 266.0 %copy-start.45 = (f32[1280]{0:T(1024)}, f32[1280]{0:T(1024)S(1)}, u32[]{:S(2)}) copy-start(f32[1280]{0:T(1024)S(1)} %convert_element_type.185) | copy-start | bytes 15364
  216.0 67.3 %copy-start.7 = (bf16[160,8,2,256]{3,1,2,0:T(8,128)(2,1)}, bf16[160,8,2,256]{3,1,2,0:T(8,128)(2,1)S(1)}, u32[]{:S(2)}) copy-start(bf16[160,8,2,256]{3,1,2,0:T(8,128)(2,1)S(1)} %copy.95) | copy-start | bytes 3932164
  283.3 141.4 %copy-start.49 = (f32[512]{0:T(512)}, f32[512]{0:T(512)S(1)}, u32[]{:S(2)}) copy-start(f32[512]{0:T(512)S(1)} %broadcast_multiply_fusion) | copy-start | bytes 6148
  285.1 139.6 %copy-start.61 = (f32[512]{0:T(512)}, f32[512]{0:T(512)S(1)}, u32[]{:S(2)}) copy-start(f32[512]{0:T(512)S(1)} %fusion.45) | copy-start | bytes 6148
  285.2 125.8 %copy-start.24 = (bf16[2,256,1280]{2,1,0:T(8,128)(2,1)S(1)}, bf16[2,256,1280]{2,1,0:T(8,128)(2,1)}, u32[]{:S(2)}) copy-start(bf16[2,256,1280]{2,1,0:T(8,128)(2,1)} %param.31) | copy-start | bytes 3932164
  410.9 11.0 %copy-start.2 = (f32[512,1280]{1,0:T(8,128)S(1)}, f32[512,1280]{1,0:T(8,128)}, u32[]{:S(2)}) copy-start(f32[512,1280]{1,0:T(8,128)} %copy-done.1) | copy-start | bytes 7864324
  410.9 11.0 %copy-start.68 = (bf16[1280,1280]{1,0:T(8,128)(2,1)S(1)}, bf16[1280,1280]{1,0:T(8,128)(2,1)}, u32[]{:S(2)}) copy-start(bf16[1280,1280]{1,0:T(8,128)(2,1)} %all-gather.9.cloned.1.call-done) | copy-start | bytes 9830404
  421.9 2.8 copy-start.71
  425.5 2.9 copy-start.13
  431.3 6.6 copy-start.5
  437.9 2.1 copy-start.23
  440.0 4.0 copy-start.29
  447.0 61.5 %reduce-scatter.11.cloned.1.call-start = ((), (), s32[]{:S(2)}) async-start(), calls=%async_computation.14 | async-start | bytes 2457600 | tf_op jit(solution)/shard_map/reduce_scatter | solution.py:41
  449.9 2.7 copy-start.15
  455.2 181.0 %all-reduce.14.cloned.1.call-start = ((), (), s32[]{:S(2)}) async-start(), calls=%async_computation.12 | async-start | bytes 262144 | tf_op jit(solution)/shard_map/psum | solution.py:137
  457.3 51.3 %copy-start.8 = (bf16[160,8,2,256]{3,1,2,0:T(8,128)(2,1)S(1)}, bf16[160,8,2,256]{3,1,2,0:T(8,128)(2,1)}, u32[]{:S(2)}) copy-start(bf16[160,8,2,256]{3,1,2,0:T(8,128)(2,1)} %copy-done.7) | copy-start | bytes 3932164
  457.3 203.1 %reduce-scatter.7.cloned.1.call-start = ((), (), s32[]{:S(2)}) async-start(), calls=%async_computation.11 | async-start | bytes 819200 | tf_op jit(solution)/shard_map/reduce_scatter | solution.py:41
  460.4 257.0 %all-reduce.16.cloned.1.call-start = ((), (), s32[]{:S(2)}) async-start(), calls=%async_computation.18 | async-start | bytes 1179648 | tf_op jit(solution)/shard_map/psum | solution.py:149
  508.5 272.9 %reduce-scatter.13.cloned.1.call-start = ((), (), s32[]{:S(2)}) async-start(), calls=%async_computation.15 | async-start | bytes 4096000 | tf_op jit(solution)/shard_map/reduce_scatter | solution.py:41
  513.8 332.3 %reduce-scatter.15.cloned.1.call-start = ((), (), s32[]{:S(2)}) async-start(), calls=%async_computation.16 | async-start | bytes 4096000 | tf_op jit(solution)/shard_map/reduce_scatter | solution.py:41
  520.8 390.1 %reduce-scatter.17.cloned.1.call-start = ((), (), s32[]{:S(2)}) async-start(), calls=%async_computation.17 | async-start | bytes 4096000 | tf_op jit(solution)/shard_map/reduce_scatter | solution.py:41
  521.1 4.1 copy-start.25
  530.2 2.9 copy-start.10
  530.2 2.9 copy-start.20
  530.2 2.9 copy-start.35
  530.2 2.9 copy-start.42
  530.2 2.9 copy-start.44
  533.1 41.8 %copy-start.57 = (f32[1280]{0:T(1024)S(1)}, f32[1280]{0:T(1024)}, u32[]{:S(2)}) copy-start(f32[1280]{0:T(1024)} %get-tuple-element.15) | copy-start | bytes 15364
  533.1 41.8 %copy-start.58 = (f32[1280]{0:T(1024)S(1)}, f32[1280]{0:T(1024)}, u32[]{:S(2)}) copy-start(f32[1280]{0:T(1024)} %get-tuple-element.17) | copy-start | bytes 15364
  533.2 60.7 %copy-start.48 = (f32[1,2,2,128]{3,1,2,0:T(2,128)S(1)}, f32[1,2,2,128]{3,1,2,0:T(2,128)}, u32[]{:S(2)}) copy-start(f32[1,2,2,128]{3,1,2,0:T(2,128)} %copy-done.47) | copy-start | bytes 6148
  593.9 2.4 copy-start.27
  596.3 39.9 %copy-start.17 = (bf16[1280,256]{1,0:T(8,128)(2,1)S(1)}, bf16[1280,256]{1,0:T(8,128)(2,1)}, u32[]{:S(2)}) copy-start(bf16[1280,256]{1,0:T(8,128)(2,1)} %copy-done.16) | copy-start | bytes 1966084
  596.3 39.9 %copy-start.38 = (f32[1280]{0:T(1024)S(1)}, f32[1280]{0:T(1024)}, u32[]{:S(2)}) copy-start(f32[1280]{0:T(1024)} %copy-done.37) | copy-start | bytes 15364
  596.3 39.9 %copy-start.52 = (f32[256]{0:T(256)S(1)}, f32[256]{0:T(256)}, u32[]{:S(2)}) copy-start(f32[256]{0:T(256)} %copy-done.51) | copy-start | bytes 3076
  596.3 39.9 %copy-start.54 = (f32[256]{0:T(256)S(1)}, f32[256]{0:T(256)}, u32[]{:S(2)}) copy-start(f32[256]{0:T(256)} %copy-done.53) | copy-start | bytes 3076
  601.3 38.0 %copy-start.56 = (f32[256]{0:T(256)S(1)}, f32[256]{0:T(256)}, u32[]{:S(2)}) copy-start(f32[256]{0:T(256)} %copy-done.55) | copy-start | bytes 3076
  636.2 3.7 copy-start.33
  (22 other events, 27.4 us)
Sparse Core Ops, SparseCore 0:
  9.7 52.2 all-gather.4
  156.4 56.3 all-reduce.11
  214.4 64.8 all-gather.6
  280.8 64.2 all-gather.8
  346.6 64.2 all-gather.10
  447.1 19.1 reduce-scatter.8
  468.7 39.7 reduce-scatter.10
  514.6 121.6 all-reduce.13
  639.1 21.1 reduce-scatter.6
  663.4 53.9 all-reduce.15
  719.8 61.5 reduce-scatter.12
  783.7 62.4 reduce-scatter.14
  848.5 62.3 reduce-scatter.16

commit v2 on v1

--- a/solution.py
+++ b/solution.py
@@ -1,8 +1,12 @@
+import functools
 import math
+import types
 
 import jax
 import jax.numpy as jnp
 from jax import lax
+from jax.experimental import pallas as pl
+from jax.experimental.pallas import tpu as pltpu
 from jax.sharding import PartitionSpec as P
 
 H = 8
@@ -43,12 +47,15 @@
     ).astype(FULL)
 
 
+SEMS = 160
+
+
 def own_part(total, shard):
     size = shard.shape[0]
     return lax.dynamic_slice_in_dim(total, lax.axis_index("wshard") * size, size, 0)
 
 
-def shards(
+def plain(
     byte_feats,
     lengths,
     latent_array,
@@ -171,6 +178,916 @@
     )
 
 
+def ln_parts(values):
+    centred = values - jnp.mean(values, axis=-1, keepdims=True)
+    scale = lax.rsqrt(jnp.mean(centred * centred, axis=-1, keepdims=True) + 1e-05)
+    return centred * scale, scale
+
+
+def ln_grad(cotangent, gain, normed, scale):
+    scaled = cotangent * gain
+    first = jnp.mean(scaled, axis=-1, keepdims=True)
+    second = jnp.mean(scaled * normed, axis=-1, keepdims=True)
+    return scale * (scaled - first - normed * second)
+
+
+def lanes(rows, columns):
+    return lax.broadcasted_iota(jnp.int32, (rows, columns), 1)
+
+
+def columns_sum(values):
+    return jnp.sum(values, axis=0, keepdims=True)
+
+
+class Plan:
+    def __init__(self, ctx, zs, feats, latent, w_query, w_key, w_value, w_output, cot):
+        self.ctx, self.zs = ctx, zs
+        self.rows_in, self.din = feats.shape
+        self.lat = latent.shape[0] * zs
+        self.dl = latent.shape[1]
+        self.qk, self.vd = w_key.shape[1], w_value.shape[1]
+        self.seqs = cot.shape[0] // self.lat
+        self.slots = self.rows_in // self.seqs
+        self.head, self.vhead = self.qk // H, self.vd // H
+
+
+def scratch_table(p):
+    both = p.seqs * p.lat
+    half = p.dl // 2
+    part = p.dl // p.zs // 4
+    vpart = p.din // p.zs // 4
+    return dict(
+        wk=((p.din, p.qk), LOW),
+        wq=((p.dl, p.qk), LOW),
+        lat=((p.lat, p.dl), LOW),
+        wv=((p.din, p.vd), LOW),
+        wo=((p.vd, p.dl), LOW),
+        wu=((p.dl, p.dl), LOW),
+        wd=((p.dl, p.dl), LOW),
+        small_own=((8, 384), FULL),
+        small=((p.zs, 8, 384), FULL),
+        vec=((8, p.dl), FULL),
+        feats=((p.rows_in, p.din), LOW),
+        nin=((p.rows_in, p.din), LOW),
+        nin_t=((p.din, p.rows_in), LOW),
+        keys=((p.rows_in, p.qk), LOW),
+        keys_t=((p.qk, p.rows_in), LOW),
+        values=((p.rows_in, p.vd), LOW),
+        nlat=((p.lat, p.dl), LOW),
+        qmask=((H * p.lat, p.qk), LOW),
+        scores=((p.seqs * H * p.lat, p.slots), FULL),
+        stat=((p.lat, 128), FULL),
+        stat_t=((128, p.lat), FULL),
+        max_own=((2 * H, p.lat), FULL),
+        max_in=((p.ctx, 2 * H, p.lat), FULL),
+        max_all=((2 * H, p.lat), FULL),
+        numer=((p.lat, p.vd), FULL),
+        numer_low=((p.lat, p.vd), LOW),
+        numer_in=((p.lat, p.vd), LOW),
+        sums=((2, H, p.lat), FULL),
+        sums_in=((H, p.lat), FULL),
+        chip=((p.lat, p.vd), LOW),
+        chip_in=((4, p.lat // 4, p.vd), LOW),
+        chip_sums=((H, p.lat), FULL),
+        chip_sums_in=((4, H, p.lat), FULL),
+        scale=((p.lat // 4, p.vd), FULL),
+        att=((both, p.vd), LOW),
+        mid=((both, p.dl), LOW),
+        act=((both, p.dl), LOW),
+        dup=((both, p.dl), LOW),
+        dhid=((both, p.dl), LOW),
+        datt=((both, p.vd), LOW),
+        cot=((both, p.dl), LOW),
+        hid=((p.lat, p.dl), FULL),
+        slope=((p.lat, p.dl), FULL),
+        dmid=((p.lat, p.dl), FULL),
+        res=((p.lat, p.dl), LOW),
+        stats=((2, 2 * H, p.lat), FULL),
+        dwo=((p.vd, half), LOW),
+        dwu=((p.dl, half), LOW),
+        dwd=((p.dl, half), LOW),
+        dlat=((p.lat, half), LOW),
+        zo=((p.zs, part, half), LOW),
+        zu=((p.zs, part, half), LOW),
+        zd=((p.zs, part, half), LOW),
+        zl=((p.zs, p.lat // p.zs // 4, half), LOW),
+        fo=((part, half), LOW),
+        fu=((part, half), LOW),
+        fd=((part, half), LOW),
+        fl=((p.lat // p.zs // 4, half), LOW),
+        dkeys=((p.rows_in, p.qk), LOW),
+        dvalues=((p.rows_in, p.vd), LOW),
+        dk_sum=((p.slots, p.qk), FULL),
+        dq_t=((p.qk, p.lat), FULL),
+        dq=((p.lat, p.qk), LOW),
+        dq_in1=((p.lat, p.qk // 2), LOW),
+        dq_chip=((p.lat, p.qk // 2), LOW),
+        dq_in2=((4, p.lat, p.qk // 2), LOW),
+        dq_plane=((p.lat, p.qk // 2), LOW),
+        dq_in3=((p.zs, p.lat, p.qk // 2), LOW),
+        dq_all=((p.lat, p.qk), LOW),
+        bgrad=((p.rows_in, p.din), LOW),
+        swk=((2, p.din, p.qk // 2), LOW),
+        swv=((2, p.din, p.vd // 2), LOW),
+        rwk=((p.din, p.qk // 2), LOW),
+        rwv=((p.din, p.vd // 2), LOW),
+        cwk=((p.zs, p.din // p.zs, p.qk // 2), LOW),
+        cwv=((p.zs, p.din // p.zs, p.vd // 2), LOW),
+        pwk_in=((4, p.zs, vpart, p.qk // 2), LOW),
+        pwv_in=((4, p.zs, vpart, p.vd // 2), LOW),
+        pwk=((p.zs, vpart, p.qk // 2), LOW),
+        pwv=((p.zs, vpart, p.vd // 2), LOW),
+        zwk_in=((p.zs, vpart, p.qk // 2), LOW),
+        zwv_in=((p.zs, vpart, p.vd // 2), LOW),
+        fwk=((vpart, p.qk // 2), LOW),
+        fwv=((vpart, p.vd // 2), LOW),
+        vs=((8, p.dl), FULL),
+        vs_in1=((8, p.dl), FULL),
+        vs_chip=((8, p.dl), FULL),
+        vs_in2=((4, 8, p.dl), FULL),
+        vs_plane=((8, p.dl), FULL),
+        vs_in3=((p.zs, 8, p.dl), FULL),
+        vs_all=((8, p.dl), FULL),
+        gq=((p.dl, p.qk), FULL),
+    )
+
+
+class Copies:
+    def __init__(self, sems):
+        self.sems, self.used, self.open = sems, 0, []
+
+    def new(self):
+        self.used += 1
+        return self.sems.at[self.used - 1]
+
+    def group(self):
+        return (self.new(), self.new())
+
+    def send(self, pair, src, dst, ctx, z):
+        pltpu.make_async_remote_copy(
+            src_ref=src,
+            dst_ref=dst,
+            send_sem=pair[0],
+            recv_sem=pair[1],
+            device_id=(ctx, z),
+            device_id_type=pl.DeviceIdType.MESH,
+        ).start()
+
+    def local(self, src, dst):
+        copy = pltpu.make_async_copy(src, dst, self.new())
+        copy.start()
+        return copy
+
+    def got(self, pair, view):
+        pltpu.make_async_copy(view, view, pair[1]).wait()
+
+    def sent(self, pair, view):
+        self.open.append((pair[0], view))
+
+    def drain(self):
+        for sem, view in self.open:
+            pltpu.make_async_copy(view, view, sem).wait()
+
+
+def at(start, size, step=None):
+    return pl.ds(pl.multiple_of(start, step or size), size)
+
+
+def fused_kernel(p, names, *refs):
+    ins, refs = refs[:16], refs[16:]
+    lengths, feats_in, lat_in, wq_in, wk_in, wv_in, wo_in, wu_in, wd_in = ins[:9]
+    smalls, cot_in = ins[9:15], ins[15]
+    outs, refs = refs[:11], refs[11:]
+    res_out, byte_out, go, gu, gd, gv, gk, gl, gq_out, glat_out, vec_out = outs
+    sems = refs[-1]
+    s = types.SimpleNamespace(**dict(zip(names, refs[:-1])))
+    cp = Copies(sems)
+    ctx, zs = p.ctx, p.zs
+    c, z = lax.axis_index("ctx"), lax.axis_index("wshard")
+    h, q = lax.rem(c, 2), lax.div(c, 2)
+    x, y = lax.rem(q, 2), lax.div(q, 2)
+    other = 1 - h
+    core = c + 1 - 2 * h
+    chips = (c + 2 - 4 * x, c + 4 - 8 * y, c + 6 - 4 * x - 8 * y)
+    near = (chips[0] * (1 - h) + chips[1] * h, chips[1] * (1 - h) + chips[0] * h)
+    zed = [lax.rem(z + j, zs) for j in range(1, zs)]
+    plane = [lax.rem(c + j, ctx) for j in range(1, ctx)]
+
+    barrier = pltpu.get_barrier_semaphore()
+    for peer in plane:
+        pl.semaphore_signal(barrier, inc=1, device_id=(peer, z), device_id_type=pl.DeviceIdType.MESH)
+    for peer in zed:
+        pl.semaphore_signal(barrier, inc=1, device_id=(c, peer), device_id_type=pl.DeviceIdType.MESH)
+    pl.semaphore_wait(barrier, ctx - 1 + zs - 1)
+
+    load_feats = cp.local(feats_in, s.feats)
+    for row, ref in enumerate(smalls):
+        s.small_own[row : row + 1, 0 : ref.shape[1]] = ref[...].astype(FULL)
+    small_pair = cp.group()
+    for peer in zed:
+        cp.send(small_pair, s.small_own, s.small.at[z], c, peer)
+    cp.sent(small_pair, s.small.at[0 : zs - 1])
+
+    class Weight:
+        def __init__(self, ref, source):
+            self.ref, self.source = ref, source
+            self.rows, cols = source.shape
+            self.part, self.cols = self.rows // 4, cols // 2
+            self.mine = at(h * self.cols, self.cols)
+            self.pairs = [cp.group() for _ in range(4)]
+
+        def view(self, rows):
+            return self.ref.at[pl.ds(0, rows), pl.ds(0, self.cols)]
+
+        def block(self, zz, qq):
+            return self.ref.at[at(zz * self.rows + qq * self.part, self.part, 16), self.mine]
+
+        def start(self):
+            for peer in zed:
+                cp.send(
+                    self.pairs[0],
+                    self.source.at[at(q * self.part, self.part, 16), self.mine],
+                    self.block(z, q),
+                    c,
+                    peer,
+                )
+            cp.sent(self.pairs[0], self.view(3 * self.part))
+            self.load = cp.local(self.source, self.ref.at[at(z * self.rows, self.rows, 16), :])
+
+        def first(self):
+            cp.got(self.pairs[0], self.view(3 * self.part))
+            for zz in zed:
+                block = self.block(zz, q)
+                cp.send(self.pairs[1], block, block, near[0], z)
+            cp.sent(self.pairs[1], self.view(3 * self.part))
+
+        def second(self):
+            cp.got(self.pairs[1], self.view(3 * self.part))
+            for zz in zed:
+                for qq in (q, lax.div(near[0], 2)):
+                    block = self.block(zz, qq)
+                    cp.send(self.pairs[2], block, block, near[1], z)
+            cp.sent(self.pairs[2], self.view(6 * self.part))
+
+        def third(self):
+            cp.got(self.pairs[2], self.view(6 * self.part))
+            for zz in zed:
+                block = self.ref.at[at(zz * self.rows, self.rows, 16), self.mine]
+                cp.send(self.pairs[3], block, block, core, z)
+            cp.sent(self.pairs[3], self.view(3 * self.rows))
+
+        def ready(self):
+            cp.got(self.pairs[3], self.view(3 * self.rows))
+            self.load.wait()
+
+    wk, wq, lat = Weight(s.wk, wk_in), Weight(s.wq, wq_in), Weight(s.lat, lat_in)
+    wv = Weight(s.wv, wv_in)
+    wo, wu, wd = Weight(s.wo, wo_in), Weight(s.wu, wu_in), Weight(s.wd, wd_in)
+    for weight in (wk, wq, lat, wv, wo, wu, wd):
+        weight.start()
+    load_cot = cp.local(cot_in, s.cot)
+
+    cp.got(small_pair, s.small.at[0 : zs - 1])
+    s.small[z] = s.small_own[...]
+    for row, ref in enumerate(smalls):
+        size = ref.shape[1]
+        for zz in range(zs):
+            s.vec[row : row + 1, zz * size : (zz + 1) * size] = s.small[zz, row : row + 1, 0:size]
+    vec = s.vec
+    gain_lat, bias_lat = vec[0:1, :], vec[1:2, :]
+
+    load_feats.wait()
+
+    @pl.loop(0, p.rows_in // 64)
+    def _(i):
+        rows = at(i * 64, 64)
+        normed, _ = ln_parts(s.feats[rows, :].astype(FULL))
+        s.nin[rows, :] = (normed * vec[2:3, 0 : p.din] + vec[3:4, 0 : p.din]).astype(LOW)
+
+    wk.first()
+    wq.first()
+    lat.first()
+
+    @pl.loop(0, p.din // 128)
+    def _(i):
+        tile = at(i * 128, 128)
+        s.nin_t[tile, :] = s.nin[:, tile].T
+
+    wk.second()
+    wq.second()
+    lat.second()
+    wv.first()
+    wk.third()
+    wq.third()
+    lat.third()
+    wk.ready()
+
+    @pl.loop(0, p.seqs)
+    def _(i):
+        rows = at(i * p.slots, p.slots)
+        low = matmul(s.nin[rows, :], s.wk[...]).astype(LOW)
+        s.keys[rows, :] = low
+        s.keys_t[:, rows] = low.T
+
+    wv.second()
+    lat.ready()
+
+    @pl.loop(0, p.lat // 64)
+    def _(i):
+        rows = at(i * 64, 64)
+        normed, _ = ln_parts(s.lat[rows, :].astype(FULL))
+        s.nlat[rows, :] = (normed * gain_lat + bias_lat).astype(LOW)
+
+    wq.ready()
+    queries = matmul(s.nlat[...], s.wq[...])
+    lane_q = lanes(p.lat, p.qk)
+    for head in range(H):
+        inside = (lane_q >= head * p.head) & (lane_q < (head + 1) * p.head)
+        s.qmask[head * p.lat : (head + 1) * p.lat, :] = jnp.where(inside, queries, 0.0).astype(LOW)
+
+    score_scale = 1.0 / math.sqrt(p.head)
+    start_slot = c * p.slots
+    s.stat[...] = jnp.zeros_like(s.stat)
+    lane_stat = lanes(p.lat, 128)
+
+    @pl.loop(0, p.seqs * H)
+    def _(i):
+        seq, head = lax.div(i, H), lax.rem(i, H)
+        raw = matmul_nt(
+            s.qmask[at(head * p.lat, p.lat), :], s.keys[at(seq * p.slots, p.slots), :]
+        )
+        valid = start_slot + lanes(p.lat, p.slots) < lengths[seq]
+        scores = jnp.where(valid, raw * score_scale, -1e30)
+        s.scores[at(i * p.lat, p.lat), :] = scores
+        top = jnp.max(scores, axis=-1, keepdims=True)
+        s.stat[...] = jnp.where(lane_stat == i, top, s.stat[...])
+
+    s.stat_t[...] = s.stat[...].T
+    s.max_own[...] = s.stat_t[0 : 2 * H, :]
+    max_pair = cp.group()
+    for peer in plane:
+        cp.send(max_pair, s.max_own, s.max_in.at[c], peer, z)
+    cp.sent(max_pair, s.max_in.at[0 : ctx - 1])
+
+    wv.third()
+    wo.first()
+    wv.ready()
+
+    @pl.loop(0, p.vd // 256)
+    def _(i):
+        tile = at(i * 256, 256)
+        s.values[:, tile] = matmul(s.nin[...], s.wv[:, tile]).astype(LOW)
+
+    cp.got(max_pair, s.max_in.at[0 : ctx - 1])
+    s.max_in[c] = s.max_own[...]
+    top = s.max_in[0]
+    for i in range(1, ctx):
+        top = jnp.maximum(top, s.max_in[i])
+    s.max_all[...] = top
+    s.stat_t[0 : 2 * H, :] = top
+    max_columns = s.stat_t[...].T
+    s.stat[...] = jnp.zeros_like(s.stat)
+
+    def window(head):
+        low_lane = pl.multiple_of(lax.div(head * p.vhead, 128) * 128, 128)
+        return pl.ds(low_lane, 256), head * p.vhead - low_lane
+
+    def mask_of(rows, low_lane):
+        lane = lanes(rows, 256)
+        return ((lane >= low_lane) & (lane < low_lane + p.vhead)).astype(FULL)
+
+    def partial(seq):
+        s.numer[...] = jnp.zeros_like(s.numer)
+
+        @pl.loop(0, H)
+        def _(head):
+            i = seq * H + head
+            top = jnp.sum(jnp.where(lane_stat == i, max_columns, 0.0), axis=-1, keepdims=True)
+            weights = jnp.exp(s.scores[at(i * p.lat, p.lat), :] - top)
+            total = jnp.sum(weights, axis=-1, keepdims=True)
+            s.stat[...] = jnp.where(lane_stat == i, total, s.stat[...])
+            cols, low_lane = window(head)
+            part = s.values[at(seq * p.slots, p.slots), cols] * mask_of(p.slots, low_lane).astype(LOW)
+            s.numer[:, cols] += matmul(weights.astype(LOW), part)
+
+        s.stat_t[...] = s.stat[...].T
+        s.sums[seq] = s.stat_t[at(seq * H, H), :]
+
+    partial(other)
+    s.numer_low[...] = s.numer[...].astype(LOW)
+    pair_pair = cp.group()
+    sums_pair = cp.group()
+    cp.send(pair_pair, s.numer_low, s.numer_in, core, z)
+    cp.send(sums_pair, s.sums.at[other], s.sums_in, core, z)
+    cp.sent(pair_pair, s.numer_low)
+    cp.sent(sums_pair, s.sums_in)
+    partial(h)
+    wo.second()
+
+    cp.got(pair_pair, s.numer_in)
+    cp.got(sums_pair, s.sums_in)
+    quarter = p.lat // 4
+    s.chip[...] = (s.numer[...] + s.numer_in[...].astype(FULL)).astype(LOW)
+    s.chip_sums[...] = s.sums[h] + s.sums_in[...]
+    chip_pair = cp.group()
+    chip_sums_pair = cp.group()
+    for peer in chips:
+        peer_chip = lax.div(peer, 2)
+        cp.send(chip_pair, s.chip.at[at(peer_chip * quarter, quarter), :], s.chip_in.at[q], peer, z)
+        cp.send(chip_sums_pair, s.chip_sums, s.chip_sums_in.at[q], peer, z)
+    cp.sent(chip_pair, s.chip_in.at[0:3])
+    cp.sent(chip_sums_pair, s.chip_sums_in.at[0:3])
+    wu.first()
+    wo.third()
+
+    cp.got(chip_sums_pair, s.chip_sums_in.at[0:3])
+    s.chip_sums_in[q] = s.chip_sums[...]
+    sums = s.chip_sums_in
+    inverse = 1.0 / ((sums[0] + sums[1]) + (sums[2] + sums[3]))
+    s.stats[h, 0:H, :] = inverse
+    s.stat_t[0:H, :] = inverse
+    s.stat[...] = s.stat_t[...].T
+    s.scale[...] = jnp.zeros_like(s.scale)
+    own_quarter = s.stat[at(q * quarter, quarter), :]
+    for head in range(H):
+        low_lane = head * p.vhead // 128 * 128
+        lane = lanes(quarter, 256) + low_lane
+        inside = (lane >= head * p.vhead) & (lane < (head + 1) * p.vhead)
+        cols = slice(low_lane, low_lane + 256)
+        s.scale[:, cols] = jnp.where(inside, own_quarter[:, head : head + 1], s.scale[:, cols])
+    cp.got(chip_pair, s.chip_in.at[0:3])
+    s.chip_in[q] = s.chip[at(q * quarter, quarter), :]
+    numer = s.chip_in
+    added = (numer[0].astype(FULL) + numer[1].astype(FULL)) + (numer[2].astype(FULL) + numer[3].astype(FULL))
+    own_rows = at(h * p.lat + q * quarter, quarter)
+    s.att[own_rows, :] = (added * s.scale[...]).astype(LOW)
+    att_pair = cp.group()
+    for peer in chips:
+        cp.send(att_pair, s.att.at[own_rows, :], s.att.at[own_rows, :], peer, z)
+    cp.sent(att_pair, s.att.at[0 : 3 * quarter, :])
+    wu.second()
+    wd.first()
+    wo.ready()
+    own = at(h * p.lat, p.lat)
+    cp.got(att_pair, s.att.at[0 : 3 * quarter, :])
+
+    def share(ref):
+        pair = cp.group()
+        cp.send(pair, ref.at[own, :], ref.at[own, :], core, z)
+        cp.sent(pair, ref.at[0 : p.lat, :])
+        return pair
+
+    att_share = share(s.att)
+    tiles = p.dl // 256
+
+    @pl.loop(0, tiles)
+    def _(i):
+        tile = at(i * 256, 256)
+        s.hid[:, tile] = s.lat[:, tile].astype(FULL) + matmul(s.att[own, :], s.wo[:, tile])
+
+    wu.third()
+    wd.second()
+    gain_mlp, bias_mlp = vec[4:5, :], vec[5:6, :]
+
+    @pl.loop(0, p.lat // 64)
+    def _(i):
+        normed, _ = ln_parts(s.hid[at(i * 64, 64), :])
+        s.mid[at(h * p.lat + i * 64, 64), :] = (normed * gain_mlp + bias_mlp).astype(LOW)
+
+    mid_share = share(s.mid)
+    wu.ready()
+    load_cot.wait()
+
+    @pl.loop(0, tiles)
+    def _(i):
+        tile = at(i * 256, 256)
+        up = matmul(s.mid[own, :], s.wu[:, tile])
+        cdf = 0.5 * (1.0 + lax.erf(up * (1.0 / math.sqrt(2.0))))
+        density = jnp.exp(-0.5 * up * up) * (1.0 / math.sqrt(2.0 * math.pi))
+        s.act[own, tile] = (up * cdf).astype(LOW)
+        s.slope[:, tile] = cdf + up * density
+
+    act_share = share(s.act)
+    wd.third()
+    wd.ready()
+
+    @pl.loop(0, tiles)
+    def _(i):
+        tile = at(i * 256, 256)
+        dact = matmul_nt(s.cot[own, :], s.wd[tile, :])
+        s.dup[own, tile] = (dact * s.slope[:, tile]).astype(LOW)
+
+    dup_share = share(s.dup)
+
+    @pl.loop(0, tiles)
+    def _(i):
+        tile = at(i * 256, 256)
+        s.dmid[:, tile] = matmul_nt(s.dup[own, :], s.wu[tile, :])
+
+    s.vs[...] = jnp.zeros_like(s.vs)
+
+    @pl.loop(0, p.lat // 64)
+    def _(i):
+        rows = at(i * 64, 64)
+        full_rows = at(h * p.lat + i * 64, 64)
+        normed, scale = ln_parts(s.hid[rows, :])
+        grad = s.dmid[rows, :]
+        s.vs[0:1, :] += columns_sum(grad * normed)
+        s.vs[1:2, :] += columns_sum(grad)
+        total = s.cot[full_rows, :].astype(FULL) + ln_grad(grad, gain_mlp, normed, scale)
+        s.dhid[full_rows, :] = total.astype(LOW)
+
+    dhid_share = share(s.dhid)
+
+    @pl.loop(0, tiles)
+    def _(i):
+        tile = at(i * 256, 256)
+        s.datt[own, tile] = matmul_nt(s.dhid[own, :], s.wo[tile, :]).astype(LOW)
+
+    datt_share = share(s.datt)
+    s.stat[...] = jnp.zeros_like(s.stat)
+
+    @pl.loop(0, H)
+    def _(head):
+        cols, low_lane = window(head)
+        product = s.datt[own, cols].astype(FULL) * s.att[own, cols].astype(FULL)
+        delta = jnp.sum(product * mask_of(p.lat, low_lane), axis=-1, keepdims=True)
+        s.stat[...] = jnp.where(lane_stat == head, delta, s.stat[...])
+
+    s.stat_t[...] = s.stat[...].T
+    s.stats[h, H : 2 * H, :] = s.stat_t[0:H, :]
+    stats_pair = cp.group()
+    cp.send(stats_pair, s.stats.at[h], s.stats.at[h], core, z)
+    cp.sent(stats_pair, s.stats.at[0])
+
+    @pl.loop(0, tiles)
+    def _(i):
+        tile = at(i * 256, 256)
+        s.res[:, tile] = (s.hid[:, tile] + matmul(s.act[own, :], s.wd[:, tile])).astype(LOW)
+
+    res_pair = cp.group()
+    cp.send(res_pair, s.res, res_out.at[own, :], core, z)
+    cp.sent(res_pair, s.res)
+    stores = [cp.local(s.res, res_out.at[own, :])]
+
+    half_cols = at(h * (p.dl // 2), p.dl // 2)
+
+    class Reduce:
+        def __init__(self, left, right, grads, arrive, final, out):
+            self.left, self.right, self.out = left, right, out
+            self.grads, self.arrive, self.final = grads, arrive, final
+            self.part = self.final.shape[0]
+            self.rows = self.part * 4
+            self.pairs = [cp.group() for _ in range(3)]
+
+        def product(self):
+            @pl.loop(0, self.grads.shape[0] // 256)
+            def _(i):
+                rows = at(i * 256, 256)
+                self.grads[rows, :] = matmul_tn(self.left[:, rows], self.right[:, half_cols]).astype(LOW)
+
+        def block(self, zz):
+            return self.grads.at[at(zz * self.rows + q * self.part, self.part, 16), :]
+
+        def scatter(self):
+            for peer in zed:
+                cp.send(self.pairs[0], self.block(peer), self.arrive.at[z], c, peer)
+            cp.sent(self.pairs[0], self.arrive.at[0 : zs - 1])
+
+        def add(self):
+            cp.got(self.pairs[0], self.arrive.at[0 : zs - 1])
+            self.arrive[z] = self.grads[at(z * self.rows + q * self.part, self.part, 16), :]
+            total = self.arrive[0].astype(FULL)
+            for zz in range(1, zs):
+                total = total + self.arrive[zz].astype(FULL)
+            self.final[...] = total.astype(LOW)
+            here = self.out.at[at(q * self.part, self.part, 16), half_cols]
+            for peer in chips:
+                cp.send(self.pairs[1], self.final, here, peer, z)
+            cp.sent(self.pairs[1], self.arrive.at[0:3])
+            self.store = cp.local(self.final, here)
+
+        def spread(self):
+            cp.got(self.pairs[1], self.arrive.at[0:3])
+            self.store.wait()
+            block = self.out.at[:, half_cols]
+            cp.send(self.pairs[2], block, block, core, z)
+            cp.sent(self.pairs[2], block)
+
+        def done(self):
+            cp.got(self.pairs[2], self.out.at[:, half_cols])
+
+    down = Reduce(s.act, s.cot, s.dwd, s.zd, s.fd, gd)
+    upper = Reduce(s.mid, s.dup, s.dwu, s.zu, s.fu, gu)
+    outer = Reduce(s.att, s.dhid, s.dwo, s.zo, s.fo, go)
+    latents = Reduce(s.att, s.dhid, s.dlat, s.zl, s.fl, gl)
+
+    cp.got(act_share, s.act.at[0 : p.lat, :])
+    down.product()
+    down.scatter()
+    cp.got(mid_share, s.mid.at[0 : p.lat, :])
+    cp.got(dup_share, s.dup.at[0 : p.lat, :])
+    upper.product()
+    upper.scatter()
+    cp.got(att_share, s.att.at[0 : p.lat, :])
+    cp.got(dhid_share, s.dhid.at[0 : p.lat, :])
+    outer.product()
+    outer.scatter()
+    s.dlat[...] = (
+        s.dhid[0 : p.lat, half_cols].astype(FULL) + s.dhid[p.lat : 2 * p.lat, half_cols].astype(FULL)
+    ).astype(LOW)
+    latents.scatter()
+    cp.got(datt_share, s.datt.at[0 : p.lat, :])
+    cp.got(stats_pair, s.stats.at[0])
+
+    s.dq_t[...] = jnp.zeros_like(s.dq_t)
+    sublane = lax.broadcasted_iota(jnp.int32, (p.slots, p.lat), 0)
+
+    @pl.loop(0, p.seqs)
+    def _(seq):
+        slots = at(seq * p.slots, p.slots)
+        latent_rows = at(seq * p.lat, p.lat)
+        s.numer[...] = jnp.zeros_like(s.numer)
+        s.dk_sum[...] = jnp.zeros_like(s.dk_sum)
+
+        @pl.loop(0, H)
+        def _(head):
+            heads = at(head * p.lat, p.lat)
+            cols, low_lane = window(head)
+            raw = matmul_nt(s.keys[slots, :], s.qmask[heads, :])
+            valid = start_slot + sublane < lengths[seq]
+            top = s.max_all[pl.ds(seq * H + head, 1), :]
+            inverse = s.stats[seq, pl.ds(head, 1), :]
+            delta = s.stats[seq, pl.ds(H + head, 1), :]
+            probs = jnp.exp(jnp.where(valid, raw * score_scale, -1e30) - top) * inverse
+            grad = s.datt[latent_rows, cols] * mask_of(p.lat, low_lane).astype(LOW)
+            dprobs = matmul_nt(s.values[slots, cols], grad)
+            dscores = (probs * (dprobs - delta)).astype(LOW)
+            s.numer[:, cols] += matmul(probs.astype(LOW), grad)
+            s.dk_sum[...] += matmul(dscores, s.qmask[heads, :])
+            block = at(head * p.head, p.head)
+            s.dq_t[block, :] += matmul(s.keys_t[block, slots], dscores)
+
+        s.dkeys[slots, :] = (s.dk_sum[...] * score_scale).astype(LOW)
+        s.dvalues[slots, :] = s.numer[...].astype(LOW)
+
+    s.dq[...] = (s.dq_t[...] * score_scale).T.astype(LOW)
+    qhalf = p.qk // 2
+    dq_pairs = [cp.group() for _ in range(4)]
+    cp.send(dq_pairs[0], s.dq.at[:, at(other * qhalf, qhalf)], s.dq_in1, core, z)
+    cp.sent(dq_pairs[0], s.dq_in1)
+
+    def weight_grads(side):
+        kcols = at(side * qhalf, qhalf)
+        vcols = at(side * (p.vd // 2), p.vd // 2)
+
+        @pl.loop(0, p.din // 256)
+        def _(i):
+            rows = at(i * 256, 256)
+            s.swk[side, rows, :] = matmul(s.nin_t[rows, :], s.dkeys[:, kcols]).astype(LOW)
+            s.swv[side, rows, :] = matmul(s.nin_t[rows, :], s.dvalues[:, vcols]).astype(LOW)
+
+    weight_grads(other)
+    kv_pairs = [[cp.group() for _ in range(4)] for _ in range(2)]
+    for pairs, send, arrive in ((kv_pairs[0], s.swk, s.rwk), (kv_pairs[1], s.swv, s.rwv)):
+        cp.send(pairs[0], send.at[other], arrive, core, z)
+        cp.sent(pairs[0], arrive)
+    weight_grads(h)
+
+    down.add()
+    upper.add()
+    outer.add()
+    latents.add()
+    cp.got(dq_pairs[0], s.dq_in1)
+    s.dq_chip[...] = (
+        s.dq[:, at(h * qhalf, qhalf)].astype(FULL) + s.dq_in1[...].astype(FULL)
+    ).astype(LOW)
+    for peer in chips:
+        cp.send(dq_pairs[1], s.dq_chip, s.dq_in2.at[q], peer, z)
+    cp.sent(dq_pairs[1], s.dq_in2.at[0:3])
+
+    kv = (
+        (kv_pairs[0], s.swk, s.rwk, s.cwk, s.pwk_in, s.pwk, s.zwk_in, s.fwk, gk, qhalf),
+        (kv_pairs[1], s.swv, s.rwv, s.cwv, s.pwv_in, s.pwv, s.zwv_in, s.fwv, gv, p.vd // 2),
+    )
+    zrows = p.din // zs
+    vpart = zrows // 4
+    for pairs, send, arrive, chip, plane_in, plane_sum, z_in, final, out, width in kv:
+        cp.got(pairs[0], arrive)
+
+        @pl.loop(0, zs)
+        def _(zz):
+            rows = at(zz * zrows, zrows)
+            chip[zz] = (send[h, rows, :].astype(FULL) + arrive[rows, :].astype(FULL)).astype(LOW)
+
+        for peer in chips:
+            rows = at(lax.div(peer, 2) * vpart, vpart)
+            cp.send(pairs[1], chip.at[:, rows, :], plane_in.at[q], peer, z)
+        cp.sent(pairs[1], plane_in.at[0:3])
+
+    @pl.loop(0, p.rows_in // 64)
+    def _(i):
+        rows = at(i * 64, 64)
+        grad = matmul_nt(s.dkeys[rows, :], s.wk[...]) + matmul_nt(s.dvalues[rows, :], s.wv[...])
+        normed, scale = ln_parts(s.feats[rows, :].astype(FULL))
+        s.vs[2:3, 0 : p.din] += columns_sum(grad * normed)
+        s.vs[3:4, 0 : p.din] += columns_sum(grad)
+        s.bgrad[rows, :] = ln_grad(grad, vec[2:3, 0 : p.din], normed, scale).astype(LOW)
+
+    stores.append(cp.local(s.bgrad, byte_out))
+    vs_pairs = [cp.group() for _ in range(3)]
+    cp.send(vs_pairs[0], s.vs, s.vs_in1, core, z)
+    cp.sent(vs_pairs[0], s.vs)
+
+    cp.got(dq_pairs[1], s.dq_in2.at[0:3])
+    s.dq_in2[q] = s.dq_chip[...]
+    parts = s.dq_in2
+    s.dq_plane[...] = (
+        (parts[0].astype(FULL) + parts[1].astype(FULL)) + (parts[2].astype(FULL) + parts[3].astype(FULL))
+    ).astype(LOW)
+    for peer in zed:
+        cp.send(dq_pairs[2], s.dq_plane, s.dq_in3.at[z], c, peer)
+    cp.sent(dq_pairs[2], s.dq_in3.at[0 : zs - 1])
+
+    cp.got(vs_pairs[0], s.vs_in1)
+    s.vs_chip[...] = s.vs[...] + s.vs_in1[...]
+    for peer in chips:
+        cp.send(vs_pairs[1], s.vs_chip, s.vs_in2.at[q], peer, z)
+    cp.sent(vs_pairs[1], s.vs_in2.at[0:3])
+
+    for pairs, send, arrive, chip, plane_in, plane_sum, z_in, final, out, width in kv:
+        cp.got(pairs[1], plane_in.at[0:3])
+        for zz in range(zs):
+            plane_in[q, zz] = chip[zz, at(q * vpart, vpart, 16), :]
+        parts = plane_in
+        for zz in range(zs):
+            plane_sum[zz] = (
+                (parts[0, zz].astype(FULL) + parts[1, zz].astype(FULL))
+                + (parts[2, zz].astype(FULL) + parts[3, zz].astype(FULL))
+            ).astype(LOW)
+        for peer in zed:
+            cp.send(pairs[2], plane_sum.at[peer], z_in.at[z], c, peer)
+        cp.sent(pairs[2], z_in.at[0 : zs - 1])
+
+    cp.got(vs_pairs[1], s.vs_in2.at[0:3])
+    s.vs_in2[q] = s.vs_chip[...]
+    parts = s.vs_in2
+    total = (parts[0] + parts[1]) + (parts[2] + parts[3])
+    row_ids = lax.broadcasted_iota(jnp.int32, (8, p.dl), 0)
+    s.vs_plane[...] = jnp.where(row_ids < 2, s.vs_chip[...], total)
+    for peer in zed:
+        cp.send(vs_pairs[2], s.vs_plane, s.vs_in3.at[z], c, peer)
+    cp.sent(vs_pairs[2], s.vs_in3.at[0 : zs - 1])
+
+    reduces = (down, upper, outer, latents)
+    for reduce in reduces:
+        reduce.spread()
+
+    cp.got(dq_pairs[2], s.dq_in3.at[0 : zs - 1])
+    s.dq_in3[z] = s.dq_plane[...]
+    parts = s.dq_in3
+    total = parts[0].astype(FULL)
+    for zz in range(1, zs):
+        total = total + parts[zz].astype(FULL)
+    own_half = at(h * qhalf, qhalf)
+    s.dq_all[:, own_half] = total.astype(LOW)
+    cp.send(dq_pairs[3], s.dq_all.at[:, own_half], s.dq_all.at[:, own_half], core, z)
+    cp.sent(dq_pairs[3], s.dq_in1)
+
+    for pairs, send, arrive, chip, plane_in, plane_sum, z_in, final, out, width in kv:
+        cp.got(pairs[2], z_in.at[0 : zs - 1])
+        z_in[z] = plane_sum[z]
+        total = z_in[0].astype(FULL)
+        for zz in range(1, zs):
+            total = total + z_in[zz].astype(FULL)
+        final[...] = total.astype(LOW)
+        here = out.at[at(q * vpart, vpart, 16), at(h * width, width)]
+        for peer in plane:
+            cp.send(pairs[3], final, here, peer, z)
+        cp.sent(pairs[3], send.at[0, 0 : (ctx - 1) * vpart, :])
+        stores.append(cp.local(final, here))
+
+    cp.got(dq_pairs[3], s.dq_in1)
+
+    @pl.loop(0, tiles)
+    def _(i):
+        tile = at(i * 256, 256)
+        s.gq[tile, :] = matmul_tn(s.nlat[:, tile], s.dq_all[...])
+        s.dmid[:, tile] = matmul_nt(s.dq_all[...], s.wq[tile, :])
+
+    stores.append(cp.local(s.gq.at[at(z * (p.dl // zs), p.dl // zs, 16), :], gq_out))
+    cp.got(vs_pairs[2], s.vs_in3.at[0 : zs - 1])
+    s.vs_in3[z] = s.vs_plane[...]
+    total = s.vs_in3[0]
+    for zz in range(1, zs):
+        total = total + s.vs_in3[zz]
+    s.vs_all[...] = total
+    s.vs_all[4:6, :] = jnp.zeros((2, p.dl), FULL)
+
+    @pl.loop(0, p.lat // 64)
+    def _(i):
+        rows = at(i * 64, 64)
+        normed, scale = ln_parts(s.lat[rows, :].astype(FULL))
+        grad = s.dmid[rows, :]
+        s.vs_all[4:5, :] += columns_sum(grad * normed)
+        s.vs_all[5:6, :] += columns_sum(grad)
+        s.slope[rows, :] = ln_grad(grad, gain_lat, normed, scale)
+
+    stores.append(cp.local(s.slope.at[at(z * (p.lat // zs), p.lat // zs, 16), :], glat_out))
+    stores.append(cp.local(s.vs_all, vec_out))
+    for reduce in reduces:
+        reduce.done()
+    cp.got(res_pair, s.res)
+    for pairs, send, *_ in kv:
+        cp.got(pairs[3], send.at[0, 0 : (ctx - 1) * vpart, :])
+    for store in stores:
+        store.wait()
+    cp.drain()
+
+
+def finish_kernel(p, res, byte, go, gu, gd, gv, gk, gl, gq, glat, vec, *outs):
+    z = lax.axis_index("wshard")
+    outs[0][...] = res[...]
+    outs[1][...] = byte[...]
+    outs[2][...] = glat[...] + gl[...].astype(FULL)
+    for out, row in ((3, 4), (4, 5), (5, 2), (6, 3), (11, 0), (12, 1)):
+        size = outs[out].shape[1]
+        picked = vec[row : row + 1, 0:size]
+        for zz in range(1, p.zs):
+            picked = jnp.where(z == zz, vec[row : row + 1, zz * size : (zz + 1) * size], picked)
+        outs[out][...] = picked
+    outs[7][...] = gq[...]
+    for out, source in ((8, gk), (9, gv), (10, go), (13, gu), (14, gd)):
+        outs[out][...] = source[...].astype(FULL)
+
+
+def fused(*args):
+    (byte_feats, lengths, latent, *smalls, cot) = (args[0], args[1], args[2], *args[3:7], args[11], args[12], args[15])
+    w_query, w_key, w_value, w_output = args[7:11]
+    w_up, w_down = args[13:15]
+    seqs, slots, din = byte_feats.shape
+    ctx, zs = lax.axis_size("ctx"), lax.axis_size("wshard")
+    feats = byte_feats.reshape(seqs * slots, din)
+    cot_flat = cot.reshape(-1, cot.shape[-1])
+    smalls = [small.reshape(1, -1) for small in smalls]
+    p = Plan(ctx, zs, feats, latent, w_query, w_key, w_value, w_output, cot_flat)
+    table = scratch_table(p)
+    anywhere = pl.BlockSpec(memory_space=pl.ANY)
+    in_vmem = pl.BlockSpec(memory_space=pltpu.VMEM)
+    struct = jax.ShapeDtypeStruct
+    made = pl.pallas_call(
+        functools.partial(fused_kernel, p, tuple(table)),
+        out_shape=(
+            struct(cot_flat.shape, LOW),
+            struct(feats.shape, LOW),
+            struct(w_output.shape, LOW),
+            struct(w_up.shape, LOW),
+            struct(w_down.shape, LOW),
+            struct(w_value.shape, LOW),
+            struct(w_key.shape, LOW),
+            struct(latent.shape, LOW),
+            struct(w_query.shape, FULL),
+            struct(latent.shape, FULL),
+            struct((8, p.dl), FULL),
+        ),
+        in_specs=[pl.BlockSpec(memory_space=pltpu.SMEM)] + [anywhere] * 8 + [in_vmem] * 6 + [anywhere],
+        out_specs=(anywhere,) * 11,
+        scratch_shapes=[pltpu.VMEM(shape, kind) for shape, kind in table.values()]
+        + [pltpu.SemaphoreType.DMA((SEMS,))],
+        compiler_params=pltpu.CompilerParams(
+            collective_id=0, has_side_effects=True, vmem_limit_bytes=67043328
+        ),
+        name="block",
+    )(lengths, feats, latent, w_query, w_key, w_value, w_output, w_up, w_down, *smalls, cot_flat)
+    shapes = (
+        (cot_flat.shape, LOW),
+        (feats.shape, LOW),
+        (latent.shape, FULL),
+        *((smalls[i].shape, FULL) for i in range(4)),
+        *((w.shape, FULL) for w in (w_query, w_key, w_value, w_output)),
+        *((smalls[i].shape, FULL) for i in (4, 5)),
+        *((w.shape, FULL) for w in (w_up, w_down)),
+    )
+    outs = pl.pallas_call(
+        functools.partial(finish_kernel, p),
+        out_shape=tuple(struct(shape, kind) for shape, kind in shapes),
+        in_specs=[in_vmem] * 11,
+        out_specs=(in_vmem,) * 15,
+        compiler_params=pltpu.CompilerParams(vmem_limit_bytes=60 * 2**20),
+        name="finish",
+    )(*made)
+    return tuple(
+        out.reshape(-1) if out.shape[0] == 1 else out
+        for out in (outs[0].reshape(cot.shape), outs[1].reshape(byte_feats.shape), *outs[2:])
+    )
+
+
+def shards(*args):
+    if lax.axis_size("ctx") == 8 and lax.axis_size("wshard") == 4 and args[0].shape[0] == 2:
+        return fused(*args)
+    return plain(*args)
+
+
 def solution(mesh):
     sharded, plain = P("wshard", None), P("wshard")
     return jax.shard_map(

time: 929 us -> 190 us (0.20)
  waiting for transfers between devices: 580 us -> 0 us
  Pallas kernels: 0 us -> 177 us
  blocking collectives: 175 us -> 0 us
  matrix products: 76.5 us -> 0 us
  other arithmetic: 36.8 us -> 4.99 us
  local copies, waits for them, and re-layouts: 34.6 us -> 7.41 us
  between operations: 16.6 us -> 0.66 us
    reduce_scatter x6 -> x0, waiting for transfers between devices: 252 us -> none  [scatter(): lax.psum_scatter(total.astype(LOW), 'wshard', scatter_dimension=0, tiled=...]
    all_gather x4 -> x0, waiting for transfers between devices: 183 us -> none  [gather(): return lax.all_gather(shard, 'wshard', axis=0, tiled=True)]
    pallas_call x0 -> x2, Pallas kernels: none -> 177 us  [the longest x1 171 us: fused(): pl.pallas_call(functools.partial(fused_kernel, p, tuple(table)), out_shap...]
    psum x3 -> x0, waiting for transfers between devices: 143 us -> none  [the longest x1 55.3 us: shards(): lax.psum(scatter(matmul_tn(input_low, dkeys)).astype(LOW), 'ctx')]
    psum x3 -> x0, blocking collectives: 79.5 us -> none  [the longest x1 39.6 us: shards(): in_sums = lax.psum(jnp.concatenate([grad_gin, grad_bin]), ('ctx', 'wshard'))]
    dot_general x24 -> x0, matrix products: 76.5 us -> none  [the longest x6 22.2 us: matmul_nt(): lax.dot_general(left, right, (((1,), (1,)), ((), ())), preferred_element_...]
    all_gather x3 -> x0, blocking collectives: 53 us -> none  [gather(): return lax.all_gather(shard, 'wshard', axis=0, tiled=True)]
    convert_element_type x18 -> x0, other arithmetic: 22.8 us -> none  [the longest x3 7.25 us: scatter(): return lax.psum_scatter(total.astype(LOW), 'wshard', scatter_dimension=0,...]
  transfers between devices with their start and end apart: 13 -> 0, of which waited for: 12 -> 0; matrix products, arithmetic and copies ran while one was open for 10% -> 0% of each run, Pallas kernels for 0% -> 0%
where the time goes in v2:
time: 190 us
  Pallas kernels  177 us (93%)
  local copies, waits for them, and re-layouts  7.41 us (4%)
  other arithmetic  4.99 us (3%)
    pallas_call x1, Pallas kernels, fused(): pl.pallas_call(functools.partial(fused_kernel, p, tuple(table)), out_shap...  171 us
    reshape x6, local copies, waits for them, and re-layouts, fused(): smalls = [small.reshape(1, -1) for small in smalls]  7.41 us
    pallas_call x1, Pallas kernels, fused(): pl.pallas_call(functools.partial(finish_kernel, p), out_shape=tuple((stru...  6.43 us
    pallas_call x4, other arithmetic, fused(): pl.pallas_call(functools.partial(finish_kernel, p), out_shape=tuple((stru...  4.99 us

profile of v2, /device:TPU:0, one launch (start us, length us, event | category | flops | bytes accessed | tf_op | source)
XLA Modules:
  0.0 190.1 jit_solution(624949650748797725)
XLA Ops:
  0.6 1.2 reshape.81.refs_11_
  1.9 1.2 reshape.82.refs_12_
  3.1 1.2 reshape.79.refs_9_
  4.3 1.2 reshape.80.refs_10_
  5.6 1.2 reshape.83.refs_13_
  6.8 1.2 reshape.84.refs_14_
  8.1 170.7 %block.1 = (bf16[512,1280]{1,0:T(8,128)(2,1)}, bf16[512,768]{1,0:T(8,128)(2,1)}, bf16[320,1280]{1,0:T(8,128)(2,1)}, bf16[320,1280]{1,0:T(8,128)(2,1)}, bf16[320,...) custom-call(s32[2]{0:T(128)} %refs_0_.1, ...), custom_call_target="tpu_custom_call" | custom-call | tf_op jit(solution)/shard_map/block/pallas_call | solution.py:1038
  178.7 6.4 %finish.1 = (bf16[512,1280]{1,0:T(8,128)(2,1)}, bf16[512,768]{1,0:T(8,128)(2,1)}, f32[64,1280]{1,0:T(8,128)}, f32[1,320]{1,0:T(1,128)}, f32[1,320]{1,0:T(1,128)}...) custom-call(bf16[512,1280]{1,0:T(8,128)(2,1)} %get-tuple-element.41., ...), custom_call_target="tpu_custom_call" | custom-call | tf_op jit(solution)/shard_map/finish/pallas_call | solution.py:1071
  185.2 1.3 reduce
  186.4 1.3 reduce.1
  187.7 1.2 reduce.2
  188.9 1.2 reduce.3

commit v3 on v2

--- a/solution.py
+++ b/solution.py
@@ -47,7 +47,7 @@
     ).astype(FULL)
 
 
-SEMS = 160
+SEMS = 224
 
 
 def own_part(total, shard):
@@ -382,17 +382,18 @@
 
     load_feats = cp.local(feats_in, s.feats)
     for row, ref in enumerate(smalls):
-        s.small_own[row : row + 1, 0 : ref.shape[1]] = ref[...].astype(FULL)
+        s.small_own[row : row + 1, 0 : ref.shape[0]] = ref[...].reshape(1, -1).astype(FULL)
     small_pair = cp.group()
     for peer in zed:
         cp.send(small_pair, s.small_own, s.small.at[z], c, peer)
     cp.sent(small_pair, s.small.at[0 : zs - 1])
 
     class Weight:
-        def __init__(self, ref, source):
-            self.ref, self.source = ref, source
+        def __init__(self, ref, source, cuts):
+            self.ref, self.source, self.cuts = ref, source, cuts
             self.rows, cols = source.shape
-            self.part, self.cols = self.rows // 4, cols // 2
+            self.part, self.cols = self.rows // cuts, cols // 2
+            self.slot = q if cuts == 4 else lax.rem(x + y, 2)
             self.mine = at(h * self.cols, self.cols)
             self.pairs = [cp.group() for _ in range(4)]
 
@@ -406,8 +407,8 @@
             for peer in zed:
                 cp.send(
                     self.pairs[0],
-                    self.source.at[at(q * self.part, self.part, 16), self.mine],
-                    self.block(z, q),
+                    self.source.at[at(self.slot * self.part, self.part, 16), self.mine],
+                    self.block(z, self.slot),
                     c,
                     peer,
                 )
@@ -417,7 +418,7 @@
         def first(self):
             cp.got(self.pairs[0], self.view(3 * self.part))
             for zz in zed:
-                block = self.block(zz, q)
+                block = self.block(zz, self.slot)
                 cp.send(self.pairs[1], block, block, near[0], z)
             cp.sent(self.pairs[1], self.view(3 * self.part))
 
@@ -430,7 +431,10 @@
             cp.sent(self.pairs[2], self.view(6 * self.part))
 
         def third(self):
-            cp.got(self.pairs[2], self.view(6 * self.part))
+            if self.cuts == 4:
+                cp.got(self.pairs[2], self.view(6 * self.part))
+            else:
+                cp.got(self.pairs[1], self.view(3 * self.part))
             for zz in zed:
                 block = self.ref.at[at(zz * self.rows, self.rows, 16), self.mine]
                 cp.send(self.pairs[3], block, block, core, z)
@@ -440,9 +444,9 @@
             cp.got(self.pairs[3], self.view(3 * self.rows))
             self.load.wait()
 
-    wk, wq, lat = Weight(s.wk, wk_in), Weight(s.wq, wq_in), Weight(s.lat, lat_in)
-    wv = Weight(s.wv, wv_in)
-    wo, wu, wd = Weight(s.wo, wo_in), Weight(s.wu, wu_in), Weight(s.wd, wd_in)
+    wk, wq, lat = Weight(s.wk, wk_in, 4), Weight(s.wq, wq_in, 4), Weight(s.lat, lat_in, 4)
+    wv, wo = Weight(s.wv, wv_in, 4), Weight(s.wo, wo_in, 4)
+    wu, wd = Weight(s.wu, wu_in, 2), Weight(s.wd, wd_in, 2)
     for weight in (wk, wq, lat, wv, wo, wu, wd):
         weight.start()
     load_cot = cp.local(cot_in, s.cot)
@@ -450,7 +454,7 @@
     cp.got(small_pair, s.small.at[0 : zs - 1])
     s.small[z] = s.small_own[...]
     for row, ref in enumerate(smalls):
-        size = ref.shape[1]
+        size = ref.shape[0]
         for zz in range(zs):
             s.vec[row : row + 1, zz * size : (zz + 1) * size] = s.small[zz, row : row + 1, 0:size]
     vec = s.vec
@@ -476,7 +480,6 @@
     wk.second()
     wq.second()
     lat.second()
-    wv.first()
     wk.third()
     wq.third()
     lat.third()
@@ -489,7 +492,7 @@
         s.keys[rows, :] = low
         s.keys_t[:, rows] = low.T
 
-    wv.second()
+    wv.first()
     lat.ready()
 
     @pl.loop(0, p.lat // 64)
@@ -505,6 +508,7 @@
         inside = (lane_q >= head * p.head) & (lane_q < (head + 1) * p.head)
         s.qmask[head * p.lat : (head + 1) * p.lat, :] = jnp.where(inside, queries, 0.0).astype(LOW)
 
+    wv.second()
     score_scale = 1.0 / math.sqrt(p.head)
     start_slot = c * p.slots
     s.stat[...] = jnp.zeros_like(s.stat)
@@ -538,6 +542,7 @@
         tile = at(i * 256, 256)
         s.values[:, tile] = matmul(s.nin[...], s.wv[:, tile]).astype(LOW)
 
+    wo.second()
     cp.got(max_pair, s.max_in.at[0 : ctx - 1])
     s.max_in[c] = s.max_own[...]
     top = s.max_in[0]
@@ -582,7 +587,6 @@
     cp.sent(pair_pair, s.numer_low)
     cp.sent(sums_pair, s.sums_in)
     partial(h)
-    wo.second()
 
     cp.got(pair_pair, s.numer_in)
     cp.got(sums_pair, s.sums_in)
@@ -625,8 +629,6 @@
     for peer in chips:
         cp.send(att_pair, s.att.at[own_rows, :], s.att.at[own_rows, :], peer, z)
     cp.sent(att_pair, s.att.at[0 : 3 * quarter, :])
-    wu.second()
-    wd.first()
     wo.ready()
     own = at(h * p.lat, p.lat)
     cp.got(att_pair, s.att.at[0 : 3 * quarter, :])
@@ -638,6 +640,7 @@
         return pair
 
     att_share = share(s.att)
+    wd.first()
     tiles = p.dl // 256
 
     @pl.loop(0, tiles)
@@ -646,7 +649,6 @@
         s.hid[:, tile] = s.lat[:, tile].astype(FULL) + matmul(s.att[own, :], s.wo[:, tile])
 
     wu.third()
-    wd.second()
     gain_mlp, bias_mlp = vec[4:5, :], vec[5:6, :]
 
     @pl.loop(0, p.lat // 64)
@@ -666,69 +668,6 @@
         density = jnp.exp(-0.5 * up * up) * (1.0 / math.sqrt(2.0 * math.pi))
         s.act[own, tile] = (up * cdf).astype(LOW)
         s.slope[:, tile] = cdf + up * density
-
-    act_share = share(s.act)
-    wd.third()
-    wd.ready()
-
-    @pl.loop(0, tiles)
-    def _(i):
-        tile = at(i * 256, 256)
-        dact = matmul_nt(s.cot[own, :], s.wd[tile, :])
-        s.dup[own, tile] = (dact * s.slope[:, tile]).astype(LOW)
-
-    dup_share = share(s.dup)
-
-    @pl.loop(0, tiles)
-    def _(i):
-        tile = at(i * 256, 256)
-        s.dmid[:, tile] = matmul_nt(s.dup[own, :], s.wu[tile, :])
-
-    s.vs[...] = jnp.zeros_like(s.vs)
-
-    @pl.loop(0, p.lat // 64)
-    def _(i):
-        rows = at(i * 64, 64)
-        full_rows = at(h * p.lat + i * 64, 64)
-        normed, scale = ln_parts(s.hid[rows, :])
-        grad = s.dmid[rows, :]
-        s.vs[0:1, :] += columns_sum(grad * normed)
-        s.vs[1:2, :] += columns_sum(grad)
-        total = s.cot[full_rows, :].astype(FULL) + ln_grad(grad, gain_mlp, normed, scale)
-        s.dhid[full_rows, :] = total.astype(LOW)
-
-    dhid_share = share(s.dhid)
-
-    @pl.loop(0, tiles)
-    def _(i):
-        tile = at(i * 256, 256)
-        s.datt[own, tile] = matmul_nt(s.dhid[own, :], s.wo[tile, :]).astype(LOW)
-
-    datt_share = share(s.datt)
-    s.stat[...] = jnp.zeros_like(s.stat)
-
-    @pl.loop(0, H)
-    def _(head):
-        cols, low_lane = window(head)
-        product = s.datt[own, cols].astype(FULL) * s.att[own, cols].astype(FULL)
-        delta = jnp.sum(product * mask_of(p.lat, low_lane), axis=-1, keepdims=True)
-        s.stat[...] = jnp.where(lane_stat == head, delta, s.stat[...])
-
-    s.stat_t[...] = s.stat[...].T
-    s.stats[h, H : 2 * H, :] = s.stat_t[0:H, :]
-    stats_pair = cp.group()
-    cp.send(stats_pair, s.stats.at[h], s.stats.at[h], core, z)
-    cp.sent(stats_pair, s.stats.at[0])
-
-    @pl.loop(0, tiles)
-    def _(i):
-        tile = at(i * 256, 256)
-        s.res[:, tile] = (s.hid[:, tile] + matmul(s.act[own, :], s.wd[:, tile])).astype(LOW)
-
-    res_pair = cp.group()
-    cp.send(res_pair, s.res, res_out.at[own, :], core, z)
-    cp.sent(res_pair, s.res)
-    stores = [cp.local(s.res, res_out.at[own, :])]
 
     half_cols = at(h * (p.dl // 2), p.dl // 2)
 
@@ -782,21 +721,67 @@
     outer = Reduce(s.att, s.dhid, s.dwo, s.zo, s.fo, go)
     latents = Reduce(s.att, s.dhid, s.dlat, s.zl, s.fl, gl)
 
+    act_share = share(s.act)
+    wd.third()
     cp.got(act_share, s.act.at[0 : p.lat, :])
     down.product()
     down.scatter()
+    wd.ready()
+
+    @pl.loop(0, tiles)
+    def _(i):
+        tile = at(i * 256, 256)
+        dact = matmul_nt(s.cot[own, :], s.wd[tile, :])
+        s.dup[own, tile] = (dact * s.slope[:, tile]).astype(LOW)
+
+    dup_share = share(s.dup)
+
+    @pl.loop(0, tiles)
+    def _(i):
+        tile = at(i * 256, 256)
+        s.dmid[:, tile] = matmul_nt(s.dup[own, :], s.wu[tile, :])
+
+    s.vs[...] = jnp.zeros_like(s.vs)
+
+    @pl.loop(0, p.lat // 64)
+    def _(i):
+        rows = at(i * 64, 64)
+        full_rows = at(h * p.lat + i * 64, 64)
+        normed, scale = ln_parts(s.hid[rows, :])
+        grad = s.dmid[rows, :]
+        s.vs[0:1, :] += columns_sum(grad * normed)
+        s.vs[1:2, :] += columns_sum(grad)
+        total = s.cot[full_rows, :].astype(FULL) + ln_grad(grad, gain_mlp, normed, scale)
+        s.dhid[full_rows, :] = total.astype(LOW)
+
+    dhid_share = share(s.dhid)
+
+    @pl.loop(0, tiles)
+    def _(i):
+        tile = at(i * 256, 256)
+        s.datt[own, tile] = matmul_nt(s.dhid[own, :], s.wo[tile, :]).astype(LOW)
+
+    datt_share = share(s.datt)
+    s.stat[...] = jnp.zeros_like(s.stat)
+
+    @pl.loop(0, H)
+    def _(head):
+        cols, low_lane = window(head)
+        product = s.datt[own, cols].astype(FULL) * s.att[own, cols].astype(FULL)
+        delta = jnp.sum(product * mask_of(p.lat, low_lane), axis=-1, keepdims=True)
+        s.stat[...] = jnp.where(lane_stat == head, delta, s.stat[...])
+
+    s.stat_t[...] = s.stat[...].T
+    s.stats[h, H : 2 * H, :] = s.stat_t[0:H, :]
+    stats_pair = cp.group()
+    cp.send(stats_pair, s.stats.at[h], s.stats.at[h], core, z)
+    cp.sent(stats_pair, s.stats.at[0])
+
     cp.got(mid_share, s.mid.at[0 : p.lat, :])
     cp.got(dup_share, s.dup.at[0 : p.lat, :])
     upper.product()
     upper.scatter()
-    cp.got(att_share, s.att.at[0 : p.lat, :])
-    cp.got(dhid_share, s.dhid.at[0 : p.lat, :])
-    outer.product()
-    outer.scatter()
-    s.dlat[...] = (
-        s.dhid[0 : p.lat, half_cols].astype(FULL) + s.dhid[p.lat : 2 * p.lat, half_cols].astype(FULL)
-    ).astype(LOW)
-    latents.scatter()
+    down.add()
     cp.got(datt_share, s.datt.at[0 : p.lat, :])
     cp.got(stats_pair, s.stats.at[0])
 
@@ -848,16 +833,69 @@
             s.swv[side, rows, :] = matmul(s.nin_t[rows, :], s.dvalues[:, vcols]).astype(LOW)
 
     weight_grads(other)
-    kv_pairs = [[cp.group() for _ in range(4)] for _ in range(2)]
-    for pairs, send, arrive in ((kv_pairs[0], s.swk, s.rwk), (kv_pairs[1], s.swv, s.rwv)):
-        cp.send(pairs[0], send.at[other], arrive, core, z)
-        cp.sent(pairs[0], arrive)
+    zrows = p.din // zs
+    vpart = zrows // 4
+
+    class Local:
+        def __init__(self, grads, arrive, chip, plane_in, plane, z_in, final, out):
+            self.grads, self.arrive, self.chip, self.plane_in = grads, arrive, chip, plane_in
+            self.plane, self.z_in, self.final, self.out = plane, z_in, final, out
+            self.width = final.shape[1]
+            self.pairs = [cp.group() for _ in range(4)]
+            self.chunks = [cp.group() for _ in range(zs)]
+
+        def pair(self):
+            cp.send(self.pairs[0], self.grads.at[other], self.arrive, core, z)
+            cp.sent(self.pairs[0], self.arrive)
+
+        def chunk(self, i, zz):
+            rows = at(zz * zrows, zrows)
+            total = self.grads[h, rows, :].astype(FULL) + self.arrive[rows, :].astype(FULL)
+            self.chip[zz] = total.astype(LOW)
+            for peer in chips:
+                rows = at(lax.div(peer, 2) * vpart, vpart)
+                cp.send(self.chunks[i], self.chip.at[zz, rows, :], self.plane_in.at[q, zz], peer, z)
+            cp.sent(self.chunks[i], self.plane_in.at[0, 0:3])
+
+        def add(self, i, zz):
+            cp.got(self.chunks[i], self.plane_in.at[0, 0:3])
+            self.plane_in[q, zz] = self.chip[zz, at(q * vpart, vpart, 16), :]
+            parts = [self.plane_in[qq, zz].astype(FULL) for qq in range(4)]
+            self.plane[zz] = ((parts[0] + parts[1]) + (parts[2] + parts[3])).astype(LOW)
+            if i < zs - 1:
+                cp.send(self.pairs[1], self.plane.at[zz], self.z_in.at[z], c, zz)
+            else:
+                cp.sent(self.pairs[1], self.z_in.at[0 : zs - 1])
+
+        def finish(self):
+            cp.got(self.pairs[1], self.z_in.at[0 : zs - 1])
+            self.z_in[z] = self.plane[z]
+            total = self.z_in[0].astype(FULL)
+            for zz in range(1, zs):
+                total = total + self.z_in[zz].astype(FULL)
+            self.final[...] = total.astype(LOW)
+            here = self.out.at[at(q * vpart, vpart, 16), at(h * self.width, self.width)]
+            for peer in chips:
+                cp.send(self.pairs[2], self.final, here, peer, z)
+            cp.sent(self.pairs[2], self.z_in.at[0:3])
+            self.store = cp.local(self.final, here)
+
+        def spread(self):
+            cp.got(self.pairs[2], self.z_in.at[0:3])
+            self.store.wait()
+            block = self.out.at[:, at(h * self.width, self.width)]
+            cp.send(self.pairs[3], block, block, core, z)
+            cp.sent(self.pairs[3], block)
+
+        def done(self):
+            cp.got(self.pairs[3], self.out.at[:, at(h * self.width, self.width)])
+
+    key_grads = Local(s.swk, s.rwk, s.cwk, s.pwk_in, s.pwk, s.zwk_in, s.fwk, gk)
+    value_grads = Local(s.swv, s.rwv, s.cwv, s.pwv_in, s.pwv, s.zwv_in, s.fwv, gv)
+    kv = (value_grads, key_grads)
+    for grads in kv:
+        grads.pair()
     weight_grads(h)
-
-    down.add()
-    upper.add()
-    outer.add()
-    latents.add()
     cp.got(dq_pairs[0], s.dq_in1)
     s.dq_chip[...] = (
         s.dq[:, at(h * qhalf, qhalf)].astype(FULL) + s.dq_in1[...].astype(FULL)
@@ -865,40 +903,42 @@
     for peer in chips:
         cp.send(dq_pairs[1], s.dq_chip, s.dq_in2.at[q], peer, z)
     cp.sent(dq_pairs[1], s.dq_in2.at[0:3])
-
-    kv = (
-        (kv_pairs[0], s.swk, s.rwk, s.cwk, s.pwk_in, s.pwk, s.zwk_in, s.fwk, gk, qhalf),
-        (kv_pairs[1], s.swv, s.rwv, s.cwv, s.pwv_in, s.pwv, s.zwv_in, s.fwv, gv, p.vd // 2),
-    )
-    zrows = p.din // zs
-    vpart = zrows // 4
-    for pairs, send, arrive, chip, plane_in, plane_sum, z_in, final, out, width in kv:
-        cp.got(pairs[0], arrive)
-
-        @pl.loop(0, zs)
-        def _(zz):
-            rows = at(zz * zrows, zrows)
-            chip[zz] = (send[h, rows, :].astype(FULL) + arrive[rows, :].astype(FULL)).astype(LOW)
-
-        for peer in chips:
-            rows = at(lax.div(peer, 2) * vpart, vpart)
-            cp.send(pairs[1], chip.at[:, rows, :], plane_in.at[q], peer, z)
-        cp.sent(pairs[1], plane_in.at[0:3])
-
-    @pl.loop(0, p.rows_in // 64)
-    def _(i):
-        rows = at(i * 64, 64)
-        grad = matmul_nt(s.dkeys[rows, :], s.wk[...]) + matmul_nt(s.dvalues[rows, :], s.wv[...])
-        normed, scale = ln_parts(s.feats[rows, :].astype(FULL))
-        s.vs[2:3, 0 : p.din] += columns_sum(grad * normed)
-        s.vs[3:4, 0 : p.din] += columns_sum(grad)
-        s.bgrad[rows, :] = ln_grad(grad, vec[2:3, 0 : p.din], normed, scale).astype(LOW)
-
-    stores.append(cp.local(s.bgrad, byte_out))
+    for grads in kv:
+        cp.got(grads.pairs[0], grads.arrive)
+    order = [*zed, z]
+    for i, zz in enumerate(order):
+        for grads in kv:
+            grads.chunk(i, zz)
+
+    cp.got(att_share, s.att.at[0 : p.lat, :])
+    cp.got(dhid_share, s.dhid.at[0 : p.lat, :])
+    outer.product()
+    outer.scatter()
+    s.dlat[...] = (
+        s.dhid[0 : p.lat, half_cols].astype(FULL) + s.dhid[p.lat : 2 * p.lat, half_cols].astype(FULL)
+    ).astype(LOW)
+    latents.scatter()
+    down.spread()
+
+    def byte_part(part):
+        @pl.loop(part * 2, part * 2 + 2)
+        def _(i):
+            rows = at(i * 64, 64)
+            grad = matmul_nt(s.dkeys[rows, :], s.wk[...]) + matmul_nt(s.dvalues[rows, :], s.wv[...])
+            normed, scale = ln_parts(s.feats[rows, :].astype(FULL))
+            s.vs[2:3, 0 : p.din] += columns_sum(grad * normed)
+            s.vs[3:4, 0 : p.din] += columns_sum(grad)
+            s.bgrad[rows, :] = ln_grad(grad, vec[2:3, 0 : p.din], normed, scale).astype(LOW)
+
+    for i, zz in enumerate(order):
+        for grads in kv:
+            grads.add(i, zz)
+        byte_part(i)
+
+    stores = [cp.local(s.bgrad, byte_out)]
     vs_pairs = [cp.group() for _ in range(3)]
     cp.send(vs_pairs[0], s.vs, s.vs_in1, core, z)
     cp.sent(vs_pairs[0], s.vs)
-
     cp.got(dq_pairs[1], s.dq_in2.at[0:3])
     s.dq_in2[q] = s.dq_chip[...]
     parts = s.dq_in2
@@ -908,27 +948,25 @@
     for peer in zed:
         cp.send(dq_pairs[2], s.dq_plane, s.dq_in3.at[z], c, peer)
     cp.sent(dq_pairs[2], s.dq_in3.at[0 : zs - 1])
-
     cp.got(vs_pairs[0], s.vs_in1)
     s.vs_chip[...] = s.vs[...] + s.vs_in1[...]
     for peer in chips:
         cp.send(vs_pairs[1], s.vs_chip, s.vs_in2.at[q], peer, z)
     cp.sent(vs_pairs[1], s.vs_in2.at[0:3])
-
-    for pairs, send, arrive, chip, plane_in, plane_sum, z_in, final, out, width in kv:
-        cp.got(pairs[1], plane_in.at[0:3])
-        for zz in range(zs):
-            plane_in[q, zz] = chip[zz, at(q * vpart, vpart, 16), :]
-        parts = plane_in
-        for zz in range(zs):
-            plane_sum[zz] = (
-                (parts[0, zz].astype(FULL) + parts[1, zz].astype(FULL))
-                + (parts[2, zz].astype(FULL) + parts[3, zz].astype(FULL))
-            ).astype(LOW)
-        for peer in zed:
-            cp.send(pairs[2], plane_sum.at[peer], z_in.at[z], c, peer)
-        cp.sent(pairs[2], z_in.at[0 : zs - 1])
-
+    upper.add()
+
+    @pl.loop(0, tiles)
+    def _(i):
+        tile = at(i * 256, 256)
+        s.res[:, tile] = (s.hid[:, tile] + matmul(s.act[own, :], s.wd[:, tile])).astype(LOW)
+
+    res_pair = cp.group()
+    cp.send(res_pair, s.res, res_out.at[own, :], core, z)
+    cp.sent(res_pair, s.res)
+    stores.append(cp.local(s.res, res_out.at[own, :]))
+
+    for grads in kv:
+        grads.finish()
     cp.got(vs_pairs[1], s.vs_in2.at[0:3])
     s.vs_in2[q] = s.vs_chip[...]
     parts = s.vs_in2
@@ -938,11 +976,6 @@
     for peer in zed:
         cp.send(vs_pairs[2], s.vs_plane, s.vs_in3.at[z], c, peer)
     cp.sent(vs_pairs[2], s.vs_in3.at[0 : zs - 1])
-
-    reduces = (down, upper, outer, latents)
-    for reduce in reduces:
-        reduce.spread()
-
     cp.got(dq_pairs[2], s.dq_in3.at[0 : zs - 1])
     s.dq_in3[z] = s.dq_plane[...]
     parts = s.dq_in3
@@ -953,20 +986,12 @@
     s.dq_all[:, own_half] = total.astype(LOW)
     cp.send(dq_pairs[3], s.dq_all.at[:, own_half], s.dq_all.at[:, own_half], core, z)
     cp.sent(dq_pairs[3], s.dq_in1)
-
-    for pairs, send, arrive, chip, plane_in, plane_sum, z_in, final, out, width in kv:
-        cp.got(pairs[2], z_in.at[0 : zs - 1])
-        z_in[z] = plane_sum[z]
-        total = z_in[0].astype(FULL)
-        for zz in range(1, zs):
-            total = total + z_in[zz].astype(FULL)
-        final[...] = total.astype(LOW)
-        here = out.at[at(q * vpart, vpart, 16), at(h * width, width)]
-        for peer in plane:
-            cp.send(pairs[3], final, here, peer, z)
-        cp.sent(pairs[3], send.at[0, 0 : (ctx - 1) * vpart, :])
-        stores.append(cp.local(final, here))
-
+    outer.add()
+    latents.add()
+    upper.spread()
+    reduces = (down, upper, outer, latents)
+    for grads in kv:
+        grads.spread()
     cp.got(dq_pairs[3], s.dq_in1)
 
     @pl.loop(0, tiles)
@@ -995,11 +1020,11 @@
 
     stores.append(cp.local(s.slope.at[at(z * (p.lat // zs), p.lat // zs, 16), :], glat_out))
     stores.append(cp.local(s.vs_all, vec_out))
-    for reduce in reduces:
+    outer.spread()
+    latents.spread()
+    for reduce in (*reduces, *kv):
         reduce.done()
     cp.got(res_pair, s.res)
-    for pairs, send, *_ in kv:
-        cp.got(pairs[3], send.at[0, 0 : (ctx - 1) * vpart, :])
     for store in stores:
         store.wait()
     cp.drain()
@@ -1011,11 +1036,11 @@
     outs[1][...] = byte[...]
     outs[2][...] = glat[...] + gl[...].astype(FULL)
     for out, row in ((3, 4), (4, 5), (5, 2), (6, 3), (11, 0), (12, 1)):
-        size = outs[out].shape[1]
+        size = outs[out].shape[0]
         picked = vec[row : row + 1, 0:size]
         for zz in range(1, p.zs):
             picked = jnp.where(z == zz, vec[row : row + 1, zz * size : (zz + 1) * size], picked)
-        outs[out][...] = picked
+        outs[out][...] = picked.reshape(size)
     outs[7][...] = gq[...]
     for out, source in ((8, gk), (9, gv), (10, go), (13, gu), (14, gd)):
         outs[out][...] = source[...].astype(FULL)
@@ -1029,7 +1054,6 @@
     ctx, zs = lax.axis_size("ctx"), lax.axis_size("wshard")
     feats = byte_feats.reshape(seqs * slots, din)
     cot_flat = cot.reshape(-1, cot.shape[-1])
-    smalls = [small.reshape(1, -1) for small in smalls]
     p = Plan(ctx, zs, feats, latent, w_query, w_key, w_value, w_output, cot_flat)
     table = scratch_table(p)
     anywhere = pl.BlockSpec(memory_space=pl.ANY)
@@ -1076,10 +1100,7 @@
         compiler_params=pltpu.CompilerParams(vmem_limit_bytes=60 * 2**20),
         name="finish",
     )(*made)
-    return tuple(
-        out.reshape(-1) if out.shape[0] == 1 else out
-        for out in (outs[0].reshape(cot.shape), outs[1].reshape(byte_feats.shape), *outs[2:])
-    )
+    return (outs[0].reshape(cot.shape), outs[1].reshape(byte_feats.shape), *outs[2:])
 
 
 def shards(*args):

time: 190 us -> 162 us (0.85)
  Pallas kernels: 177 us -> 160 us
  local copies, waits for them, and re-layouts: 7.41 us -> 0 us
  other arithmetic: 4.99 us -> 0 us
    pallas_call x1, Pallas kernels: 171 us -> 154 us  [fused(): pl.pallas_call(functools.partial(fused_kernel, p, tuple(table)), out_shap...]
    reshape x6 -> x0, local copies, waits for them, and re-layouts: 7.41 us -> none  [fused(): smalls = [small.reshape(1, -1) for small in smalls]]
    pallas_call x4 -> x0, other arithmetic: 4.99 us -> none  [fused(): pl.pallas_call(functools.partial(finish_kernel, p), out_shape=tuple((stru...]
where the time goes in v3:
time: 162 us; the launch traced here: 161 us
  Pallas kernels  160 us (99%)
    pallas_call x1, Pallas kernels, fused(): pl.pallas_call(functools.partial(fused_kernel, p, tuple(table)), out_shap...  154 us
    pallas_call x1, Pallas kernels, fused(): pl.pallas_call(functools.partial(finish_kernel, p), out_shape=tuple((stru...  6.43 us

profile of v3, /device:TPU:0, one launch (start us, length us, event | category | flops | bytes accessed | tf_op | source)
XLA Modules:
  0.0 161.0 jit_solution(11162427282416501584)
XLA Ops:
  0.7 153.9 %block.1 = (bf16[512,1280]{1,0:T(8,128)(2,1)}, bf16[512,768]{1,0:T(8,128)(2,1)}, bf16[320,1280]{1,0:T(8,128)(2,1)}, bf16[320,1280]{1,0:T(8,128)(2,1)}, bf16[320,...) custom-call(s32[2]{0:T(128)} %refs_0_.1, ...), custom_call_target="tpu_custom_call" | custom-call | tf_op jit(solution)/shard_map/block/pallas_call | solution.py:1062
  154.6 6.4 %finish.1 = (bf16[512,1280]{1,0:T(8,128)(2,1)}, bf16[512,768]{1,0:T(8,128)(2,1)}, f32[64,1280]{1,0:T(8,128)}, f32[320]{0:T(512)}, f32[320]{0:T(512)}, /*index=5*...) custom-call(bf16[512,1280]{1,0:T(8,128)(2,1)} %get-tuple-element.41., ...), custom_call_target="tpu_custom_call" | custom-call | tf_op jit(solution)/shard_map/finish/pallas_call | solution.py:1095

commit v4 on v3

--- a/solution.py
+++ b/solution.py
@@ -47,7 +47,7 @@
     ).astype(FULL)
 
 
-SEMS = 224
+SEMS = 256
 
 
 def own_part(total, shard):
@@ -235,9 +235,10 @@
         values=((p.rows_in, p.vd), LOW),
         nlat=((p.lat, p.dl), LOW),
         qmask=((H * p.lat, p.qk), LOW),
-        scores=((p.seqs * H * p.lat, p.slots), FULL),
+        scores=((p.seqs * H * max(p.lat, p.slots), max(p.lat, p.slots)), FULL),
         stat=((p.lat, 128), FULL),
         stat_t=((128, p.lat), FULL),
+        max_t=((p.lat, 128), FULL),
         max_own=((2 * H, p.lat), FULL),
         max_in=((p.ctx, 2 * H, p.lat), FULL),
         max_all=((2 * H, p.lat), FULL),
@@ -341,12 +342,16 @@
     def got(self, pair, view):
         pltpu.make_async_copy(view, view, pair[1]).wait()
 
-    def sent(self, pair, view):
-        self.open.append((pair[0], view))
+    def sent(self, pair, view, when=None):
+        self.open.append((pair[0], view, when))
 
     def drain(self):
-        for sem, view in self.open:
-            pltpu.make_async_copy(view, view, sem).wait()
+        for sem, view, when in self.open:
+            wait = pltpu.make_async_copy(view, view, sem).wait
+            if when is None:
+                wait()
+            else:
+                pl.when(when)(wait)
 
 
 def at(start, size, step=None):
@@ -389,8 +394,11 @@
     cp.sent(small_pair, s.small.at[0 : zs - 1])
 
     class Weight:
-        def __init__(self, ref, source, cuts):
-            self.ref, self.source, self.cuts = ref, source, cuts
+        def __init__(self, ref, source, cuts, line):
+            self.ref, self.source, self.cuts, self.line = ref, source, cuts, line
+            if line:
+                self.up = [cp.group() for _ in range(zs - 1)]
+                self.down = [cp.group() for _ in range(zs - 1)]
             self.rows, cols = source.shape
             self.part, self.cols = self.rows // cuts, cols // 2
             self.slot = q if cuts == 4 else lax.rem(x + y, 2)
@@ -402,6 +410,39 @@
 
         def block(self, zz, qq):
             return self.ref.at[at(zz * self.rows + qq * self.part, self.part, 16), self.mine]
+
+        def hop(self, i):
+            one = self.view(self.part)
+
+            def forward(pair, source, dest, when):
+                @pl.when(when)
+                def _():
+                    cp.send(pair, source, self.block(dest[0], self.slot), c, dest[1])
+
+                cp.sent(pair, one, when)
+
+            if i == 0:
+                mine = self.source.at[at(self.slot * self.part, self.part, 16), self.mine]
+                forward(self.up[0], mine, (z, z + 1), z < zs - 1)
+                forward(self.down[0], mine, (z, z - 1), z > 0)
+                self.load = cp.local(self.source, self.ref.at[at(z * self.rows, self.rows, 16), :])
+                return
+
+            @pl.when(z >= i)
+            def _():
+                cp.got(self.up[i - 1], one)
+
+            if i < zs - 1:
+                block = self.block(lax.rem(z + zs - i, zs), self.slot)
+                forward(self.up[i], block, (lax.rem(z + zs - i, zs), z + 1), (z >= i) & (z < zs - 1))
+
+            @pl.when(z + i < zs)
+            def _():
+                cp.got(self.down[i - 1], one)
+
+            if i < zs - 1:
+                block = self.block(lax.rem(z + i, zs), self.slot)
+                forward(self.down[i], block, (lax.rem(z + i, zs), z - 1), (z + i < zs) & (z > 0))
 
         def start(self):
             for peer in zed:
@@ -416,7 +457,10 @@
             self.load = cp.local(self.source, self.ref.at[at(z * self.rows, self.rows, 16), :])
 
         def first(self):
-            cp.got(self.pairs[0], self.view(3 * self.part))
+            if self.line:
+                self.hop(zs - 1)
+            else:
+                cp.got(self.pairs[0], self.view(3 * self.part))
             for zz in zed:
                 block = self.block(zz, self.slot)
                 cp.send(self.pairs[1], block, block, near[0], z)
@@ -444,11 +488,12 @@
             cp.got(self.pairs[3], self.view(3 * self.rows))
             self.load.wait()
 
-    wk, wq, lat = Weight(s.wk, wk_in, 4), Weight(s.wq, wq_in, 4), Weight(s.lat, lat_in, 4)
-    wv, wo = Weight(s.wv, wv_in, 4), Weight(s.wo, wo_in, 4)
-    wu, wd = Weight(s.wu, wu_in, 2), Weight(s.wd, wd_in, 2)
-    for weight in (wk, wq, lat, wv, wo, wu, wd):
+    wk, wq, lat = Weight(s.wk, wk_in, 4, False), Weight(s.wq, wq_in, 4, False), Weight(s.lat, lat_in, 4, False)
+    wv, wo = Weight(s.wv, wv_in, 4, False), Weight(s.wo, wo_in, 4, True)
+    wu, wd = Weight(s.wu, wu_in, 4, True), Weight(s.wd, wd_in, 2, True)
+    for weight in (wk, wq, lat, wv):
         weight.start()
+    wo.hop(0)
     load_cot = cp.local(cot_in, s.cot)
 
     cp.got(small_pair, s.small.at[0 : zs - 1])
@@ -460,98 +505,19 @@
     vec = s.vec
     gain_lat, bias_lat = vec[0:1, :], vec[1:2, :]
 
-    load_feats.wait()
-
-    @pl.loop(0, p.rows_in // 64)
-    def _(i):
-        rows = at(i * 64, 64)
-        normed, _ = ln_parts(s.feats[rows, :].astype(FULL))
-        s.nin[rows, :] = (normed * vec[2:3, 0 : p.din] + vec[3:4, 0 : p.din]).astype(LOW)
-
-    wk.first()
-    wq.first()
-    lat.first()
-
-    @pl.loop(0, p.din // 128)
-    def _(i):
-        tile = at(i * 128, 128)
-        s.nin_t[tile, :] = s.nin[:, tile].T
-
-    wk.second()
-    wq.second()
-    lat.second()
-    wk.third()
-    wq.third()
-    lat.third()
-    wk.ready()
-
-    @pl.loop(0, p.seqs)
-    def _(i):
-        rows = at(i * p.slots, p.slots)
-        low = matmul(s.nin[rows, :], s.wk[...]).astype(LOW)
-        s.keys[rows, :] = low
-        s.keys_t[:, rows] = low.T
-
-    wv.first()
-    lat.ready()
-
-    @pl.loop(0, p.lat // 64)
-    def _(i):
-        rows = at(i * 64, 64)
-        normed, _ = ln_parts(s.lat[rows, :].astype(FULL))
-        s.nlat[rows, :] = (normed * gain_lat + bias_lat).astype(LOW)
-
-    wq.ready()
-    queries = matmul(s.nlat[...], s.wq[...])
-    lane_q = lanes(p.lat, p.qk)
-    for head in range(H):
-        inside = (lane_q >= head * p.head) & (lane_q < (head + 1) * p.head)
-        s.qmask[head * p.lat : (head + 1) * p.lat, :] = jnp.where(inside, queries, 0.0).astype(LOW)
-
-    wv.second()
+    half_cols = at(h * (p.dl // 2), p.dl // 2)
+    own = at(h * p.lat, p.lat)
+    tiles = p.dl // 256
+    quarter = p.lat // 4
+    own_rows = at(h * p.lat + q * quarter, quarter)
     score_scale = 1.0 / math.sqrt(p.head)
     start_slot = c * p.slots
-    s.stat[...] = jnp.zeros_like(s.stat)
     lane_stat = lanes(p.lat, 128)
-
-    @pl.loop(0, p.seqs * H)
-    def _(i):
-        seq, head = lax.div(i, H), lax.rem(i, H)
-        raw = matmul_nt(
-            s.qmask[at(head * p.lat, p.lat), :], s.keys[at(seq * p.slots, p.slots), :]
-        )
-        valid = start_slot + lanes(p.lat, p.slots) < lengths[seq]
-        scores = jnp.where(valid, raw * score_scale, -1e30)
-        s.scores[at(i * p.lat, p.lat), :] = scores
-        top = jnp.max(scores, axis=-1, keepdims=True)
-        s.stat[...] = jnp.where(lane_stat == i, top, s.stat[...])
-
-    s.stat_t[...] = s.stat[...].T
-    s.max_own[...] = s.stat_t[0 : 2 * H, :]
-    max_pair = cp.group()
-    for peer in plane:
-        cp.send(max_pair, s.max_own, s.max_in.at[c], peer, z)
-    cp.sent(max_pair, s.max_in.at[0 : ctx - 1])
-
-    wv.third()
-    wo.first()
-    wv.ready()
-
-    @pl.loop(0, p.vd // 256)
-    def _(i):
-        tile = at(i * 256, 256)
-        s.values[:, tile] = matmul(s.nin[...], s.wv[:, tile]).astype(LOW)
-
-    wo.second()
-    cp.got(max_pair, s.max_in.at[0 : ctx - 1])
-    s.max_in[c] = s.max_own[...]
-    top = s.max_in[0]
-    for i in range(1, ctx):
-        top = jnp.maximum(top, s.max_in[i])
-    s.max_all[...] = top
-    s.stat_t[0 : 2 * H, :] = top
-    max_columns = s.stat_t[...].T
-    s.stat[...] = jnp.zeros_like(s.stat)
+    gain_mlp, bias_mlp = vec[4:5, :], vec[5:6, :]
+    qhalf, vhalf = p.qk // 2, p.vd // 2
+    zrows = p.din // zs
+    vpart = zrows // 4
+    order = [*zed, z]
 
     def window(head):
         low_lane = pl.multiple_of(lax.div(head * p.vhead, 128) * 128, 128)
@@ -561,16 +527,94 @@
         lane = lanes(rows, 256)
         return ((lane >= low_lane) & (lane < low_lane + p.vhead)).astype(FULL)
 
+    def normed_bytes():
+        load_feats.wait()
+
+        @pl.loop(0, p.rows_in // 64)
+        def _(i):
+            rows = at(i * 64, 64)
+            normed, _ = ln_parts(s.feats[rows, :].astype(FULL))
+            s.nin[rows, :] = (normed * vec[2:3, 0 : p.din] + vec[3:4, 0 : p.din]).astype(LOW)
+
+    def turned_bytes():
+        @pl.loop(0, p.din // 128)
+        def _(i):
+            tile = at(i * 128, 128)
+            s.nin_t[tile, :] = s.nin[:, tile].T
+
+    def make_keys():
+        @pl.loop(0, p.seqs)
+        def _(i):
+            rows = at(i * p.slots, p.slots)
+            low = matmul(s.nin[rows, :], s.wk[...]).astype(LOW)
+            s.keys[rows, :] = low
+            s.keys_t[:, rows] = low.T
+
+    def normed_latents():
+        @pl.loop(0, p.lat // 64)
+        def _(i):
+            rows = at(i * 64, 64)
+            normed, _ = ln_parts(s.lat[rows, :].astype(FULL))
+            s.nlat[rows, :] = (normed * gain_lat + bias_lat).astype(LOW)
+
+    def make_queries():
+        queries = matmul(s.nlat[...], s.wq[...])
+        lane_q = lanes(p.lat, p.qk)
+        for head in range(H):
+            inside = (lane_q >= head * p.head) & (lane_q < (head + 1) * p.head)
+            s.qmask[head * p.lat : (head + 1) * p.lat, :] = jnp.where(inside, queries, 0.0).astype(LOW)
+
+    max_pair = cp.group()
+
+    def make_scores():
+        s.stat[...] = jnp.zeros_like(s.stat)
+        for seq in range(p.seqs):
+
+            @pl.loop(0, H)
+            def _(head):
+                raw = matmul_nt(
+                    s.qmask[at(head * p.lat, p.lat), :], s.keys[seq * p.slots : (seq + 1) * p.slots, :]
+                )
+                valid = lanes(p.lat, p.slots) < lengths[seq] - start_slot
+                scores = jnp.where(valid, raw * score_scale, -1e30)
+                s.scores[at((seq * H + head) * p.lat, p.lat), :] = scores
+                top = jnp.max(scores, axis=-1, keepdims=True)
+                s.stat[...] = jnp.where(lanes(p.lat, 128) == seq * H + head, top, s.stat[...])
+
+        s.stat_t[...] = s.stat[...].T
+        s.max_own[...] = s.stat_t[0 : 2 * H, :]
+        for peer in plane:
+            cp.send(max_pair, s.max_own, s.max_in.at[c], peer, z)
+        cp.sent(max_pair, s.max_in.at[0 : ctx - 1])
+
+    def make_values():
+        @pl.loop(0, p.vd // 256)
+        def _(i):
+            tile = at(i * 256, 256)
+            s.values[:, tile] = matmul(s.nin[...], s.wv[:, tile]).astype(LOW)
+
+    def get_max():
+        cp.got(max_pair, s.max_in.at[0 : ctx - 1])
+        s.max_in[c] = s.max_own[...]
+        top = s.max_in[0]
+        for i in range(1, ctx):
+            top = jnp.maximum(top, s.max_in[i])
+        s.max_all[...] = top
+        s.stat_t[0 : 2 * H, :] = top
+        s.max_t[...] = s.stat_t[...].T
+        s.stat[...] = jnp.zeros_like(s.stat)
+
     def partial(seq):
         s.numer[...] = jnp.zeros_like(s.numer)
 
         @pl.loop(0, H)
         def _(head):
             i = seq * H + head
-            top = jnp.sum(jnp.where(lane_stat == i, max_columns, 0.0), axis=-1, keepdims=True)
+            lane = lanes(p.lat, 128)
+            top = jnp.sum(jnp.where(lane == i, s.max_t[...], 0.0), axis=-1, keepdims=True)
             weights = jnp.exp(s.scores[at(i * p.lat, p.lat), :] - top)
             total = jnp.sum(weights, axis=-1, keepdims=True)
-            s.stat[...] = jnp.where(lane_stat == i, total, s.stat[...])
+            s.stat[...] = jnp.where(lane == i, total, s.stat[...])
             cols, low_lane = window(head)
             part = s.values[at(seq * p.slots, p.slots), cols] * mask_of(p.slots, low_lane).astype(LOW)
             s.numer[:, cols] += matmul(weights.astype(LOW), part)
@@ -578,98 +622,129 @@
         s.stat_t[...] = s.stat[...].T
         s.sums[seq] = s.stat_t[at(seq * H, H), :]
 
-    partial(other)
-    s.numer_low[...] = s.numer[...].astype(LOW)
-    pair_pair = cp.group()
-    sums_pair = cp.group()
-    cp.send(pair_pair, s.numer_low, s.numer_in, core, z)
-    cp.send(sums_pair, s.sums.at[other], s.sums_in, core, z)
-    cp.sent(pair_pair, s.numer_low)
-    cp.sent(sums_pair, s.sums_in)
-    partial(h)
-
-    cp.got(pair_pair, s.numer_in)
-    cp.got(sums_pair, s.sums_in)
-    quarter = p.lat // 4
-    s.chip[...] = (s.numer[...] + s.numer_in[...].astype(FULL)).astype(LOW)
-    s.chip_sums[...] = s.sums[h] + s.sums_in[...]
-    chip_pair = cp.group()
+    pair_pair, sums_pair = cp.group(), cp.group()
     chip_sums_pair = cp.group()
-    for peer in chips:
-        peer_chip = lax.div(peer, 2)
-        cp.send(chip_pair, s.chip.at[at(peer_chip * quarter, quarter), :], s.chip_in.at[q], peer, z)
-        cp.send(chip_sums_pair, s.chip_sums, s.chip_sums_in.at[q], peer, z)
-    cp.sent(chip_pair, s.chip_in.at[0:3])
-    cp.sent(chip_sums_pair, s.chip_sums_in.at[0:3])
-    wu.first()
-    wo.third()
-
-    cp.got(chip_sums_pair, s.chip_sums_in.at[0:3])
-    s.chip_sums_in[q] = s.chip_sums[...]
-    sums = s.chip_sums_in
-    inverse = 1.0 / ((sums[0] + sums[1]) + (sums[2] + sums[3]))
-    s.stats[h, 0:H, :] = inverse
-    s.stat_t[0:H, :] = inverse
-    s.stat[...] = s.stat_t[...].T
-    s.scale[...] = jnp.zeros_like(s.scale)
-    own_quarter = s.stat[at(q * quarter, quarter), :]
-    for head in range(H):
-        low_lane = head * p.vhead // 128 * 128
-        lane = lanes(quarter, 256) + low_lane
-        inside = (lane >= head * p.vhead) & (lane < (head + 1) * p.vhead)
-        cols = slice(low_lane, low_lane + 256)
-        s.scale[:, cols] = jnp.where(inside, own_quarter[:, head : head + 1], s.scale[:, cols])
-    cp.got(chip_pair, s.chip_in.at[0:3])
-    s.chip_in[q] = s.chip[at(q * quarter, quarter), :]
-    numer = s.chip_in
-    added = (numer[0].astype(FULL) + numer[1].astype(FULL)) + (numer[2].astype(FULL) + numer[3].astype(FULL))
-    own_rows = at(h * p.lat + q * quarter, quarter)
-    s.att[own_rows, :] = (added * s.scale[...]).astype(LOW)
-    att_pair = cp.group()
-    for peer in chips:
-        cp.send(att_pair, s.att.at[own_rows, :], s.att.at[own_rows, :], peer, z)
-    cp.sent(att_pair, s.att.at[0 : 3 * quarter, :])
-    wo.ready()
-    own = at(h * p.lat, p.lat)
-    cp.got(att_pair, s.att.at[0 : 3 * quarter, :])
+    chip_pairs, att_pairs = [cp.group() for _ in range(2)], [cp.group() for _ in range(2)]
+    near_chip = [lax.div(near[0], 2), lax.div(near[1], 2)]
+
+    def partial_other():
+        partial(other)
+        s.numer_low[...] = s.numer[...].astype(LOW)
+        cp.send(sums_pair, s.sums.at[other], s.sums_in, core, z)
+        cp.send(pair_pair, s.numer_low, s.numer_in, core, z)
+        cp.sent(pair_pair, s.numer_low)
+        cp.sent(sums_pair, s.sums_in)
+
+    def partial_own():
+        partial(h)
+
+    def chip_numer():
+        cp.got(sums_pair, s.sums_in)
+        s.chip_sums[...] = s.sums[h] + s.sums_in[...]
+        for peer in chips:
+            cp.send(chip_sums_pair, s.chip_sums, s.chip_sums_in.at[q], peer, z)
+        cp.sent(chip_sums_pair, s.chip_sums_in.at[0:3])
+        cp.got(pair_pair, s.numer_in)
+        s.chip[...] = (s.numer[...] + s.numer_in[...].astype(FULL)).astype(LOW)
+        for slot, qq in enumerate((3 - q, near_chip[0])):
+            rows = at(qq * quarter, quarter)
+            cp.send(chip_pairs[0], s.chip.at[rows, :], s.chip_in.at[slot], near[0], z)
+        cp.sent(chip_pairs[0], s.chip_in.at[0:2])
+
+    def chip_pass():
+        cp.got(chip_pairs[0], s.chip_in.at[0:2])
+        rows = at(near_chip[1] * quarter, quarter)
+        s.chip_in[3] = (s.chip[rows, :].astype(FULL) + s.chip_in[0].astype(FULL)).astype(LOW)
+        cp.send(chip_pairs[1], s.chip_in.at[3], s.chip_in.at[2], near[1], z)
+        cp.sent(chip_pairs[1], s.chip_in.at[3])
+
+    def turned_weights():
+        for seq in range(p.seqs):
+
+            @pl.loop(0, H)
+            def _(head):
+                i = seq * H + head
+                raw = matmul_nt(
+                    s.keys[seq * p.slots : (seq + 1) * p.slots, :], s.qmask[at(head * p.lat, p.lat), :]
+                )
+                slot = lax.broadcasted_iota(jnp.int32, (p.slots, p.lat), 0)
+                masked = jnp.where(slot < lengths[seq] - start_slot, raw * score_scale, -1e30)
+                s.scores[at(i * p.slots, p.slots), :] = jnp.exp(masked - s.max_all[pl.ds(i, 1), :])
+
+    def make_scale():
+        cp.got(chip_sums_pair, s.chip_sums_in.at[0:3])
+        s.chip_sums_in[q] = s.chip_sums[...]
+        sums = s.chip_sums_in
+        inverse = 1.0 / ((sums[0] + sums[1]) + (sums[2] + sums[3]))
+        s.stats[h, 0:H, :] = inverse
+        s.stat_t[0:H, :] = inverse
+        s.stat[...] = s.stat_t[...].T
+        s.scale[...] = jnp.zeros_like(s.scale)
+        own_quarter = s.stat[at(q * quarter, quarter), :]
+        for head in range(H):
+            low_lane = head * p.vhead // 128 * 128
+            lane = lanes(quarter, 256) + low_lane
+            inside = (lane >= head * p.vhead) & (lane < (head + 1) * p.vhead)
+            cols = slice(low_lane, low_lane + 256)
+            s.scale[:, cols] = jnp.where(inside, own_quarter[:, head : head + 1], s.scale[:, cols])
+
+    def make_att():
+        cp.got(chip_pairs[1], s.chip_in.at[2])
+        own_numer = s.chip[at(q * quarter, quarter), :].astype(FULL)
+        added = own_numer + (s.chip_in[1].astype(FULL) + s.chip_in[2].astype(FULL))
+        s.att[own_rows, :] = (added * s.scale[...]).astype(LOW)
+        cp.send(att_pairs[0], s.att.at[own_rows, :], s.att.at[own_rows, :], near[0], z)
+        cp.sent(att_pairs[0], s.att.at[0:quarter, :])
+
+    def att_pass():
+        cp.got(att_pairs[0], s.att.at[0:quarter, :])
+        for qq in (q, near_chip[0]):
+            rows = at(h * p.lat + qq * quarter, quarter)
+            cp.send(att_pairs[1], s.att.at[rows, :], s.att.at[rows, :], near[1], z)
+        cp.sent(att_pairs[1], s.att.at[0 : 2 * quarter, :])
+
+    shares = {}
 
     def share(ref):
         pair = cp.group()
         cp.send(pair, ref.at[own, :], ref.at[own, :], core, z)
         cp.sent(pair, ref.at[0 : p.lat, :])
-        return pair
-
-    att_share = share(s.att)
-    wd.first()
-    tiles = p.dl // 256
-
-    @pl.loop(0, tiles)
-    def _(i):
-        tile = at(i * 256, 256)
-        s.hid[:, tile] = s.lat[:, tile].astype(FULL) + matmul(s.att[own, :], s.wo[:, tile])
-
-    wu.third()
-    gain_mlp, bias_mlp = vec[4:5, :], vec[5:6, :]
-
-    @pl.loop(0, p.lat // 64)
-    def _(i):
-        normed, _ = ln_parts(s.hid[at(i * 64, 64), :])
-        s.mid[at(h * p.lat + i * 64, 64), :] = (normed * gain_mlp + bias_mlp).astype(LOW)
-
-    mid_share = share(s.mid)
-    wu.ready()
-    load_cot.wait()
-
-    @pl.loop(0, tiles)
-    def _(i):
-        tile = at(i * 256, 256)
-        up = matmul(s.mid[own, :], s.wu[:, tile])
-        cdf = 0.5 * (1.0 + lax.erf(up * (1.0 / math.sqrt(2.0))))
-        density = jnp.exp(-0.5 * up * up) * (1.0 / math.sqrt(2.0 * math.pi))
-        s.act[own, tile] = (up * cdf).astype(LOW)
-        s.slope[:, tile] = cdf + up * density
-
-    half_cols = at(h * (p.dl // 2), p.dl // 2)
+        shares[id(ref)] = pair
+
+    def shared(ref):
+        cp.got(shares.pop(id(ref)), ref.at[0 : p.lat, :])
+
+    def get_att():
+        cp.got(att_pairs[1], s.att.at[0 : 2 * quarter, :])
+        share(s.att)
+
+    def make_hidden():
+        @pl.loop(0, tiles)
+        def _(i):
+            tile = at(i * 256, 256)
+            s.hid[:, tile] = s.lat[:, tile].astype(FULL) + matmul(s.att[own, :], s.wo[:, tile])
+
+    def make_mid():
+        @pl.loop(0, p.lat // 64)
+        def _(i):
+            normed, _ = ln_parts(s.hid[at(i * 64, 64), :])
+            s.mid[at(h * p.lat + i * 64, 64), :] = (normed * gain_mlp + bias_mlp).astype(LOW)
+
+        share(s.mid)
+
+    def make_act():
+        load_cot.wait()
+
+        @pl.loop(0, tiles)
+        def _(i):
+            tile = at(i * 256, 256)
+            up = matmul(s.mid[own, :], s.wu[:, tile])
+            cdf = 0.5 * (1.0 + lax.erf(up * (1.0 / math.sqrt(2.0))))
+            density = jnp.exp(-0.5 * up * up) * (1.0 / math.sqrt(2.0 * math.pi))
+            s.act[own, tile] = (up * cdf).astype(LOW)
+            s.slope[:, tile] = cdf + up * density
+
+        share(s.act)
 
     class Reduce:
         def __init__(self, left, right, grads, arrive, final, out):
@@ -677,7 +752,7 @@
             self.grads, self.arrive, self.final = grads, arrive, final
             self.part = self.final.shape[0]
             self.rows = self.part * 4
-            self.pairs = [cp.group() for _ in range(3)]
+            self.pairs = [cp.group() for _ in range(4)]
 
         def product(self):
             @pl.loop(0, self.grads.shape[0] // 256)
@@ -701,170 +776,207 @@
                 total = total + self.arrive[zz].astype(FULL)
             self.final[...] = total.astype(LOW)
             here = self.out.at[at(q * self.part, self.part, 16), half_cols]
-            for peer in chips:
-                cp.send(self.pairs[1], self.final, here, peer, z)
-            cp.sent(self.pairs[1], self.arrive.at[0:3])
+            cp.send(self.pairs[1], self.final, here, near[0], z)
+            cp.sent(self.pairs[1], self.final)
             self.store = cp.local(self.final, here)
 
         def spread(self):
-            cp.got(self.pairs[1], self.arrive.at[0:3])
+            cp.got(self.pairs[1], self.final)
+            here = self.out.at[at(q * self.part, self.part, 16), half_cols]
+            there = self.out.at[at(near_chip[0] * self.part, self.part, 16), half_cols]
+            cp.send(self.pairs[2], self.final, here, near[1], z)
+            cp.send(self.pairs[2], there, there, near[1], z)
+            cp.sent(self.pairs[2], self.arrive.at[0:2])
+
+        def halve(self):
+            cp.got(self.pairs[2], self.arrive.at[0:2])
             self.store.wait()
             block = self.out.at[:, half_cols]
-            cp.send(self.pairs[2], block, block, core, z)
-            cp.sent(self.pairs[2], block)
+            cp.send(self.pairs[3], block, block, core, z)
+            cp.sent(self.pairs[3], block)
 
         def done(self):
-            cp.got(self.pairs[2], self.out.at[:, half_cols])
+            cp.got(self.pairs[3], self.out.at[:, half_cols])
 
     down = Reduce(s.act, s.cot, s.dwd, s.zd, s.fd, gd)
     upper = Reduce(s.mid, s.dup, s.dwu, s.zu, s.fu, gu)
     outer = Reduce(s.att, s.dhid, s.dwo, s.zo, s.fo, go)
     latents = Reduce(s.att, s.dhid, s.dlat, s.zl, s.fl, gl)
-
-    act_share = share(s.act)
-    wd.third()
-    cp.got(act_share, s.act.at[0 : p.lat, :])
-    down.product()
-    down.scatter()
-    wd.ready()
-
-    @pl.loop(0, tiles)
-    def _(i):
-        tile = at(i * 256, 256)
-        dact = matmul_nt(s.cot[own, :], s.wd[tile, :])
-        s.dup[own, tile] = (dact * s.slope[:, tile]).astype(LOW)
-
-    dup_share = share(s.dup)
-
-    @pl.loop(0, tiles)
-    def _(i):
-        tile = at(i * 256, 256)
-        s.dmid[:, tile] = matmul_nt(s.dup[own, :], s.wu[tile, :])
-
-    s.vs[...] = jnp.zeros_like(s.vs)
-
-    @pl.loop(0, p.lat // 64)
-    def _(i):
-        rows = at(i * 64, 64)
-        full_rows = at(h * p.lat + i * 64, 64)
-        normed, scale = ln_parts(s.hid[rows, :])
-        grad = s.dmid[rows, :]
-        s.vs[0:1, :] += columns_sum(grad * normed)
-        s.vs[1:2, :] += columns_sum(grad)
-        total = s.cot[full_rows, :].astype(FULL) + ln_grad(grad, gain_mlp, normed, scale)
-        s.dhid[full_rows, :] = total.astype(LOW)
-
-    dhid_share = share(s.dhid)
-
-    @pl.loop(0, tiles)
-    def _(i):
-        tile = at(i * 256, 256)
-        s.datt[own, tile] = matmul_nt(s.dhid[own, :], s.wo[tile, :]).astype(LOW)
-
-    datt_share = share(s.datt)
-    s.stat[...] = jnp.zeros_like(s.stat)
-
-    @pl.loop(0, H)
-    def _(head):
-        cols, low_lane = window(head)
-        product = s.datt[own, cols].astype(FULL) * s.att[own, cols].astype(FULL)
-        delta = jnp.sum(product * mask_of(p.lat, low_lane), axis=-1, keepdims=True)
-        s.stat[...] = jnp.where(lane_stat == head, delta, s.stat[...])
-
-    s.stat_t[...] = s.stat[...].T
-    s.stats[h, H : 2 * H, :] = s.stat_t[0:H, :]
-    stats_pair = cp.group()
-    cp.send(stats_pair, s.stats.at[h], s.stats.at[h], core, z)
-    cp.sent(stats_pair, s.stats.at[0])
-
-    cp.got(mid_share, s.mid.at[0 : p.lat, :])
-    cp.got(dup_share, s.dup.at[0 : p.lat, :])
-    upper.product()
-    upper.scatter()
-    down.add()
-    cp.got(datt_share, s.datt.at[0 : p.lat, :])
-    cp.got(stats_pair, s.stats.at[0])
-
-    s.dq_t[...] = jnp.zeros_like(s.dq_t)
-    sublane = lax.broadcasted_iota(jnp.int32, (p.slots, p.lat), 0)
-
-    @pl.loop(0, p.seqs)
-    def _(seq):
+    reduces = (down, upper, outer, latents)
+
+    def down_grads():
+        shared(s.act)
+        down.product()
+        down.scatter()
+
+    def upper_grads():
+        shared(s.mid)
+        shared(s.dup)
+        upper.product()
+        upper.scatter()
+
+    def outer_grads():
+        shared(s.att)
+        shared(s.dhid)
+        outer.product()
+        outer.scatter()
+        s.dlat[...] = (
+            s.dhid[0 : p.lat, half_cols].astype(FULL) + s.dhid[p.lat : 2 * p.lat, half_cols].astype(FULL)
+        ).astype(LOW)
+        latents.scatter()
+
+    def make_dup():
+        @pl.loop(0, tiles)
+        def _(i):
+            tile = at(i * 256, 256)
+            dact = matmul_nt(s.cot[own, :], s.wd[tile, :])
+            s.dup[own, tile] = (dact * s.slope[:, tile]).astype(LOW)
+
+        share(s.dup)
+
+    def make_dmid():
+        @pl.loop(0, tiles)
+        def _(i):
+            tile = at(i * 256, 256)
+            s.dmid[:, tile] = matmul_nt(s.dup[own, :], s.wu[tile, :])
+
+    def make_dhid():
+        s.vs[...] = jnp.zeros_like(s.vs)
+
+        @pl.loop(0, p.lat // 64)
+        def _(i):
+            rows = at(i * 64, 64)
+            full_rows = at(h * p.lat + i * 64, 64)
+            normed, scale = ln_parts(s.hid[rows, :])
+            grad = s.dmid[rows, :]
+            s.vs[0:1, :] += columns_sum(grad * normed)
+            s.vs[1:2, :] += columns_sum(grad)
+            total = s.cot[full_rows, :].astype(FULL) + ln_grad(grad, gain_mlp, normed, scale)
+            s.dhid[full_rows, :] = total.astype(LOW)
+
+        share(s.dhid)
+
+    stats_pairs = [cp.group() for _ in range(2)]
+
+    def share_inverse():
+        cp.send(stats_pairs[0], s.stats.at[h, 0:H], s.stats.at[h, 0:H], core, z)
+        cp.sent(stats_pairs[0], s.stats.at[0, 0:H])
+
+    def make_datt():
+        @pl.loop(0, tiles)
+        def _(i):
+            tile = at(i * 256, 256)
+            s.datt[own, tile] = matmul_nt(s.dhid[own, :], s.wo[tile, :]).astype(LOW)
+
+        share(s.datt)
+
+    def make_delta():
+        s.stat[...] = jnp.zeros_like(s.stat)
+
+        @pl.loop(0, H)
+        def _(head):
+            cols, low_lane = window(head)
+            product = s.datt[own, cols].astype(FULL) * s.att[own, cols].astype(FULL)
+            delta = jnp.sum(product * mask_of(p.lat, low_lane), axis=-1, keepdims=True)
+            s.stat[...] = jnp.where(lanes(p.lat, 128) == head, delta, s.stat[...])
+
+        s.stat_t[...] = s.stat[...].T
+        s.stats[h, H : 2 * H, :] = s.stat_t[0:H, :]
+        cp.send(stats_pairs[1], s.stats.at[h, H : 2 * H], s.stats.at[h, H : 2 * H], core, z)
+        cp.sent(stats_pairs[1], s.stats.at[0, 0:H])
+
+    def values_grad(seq):
+        latent_rows = at(seq * p.lat, p.lat)
+        s.numer[...] = jnp.zeros_like(s.numer)
+
+        @pl.loop(0, H)
+        def _(head):
+            cols, low_lane = window(head)
+            inverse = s.stats[seq, pl.ds(head, 1), :]
+            probs = s.scores[at((seq * H + head) * p.slots, p.slots), :] * inverse
+            grad = s.datt[latent_rows, cols] * mask_of(p.lat, low_lane).astype(LOW)
+            s.numer[:, cols] += matmul(probs.astype(LOW), grad)
+
+        s.dvalues[at(seq * p.slots, p.slots), :] = s.numer[...].astype(LOW)
+
+    def scores_grad(seq):
         slots = at(seq * p.slots, p.slots)
         latent_rows = at(seq * p.lat, p.lat)
-        s.numer[...] = jnp.zeros_like(s.numer)
         s.dk_sum[...] = jnp.zeros_like(s.dk_sum)
 
         @pl.loop(0, H)
         def _(head):
             heads = at(head * p.lat, p.lat)
             cols, low_lane = window(head)
-            raw = matmul_nt(s.keys[slots, :], s.qmask[heads, :])
-            valid = start_slot + sublane < lengths[seq]
-            top = s.max_all[pl.ds(seq * H + head, 1), :]
             inverse = s.stats[seq, pl.ds(head, 1), :]
             delta = s.stats[seq, pl.ds(H + head, 1), :]
-            probs = jnp.exp(jnp.where(valid, raw * score_scale, -1e30) - top) * inverse
+            probs = s.scores[at((seq * H + head) * p.slots, p.slots), :] * inverse
             grad = s.datt[latent_rows, cols] * mask_of(p.lat, low_lane).astype(LOW)
             dprobs = matmul_nt(s.values[slots, cols], grad)
             dscores = (probs * (dprobs - delta)).astype(LOW)
-            s.numer[:, cols] += matmul(probs.astype(LOW), grad)
             s.dk_sum[...] += matmul(dscores, s.qmask[heads, :])
             block = at(head * p.head, p.head)
             s.dq_t[block, :] += matmul(s.keys_t[block, slots], dscores)
 
         s.dkeys[slots, :] = (s.dk_sum[...] * score_scale).astype(LOW)
-        s.dvalues[slots, :] = s.numer[...].astype(LOW)
-
-    s.dq[...] = (s.dq_t[...] * score_scale).T.astype(LOW)
-    qhalf = p.qk // 2
-    dq_pairs = [cp.group() for _ in range(4)]
-    cp.send(dq_pairs[0], s.dq.at[:, at(other * qhalf, qhalf)], s.dq_in1, core, z)
-    cp.sent(dq_pairs[0], s.dq_in1)
-
-    def weight_grads(side):
-        kcols = at(side * qhalf, qhalf)
-        vcols = at(side * (p.vd // 2), p.vd // 2)
+
+    def weight_grads(ref, grad, width, side):
+        cols = at(side * width, width)
 
         @pl.loop(0, p.din // 256)
         def _(i):
             rows = at(i * 256, 256)
-            s.swk[side, rows, :] = matmul(s.nin_t[rows, :], s.dkeys[:, kcols]).astype(LOW)
-            s.swv[side, rows, :] = matmul(s.nin_t[rows, :], s.dvalues[:, vcols]).astype(LOW)
-
-    weight_grads(other)
-    zrows = p.din // zs
-    vpart = zrows // 4
+            ref[side, rows, :] = matmul(s.nin_t[rows, :], grad[:, cols]).astype(LOW)
 
     class Local:
         def __init__(self, grads, arrive, chip, plane_in, plane, z_in, final, out):
             self.grads, self.arrive, self.chip, self.plane_in = grads, arrive, chip, plane_in
             self.plane, self.z_in, self.final, self.out = plane, z_in, final, out
             self.width = final.shape[1]
-            self.pairs = [cp.group() for _ in range(4)]
-            self.chunks = [cp.group() for _ in range(zs)]
+            self.pairs = [cp.group() for _ in range(5)]
+            self.firsts = [cp.group() for _ in range(zs // 2)]
+            self.seconds = [cp.group() for _ in range(zs // 2)]
+            self.mine = at(h * self.width, self.width)
 
         def pair(self):
             cp.send(self.pairs[0], self.grads.at[other], self.arrive, core, z)
             cp.sent(self.pairs[0], self.arrive)
 
-        def chunk(self, i, zz):
-            rows = at(zz * zrows, zrows)
-            total = self.grads[h, rows, :].astype(FULL) + self.arrive[rows, :].astype(FULL)
-            self.chip[zz] = total.astype(LOW)
-            for peer in chips:
-                rows = at(lax.div(peer, 2) * vpart, vpart)
-                cp.send(self.chunks[i], self.chip.at[zz, rows, :], self.plane_in.at[q, zz], peer, z)
-            cp.sent(self.chunks[i], self.plane_in.at[0, 0:3])
-
-        def add(self, i, zz):
-            cp.got(self.chunks[i], self.plane_in.at[0, 0:3])
-            self.plane_in[q, zz] = self.chip[zz, at(q * vpart, vpart, 16), :]
-            parts = [self.plane_in[qq, zz].astype(FULL) for qq in range(4)]
-            self.plane[zz] = ((parts[0] + parts[1]) + (parts[2] + parts[3])).astype(LOW)
-            if i < zs - 1:
-                cp.send(self.pairs[1], self.plane.at[zz], self.z_in.at[z], c, zz)
-            else:
+        def rows(self, qq):
+            return at(qq * vpart, vpart, 16)
+
+        def chunk(self, i):
+            for zz in order[2 * i : 2 * i + 2]:
+                rows = at(zz * zrows, zrows)
+                total = self.grads[h, rows, :].astype(FULL) + self.arrive[rows, :].astype(FULL)
+                self.chip[zz] = total.astype(LOW)
+                for slot, qq in enumerate((3 - q, near_chip[0])):
+                    cp.send(
+                        self.firsts[i],
+                        self.chip.at[zz, self.rows(qq), :],
+                        self.plane_in.at[slot, zz],
+                        near[0],
+                        z,
+                    )
+            cp.sent(self.firsts[i], self.plane_in.at[0])
+
+        def middle(self, i):
+            cp.got(self.firsts[i], self.plane_in.at[0])
+            for zz in order[2 * i : 2 * i + 2]:
+                mine = self.chip[zz, self.rows(near_chip[1]), :].astype(FULL)
+                self.plane_in[3, zz] = (mine + self.plane_in[0, zz].astype(FULL)).astype(LOW)
+                cp.send(self.seconds[i], self.plane_in.at[3, zz], self.plane_in.at[2, zz], near[1], z)
+            cp.sent(self.seconds[i], self.plane_in.at[0, 0:2])
+
+        def add(self, i):
+            cp.got(self.seconds[i], self.plane_in.at[0, 0:2])
+            for zz in order[2 * i : 2 * i + 2]:
+                mine = self.chip[zz, self.rows(q), :].astype(FULL)
+                parts = self.plane_in[1, zz].astype(FULL) + self.plane_in[2, zz].astype(FULL)
+                self.plane[zz] = (mine + parts).astype(LOW)
+                if zz is not order[-1]:
+                    cp.send(self.pairs[1], self.plane.at[zz], self.z_in.at[z], c, zz)
+            if i == zs // 2 - 1:
                 cp.sent(self.pairs[1], self.z_in.at[0 : zs - 1])
 
         def finish(self):
@@ -874,52 +986,31 @@
             for zz in range(1, zs):
                 total = total + self.z_in[zz].astype(FULL)
             self.final[...] = total.astype(LOW)
-            here = self.out.at[at(q * vpart, vpart, 16), at(h * self.width, self.width)]
-            for peer in chips:
-                cp.send(self.pairs[2], self.final, here, peer, z)
-            cp.sent(self.pairs[2], self.z_in.at[0:3])
+            here = self.out.at[self.rows(q), self.mine]
+            cp.send(self.pairs[2], self.final, here, near[0], z)
+            cp.sent(self.pairs[2], self.final)
             self.store = cp.local(self.final, here)
 
         def spread(self):
-            cp.got(self.pairs[2], self.z_in.at[0:3])
+            cp.got(self.pairs[2], self.final)
+            here = self.out.at[self.rows(q), self.mine]
+            there = self.out.at[self.rows(near_chip[0]), self.mine]
+            cp.send(self.pairs[3], self.final, here, near[1], z)
+            cp.send(self.pairs[3], there, there, near[1], z)
+            cp.sent(self.pairs[3], self.z_in.at[0:2])
+
+        def halve(self):
+            cp.got(self.pairs[3], self.z_in.at[0:2])
             self.store.wait()
-            block = self.out.at[:, at(h * self.width, self.width)]
-            cp.send(self.pairs[3], block, block, core, z)
-            cp.sent(self.pairs[3], block)
+            block = self.out.at[:, self.mine]
+            cp.send(self.pairs[4], block, block, core, z)
+            cp.sent(self.pairs[4], block)
 
         def done(self):
-            cp.got(self.pairs[3], self.out.at[:, at(h * self.width, self.width)])
+            cp.got(self.pairs[4], self.out.at[:, self.mine])
 
     key_grads = Local(s.swk, s.rwk, s.cwk, s.pwk_in, s.pwk, s.zwk_in, s.fwk, gk)
     value_grads = Local(s.swv, s.rwv, s.cwv, s.pwv_in, s.pwv, s.zwv_in, s.fwv, gv)
-    kv = (value_grads, key_grads)
-    for grads in kv:
-        grads.pair()
-    weight_grads(h)
-    cp.got(dq_pairs[0], s.dq_in1)
-    s.dq_chip[...] = (
-        s.dq[:, at(h * qhalf, qhalf)].astype(FULL) + s.dq_in1[...].astype(FULL)
-    ).astype(LOW)
-    for peer in chips:
-        cp.send(dq_pairs[1], s.dq_chip, s.dq_in2.at[q], peer, z)
-    cp.sent(dq_pairs[1], s.dq_in2.at[0:3])
-    for grads in kv:
-        cp.got(grads.pairs[0], grads.arrive)
-    order = [*zed, z]
-    for i, zz in enumerate(order):
-        for grads in kv:
-            grads.chunk(i, zz)
-
-    cp.got(att_share, s.att.at[0 : p.lat, :])
-    cp.got(dhid_share, s.dhid.at[0 : p.lat, :])
-    outer.product()
-    outer.scatter()
-    s.dlat[...] = (
-        s.dhid[0 : p.lat, half_cols].astype(FULL) + s.dhid[p.lat : 2 * p.lat, half_cols].astype(FULL)
-    ).astype(LOW)
-    latents.scatter()
-    down.spread()
-
     def byte_part(part):
         @pl.loop(part * 2, part * 2 + 2)
         def _(i):
@@ -930,100 +1021,264 @@
             s.vs[3:4, 0 : p.din] += columns_sum(grad)
             s.bgrad[rows, :] = ln_grad(grad, vec[2:3, 0 : p.din], normed, scale).astype(LOW)
 
-    for i, zz in enumerate(order):
-        for grads in kv:
-            grads.add(i, zz)
-        byte_part(i)
-
-    stores = [cp.local(s.bgrad, byte_out)]
+    kv = (value_grads, key_grads)
+    dq_pairs = [cp.group() for _ in range(5)]
     vs_pairs = [cp.group() for _ in range(3)]
-    cp.send(vs_pairs[0], s.vs, s.vs_in1, core, z)
-    cp.sent(vs_pairs[0], s.vs)
-    cp.got(dq_pairs[1], s.dq_in2.at[0:3])
-    s.dq_in2[q] = s.dq_chip[...]
-    parts = s.dq_in2
-    s.dq_plane[...] = (
-        (parts[0].astype(FULL) + parts[1].astype(FULL)) + (parts[2].astype(FULL) + parts[3].astype(FULL))
-    ).astype(LOW)
-    for peer in zed:
-        cp.send(dq_pairs[2], s.dq_plane, s.dq_in3.at[z], c, peer)
-    cp.sent(dq_pairs[2], s.dq_in3.at[0 : zs - 1])
-    cp.got(vs_pairs[0], s.vs_in1)
-    s.vs_chip[...] = s.vs[...] + s.vs_in1[...]
-    for peer in chips:
-        cp.send(vs_pairs[1], s.vs_chip, s.vs_in2.at[q], peer, z)
-    cp.sent(vs_pairs[1], s.vs_in2.at[0:3])
+    res_pair = cp.group()
+    stores = []
+    own_half = at(h * qhalf, qhalf)
+
+    def values_own():
+        values_grad(h)
+
+    def values_other():
+        cp.got(stats_pairs[0], s.stats.at[0, 0:H])
+        shared(s.datt)
+        values_grad(other)
+
+    def value_weights():
+        weight_grads(s.swv, s.dvalues, vhalf, other)
+        value_grads.pair()
+
+    def value_weights_own():
+        weight_grads(s.swv, s.dvalues, vhalf, h)
+
+    def value_chunks():
+        cp.got(value_grads.pairs[0], value_grads.arrive)
+        for i in range(zs // 2):
+            value_grads.chunk(i)
+
+    def scores_own():
+        s.dq_t[...] = jnp.zeros_like(s.dq_t)
+        scores_grad(h)
+
+    def scores_other():
+        cp.got(stats_pairs[1], s.stats.at[0, 0:H])
+        scores_grad(other)
+        s.dq[...] = (s.dq_t[...] * score_scale).T.astype(LOW)
+        cp.send(dq_pairs[0], s.dq.at[:, at(other * qhalf, qhalf)], s.dq_in1, core, z)
+        cp.sent(dq_pairs[0], s.dq_in1)
+
+    def key_weights():
+        weight_grads(s.swk, s.dkeys, qhalf, other)
+        key_grads.pair()
+        weight_grads(s.swk, s.dkeys, qhalf, h)
+
+    def dq_chip():
+        cp.got(dq_pairs[0], s.dq_in1)
+        s.dq_chip[...] = (s.dq[:, own_half].astype(FULL) + s.dq_in1[...].astype(FULL)).astype(LOW)
+        cp.send(dq_pairs[1], s.dq_chip, s.dq_in2.at[0], near[0], z)
+        cp.sent(dq_pairs[1], s.dq_chip)
+
+    def dq_pass():
+        cp.got(dq_pairs[1], s.dq_chip)
+        s.dq_in2[2] = (s.dq_chip[...].astype(FULL) + s.dq_in2[0].astype(FULL)).astype(LOW)
+        cp.send(dq_pairs[4], s.dq_in2.at[2], s.dq_in2.at[1], near[1], z)
+        cp.sent(dq_pairs[4], s.dq_chip)
+
+    def key_chunks():
+        cp.got(key_grads.pairs[0], key_grads.arrive)
+        for i in range(zs // 2):
+            key_grads.chunk(i)
+
+    def byte_store():
+        stores.append(cp.local(s.bgrad, byte_out))
+        cp.send(vs_pairs[0], s.vs, s.vs_in1, core, z)
+        cp.sent(vs_pairs[0], s.vs)
+
+    def dq_plane():
+        cp.got(dq_pairs[4], s.dq_chip)
+        s.dq_plane[...] = (s.dq_in2[1].astype(FULL) + s.dq_in2[2].astype(FULL)).astype(LOW)
+        for peer in zed:
+            cp.send(dq_pairs[2], s.dq_plane, s.dq_in3.at[z], c, peer)
+        cp.sent(dq_pairs[2], s.dq_in3.at[0 : zs - 1])
+
+    def vs_chip():
+        cp.got(vs_pairs[0], s.vs_in1)
+        s.vs_chip[...] = s.vs[...] + s.vs_in1[...]
+        for peer in chips:
+            cp.send(vs_pairs[1], s.vs_chip, s.vs_in2.at[q], peer, z)
+        cp.sent(vs_pairs[1], s.vs_in2.at[0:3])
+
+    def make_result():
+        @pl.loop(0, tiles)
+        def _(i):
+            tile = at(i * 256, 256)
+            s.res[:, tile] = (s.hid[:, tile] + matmul(s.act[own, :], s.wd[:, tile])).astype(LOW)
+
+        cp.send(res_pair, s.res, res_out.at[own, :], core, z)
+        cp.sent(res_pair, s.res)
+        stores.append(cp.local(s.res, res_out.at[own, :]))
+
+    def vs_plane():
+        cp.got(vs_pairs[1], s.vs_in2.at[0:3])
+        s.vs_in2[q] = s.vs_chip[...]
+        parts = s.vs_in2
+        total = (parts[0] + parts[1]) + (parts[2] + parts[3])
+        row_ids = lax.broadcasted_iota(jnp.int32, (8, p.dl), 0)
+        s.vs_plane[...] = jnp.where(row_ids < 2, s.vs_chip[...], total)
+        for peer in zed:
+            cp.send(vs_pairs[2], s.vs_plane, s.vs_in3.at[z], c, peer)
+        cp.sent(vs_pairs[2], s.vs_in3.at[0 : zs - 1])
+
+    def dq_total():
+        cp.got(dq_pairs[2], s.dq_in3.at[0 : zs - 1])
+        s.dq_in3[z] = s.dq_plane[...]
+        parts = s.dq_in3
+        total = parts[0].astype(FULL)
+        for zz in range(1, zs):
+            total = total + parts[zz].astype(FULL)
+        s.dq_all[:, own_half] = total.astype(LOW)
+        cp.send(dq_pairs[3], s.dq_all.at[:, own_half], s.dq_all.at[:, own_half], core, z)
+        cp.sent(dq_pairs[3], s.dq_in1)
+
+    def query_grads():
+        cp.got(dq_pairs[3], s.dq_in1)
+
+        @pl.loop(0, tiles)
+        def _(i):
+            tile = at(i * 256, 256)
+            s.gq[tile, :] = matmul_tn(s.nlat[:, tile], s.dq_all[...])
+            s.dmid[:, tile] = matmul_nt(s.dq_all[...], s.wq[tile, :])
+
+        stores.append(cp.local(s.gq.at[at(z * (p.dl // zs), p.dl // zs, 16), :], gq_out))
+
+    def latent_grads():
+        cp.got(vs_pairs[2], s.vs_in3.at[0 : zs - 1])
+        s.vs_in3[z] = s.vs_plane[...]
+        total = s.vs_in3[0]
+        for zz in range(1, zs):
+            total = total + s.vs_in3[zz]
+        s.vs_all[...] = total
+        s.vs_all[4:6, :] = jnp.zeros((2, p.dl), FULL)
+
+        @pl.loop(0, p.lat // 64)
+        def _(i):
+            rows = at(i * 64, 64)
+            normed, scale = ln_parts(s.lat[rows, :].astype(FULL))
+            grad = s.dmid[rows, :]
+            s.vs_all[4:5, :] += columns_sum(grad * normed)
+            s.vs_all[5:6, :] += columns_sum(grad)
+            s.slope[rows, :] = ln_grad(grad, gain_lat, normed, scale)
+
+        stores.append(cp.local(s.slope.at[at(z * (p.lat // zs), p.lat // zs, 16), :], glat_out))
+        stores.append(cp.local(s.vs_all, vec_out))
+
+    wq.first()
+    wk.first()
+    normed_bytes()
+    lat.first()
+    lat.second()
+    turned_bytes()
+    wk.second()
+    wq.second()
+    wk.third()
+    wq.third()
+    wk.ready()
+    wv.first()
+    wo.hop(1)
+    make_keys()
+    wq.ready()
+    lat.third()
+    wu.hop(0)
+    lat.ready()
+    normed_latents()
+    make_queries()
+    wo.hop(2)
+    wv.second()
+    make_scores()
+    wd.hop(0)
+    wo.first()
+    wv.third()
+    get_max()
+    wu.hop(1)
+    wv.ready()
+    make_values()
+    wo.second()
+    wu.hop(2)
+    partial_other()
+    partial_own()
+    chip_numer()
+    wd.hop(1)
+    wu.first()
+    wo.third()
+    turned_weights()
+    chip_pass()
+    wu.second()
+    wd.hop(2)
+    make_scale()
+    make_att()
+    att_pass()
+    wu.third()
+    share_inverse()
+    wo.ready()
+    wd.first()
+    get_att()
+    make_hidden()
+    make_mid()
+    wu.ready()
+    make_act()
+    wd.third()
+    down_grads()
+    wd.ready()
+    make_dup()
+    make_dmid()
+    make_dhid()
+    make_datt()
+    make_delta()
+    values_own()
+    values_other()
+    value_weights()
+    down.add()
+    upper_grads()
+    value_weights_own()
+    value_chunks()
+    scores_own()
+    scores_other()
+    value_grads.middle(0)
+    value_grads.middle(1)
+    dq_chip()
+    key_weights()
+    value_grads.add(0)
+    down.spread()
+    value_grads.add(1)
+    key_chunks()
+    outer_grads()
+    down.halve()
+    key_grads.middle(0)
+    dq_pass()
     upper.add()
-
-    @pl.loop(0, tiles)
-    def _(i):
-        tile = at(i * 256, 256)
-        s.res[:, tile] = (s.hid[:, tile] + matmul(s.act[own, :], s.wd[:, tile])).astype(LOW)
-
-    res_pair = cp.group()
-    cp.send(res_pair, s.res, res_out.at[own, :], core, z)
-    cp.sent(res_pair, s.res)
-    stores.append(cp.local(s.res, res_out.at[own, :]))
-
-    for grads in kv:
-        grads.finish()
-    cp.got(vs_pairs[1], s.vs_in2.at[0:3])
-    s.vs_in2[q] = s.vs_chip[...]
-    parts = s.vs_in2
-    total = (parts[0] + parts[1]) + (parts[2] + parts[3])
-    row_ids = lax.broadcasted_iota(jnp.int32, (8, p.dl), 0)
-    s.vs_plane[...] = jnp.where(row_ids < 2, s.vs_chip[...], total)
-    for peer in zed:
-        cp.send(vs_pairs[2], s.vs_plane, s.vs_in3.at[z], c, peer)
-    cp.sent(vs_pairs[2], s.vs_in3.at[0 : zs - 1])
-    cp.got(dq_pairs[2], s.dq_in3.at[0 : zs - 1])
-    s.dq_in3[z] = s.dq_plane[...]
-    parts = s.dq_in3
-    total = parts[0].astype(FULL)
-    for zz in range(1, zs):
-        total = total + parts[zz].astype(FULL)
-    own_half = at(h * qhalf, qhalf)
-    s.dq_all[:, own_half] = total.astype(LOW)
-    cp.send(dq_pairs[3], s.dq_all.at[:, own_half], s.dq_all.at[:, own_half], core, z)
-    cp.sent(dq_pairs[3], s.dq_in1)
+    key_grads.middle(1)
+    byte_part(0)
+    byte_part(1)
+    byte_part(2)
+    byte_part(3)
+    byte_store()
+    key_grads.add(0)
+    key_grads.add(1)
+    dq_plane()
+    upper.spread()
+    value_grads.finish()
+    value_grads.spread()
+    make_result()
+    vs_chip()
     outer.add()
+    upper.halve()
+    key_grads.finish()
+    value_grads.halve()
     latents.add()
-    upper.spread()
-    reduces = (down, upper, outer, latents)
-    for grads in kv:
-        grads.spread()
-    cp.got(dq_pairs[3], s.dq_in1)
-
-    @pl.loop(0, tiles)
-    def _(i):
-        tile = at(i * 256, 256)
-        s.gq[tile, :] = matmul_tn(s.nlat[:, tile], s.dq_all[...])
-        s.dmid[:, tile] = matmul_nt(s.dq_all[...], s.wq[tile, :])
-
-    stores.append(cp.local(s.gq.at[at(z * (p.dl // zs), p.dl // zs, 16), :], gq_out))
-    cp.got(vs_pairs[2], s.vs_in3.at[0 : zs - 1])
-    s.vs_in3[z] = s.vs_plane[...]
-    total = s.vs_in3[0]
-    for zz in range(1, zs):
-        total = total + s.vs_in3[zz]
-    s.vs_all[...] = total
-    s.vs_all[4:6, :] = jnp.zeros((2, p.dl), FULL)
-
-    @pl.loop(0, p.lat // 64)
-    def _(i):
-        rows = at(i * 64, 64)
-        normed, scale = ln_parts(s.lat[rows, :].astype(FULL))
-        grad = s.dmid[rows, :]
-        s.vs_all[4:5, :] += columns_sum(grad * normed)
-        s.vs_all[5:6, :] += columns_sum(grad)
-        s.slope[rows, :] = ln_grad(grad, gain_lat, normed, scale)
-
-    stores.append(cp.local(s.slope.at[at(z * (p.lat // zs), p.lat // zs, 16), :], glat_out))
-    stores.append(cp.local(s.vs_all, vec_out))
+    vs_plane()
     outer.spread()
+    key_grads.spread()
+    dq_total()
     latents.spread()
-    for reduce in (*reduces, *kv):
-        reduce.done()
+    query_grads()
+    key_grads.halve()
+    outer.halve()
+    latents.halve()
+    latent_grads()
+    for part in (*reduces, *kv):
+        part.done()
     cp.got(res_pair, s.res)
     for store in stores:
         store.wait()

time: 162 us -> 156 us (0.963)
  Pallas kernels: 160 us -> 155 us
    pallas_call x1, Pallas kernels: 154 us -> 148 us  [fused(): pl.pallas_call(functools.partial(fused_kernel, p, tuple(table)), out_shap...]
where the time goes in v4:
time: 156 us; the launch traced here: 155 us
  Pallas kernels  155 us (99%)
    pallas_call x1, Pallas kernels, fused(): pl.pallas_call(functools.partial(fused_kernel, p, tuple(table)), out_shap...  148 us
    pallas_call x1, Pallas kernels, fused(): pl.pallas_call(functools.partial(finish_kernel, p), out_shape=tuple((stru...  6.43 us

profile of v4, /device:TPU:0, one launch (start us, length us, event | category | flops | bytes accessed | tf_op | source)
XLA Modules:
  0.0 155.5 jit_solution(146410188472663452)
XLA Ops:
  0.7 148.4 %block.1 = (bf16[512,1280]{1,0:T(8,128)(2,1)}, bf16[512,768]{1,0:T(8,128)(2,1)}, bf16[320,1280]{1,0:T(8,128)(2,1)}, bf16[320,1280]{1,0:T(8,128)(2,1)}, bf16[320,...) custom-call(s32[2]{0:T(128)} %refs_0_.1, ...), custom_call_target="tpu_custom_call" | custom-call | tf_op jit(solution)/shard_map/block/pallas_call | solution.py:1317
  149.0 6.4 %finish.1 = (bf16[512,1280]{1,0:T(8,128)(2,1)}, bf16[512,768]{1,0:T(8,128)(2,1)}, f32[64,1280]{1,0:T(8,128)}, f32[320]{0:T(512)}, f32[320]{0:T(512)}, /*index=5*...) custom-call(bf16[512,1280]{1,0:T(8,128)(2,1)} %get-tuple-element.41., ...), custom_call_target="tpu_custom_call" | custom-call | tf_op jit(solution)/shard_map/finish/pallas_call | solution.py:1350

commit v5 on v4

--- a/solution.py
+++ b/solution.py
@@ -551,7 +551,7 @@
             s.keys_t[:, rows] = low.T
 
     def normed_latents():
-        @pl.loop(0, p.lat // 64)
+        @pl.loop(0, p.lat // 64, unroll=2)
         def _(i):
             rows = at(i * 64, 64)
             normed, _ = ln_parts(s.lat[rows, :].astype(FULL))
@@ -570,7 +570,7 @@
         s.stat[...] = jnp.zeros_like(s.stat)
         for seq in range(p.seqs):
 
-            @pl.loop(0, H)
+            @pl.loop(0, H, unroll=4)
             def _(head):
                 raw = matmul_nt(
                     s.qmask[at(head * p.lat, p.lat), :], s.keys[seq * p.slots : (seq + 1) * p.slots, :]
@@ -588,7 +588,7 @@
         cp.sent(max_pair, s.max_in.at[0 : ctx - 1])
 
     def make_values():
-        @pl.loop(0, p.vd // 256)
+        @pl.loop(0, p.vd // 256, unroll=True)
         def _(i):
             tile = at(i * 256, 256)
             s.values[:, tile] = matmul(s.nin[...], s.wv[:, tile]).astype(LOW)
@@ -607,7 +607,7 @@
     def partial(seq):
         s.numer[...] = jnp.zeros_like(s.numer)
 
-        @pl.loop(0, H)
+        @pl.loop(0, H, unroll=4)
         def _(head):
             i = seq * H + head
             lane = lanes(p.lat, 128)
@@ -661,7 +661,7 @@
     def turned_weights():
         for seq in range(p.seqs):
 
-            @pl.loop(0, H)
+            @pl.loop(0, H, unroll=4)
             def _(head):
                 i = seq * H + head
                 raw = matmul_nt(
@@ -719,13 +719,13 @@
         share(s.att)
 
     def make_hidden():
-        @pl.loop(0, tiles)
+        @pl.loop(0, tiles, unroll=True)
         def _(i):
             tile = at(i * 256, 256)
             s.hid[:, tile] = s.lat[:, tile].astype(FULL) + matmul(s.att[own, :], s.wo[:, tile])
 
     def make_mid():
-        @pl.loop(0, p.lat // 64)
+        @pl.loop(0, p.lat // 64, unroll=2)
         def _(i):
             normed, _ = ln_parts(s.hid[at(i * 64, 64), :])
             s.mid[at(h * p.lat + i * 64, 64), :] = (normed * gain_mlp + bias_mlp).astype(LOW)
@@ -735,7 +735,7 @@
     def make_act():
         load_cot.wait()
 
-        @pl.loop(0, tiles)
+        @pl.loop(0, tiles, unroll=True)
         def _(i):
             tile = at(i * 256, 256)
             up = matmul(s.mid[own, :], s.wu[:, tile])
@@ -755,7 +755,7 @@
             self.pairs = [cp.group() for _ in range(4)]
 
         def product(self):
-            @pl.loop(0, self.grads.shape[0] // 256)
+            @pl.loop(0, self.grads.shape[0] // 256, unroll=True)
             def _(i):
                 rows = at(i * 256, 256)
                 self.grads[rows, :] = matmul_tn(self.left[:, rows], self.right[:, half_cols]).astype(LOW)
@@ -826,7 +826,7 @@
         latents.scatter()
 
     def make_dup():
-        @pl.loop(0, tiles)
+        @pl.loop(0, tiles, unroll=True)
         def _(i):
             tile = at(i * 256, 256)
             dact = matmul_nt(s.cot[own, :], s.wd[tile, :])
@@ -835,7 +835,7 @@
         share(s.dup)
 
     def make_dmid():
-        @pl.loop(0, tiles)
+        @pl.loop(0, tiles, unroll=True)
         def _(i):
             tile = at(i * 256, 256)
             s.dmid[:, tile] = matmul_nt(s.dup[own, :], s.wu[tile, :])
@@ -843,7 +843,7 @@
     def make_dhid():
         s.vs[...] = jnp.zeros_like(s.vs)
 
-        @pl.loop(0, p.lat // 64)
+        @pl.loop(0, p.lat // 64, unroll=2)
         def _(i):
             rows = at(i * 64, 64)
             full_rows = at(h * p.lat + i * 64, 64)
@@ -863,7 +863,7 @@
         cp.sent(stats_pairs[0], s.stats.at[0, 0:H])
 
     def make_datt():
-        @pl.loop(0, tiles)
+        @pl.loop(0, tiles, unroll=True)
         def _(i):
             tile = at(i * 256, 256)
             s.datt[own, tile] = matmul_nt(s.dhid[own, :], s.wo[tile, :]).astype(LOW)
@@ -873,7 +873,7 @@
     def make_delta():
         s.stat[...] = jnp.zeros_like(s.stat)
 
-        @pl.loop(0, H)
+        @pl.loop(0, H, unroll=4)
         def _(head):
             cols, low_lane = window(head)
             product = s.datt[own, cols].astype(FULL) * s.att[own, cols].astype(FULL)
@@ -889,7 +889,7 @@
         latent_rows = at(seq * p.lat, p.lat)
         s.numer[...] = jnp.zeros_like(s.numer)
 
-        @pl.loop(0, H)
+        @pl.loop(0, H, unroll=4)
         def _(head):
             cols, low_lane = window(head)
             inverse = s.stats[seq, pl.ds(head, 1), :]
@@ -904,7 +904,7 @@
         latent_rows = at(seq * p.lat, p.lat)
         s.dk_sum[...] = jnp.zeros_like(s.dk_sum)
 
-        @pl.loop(0, H)
+        @pl.loop(0, H, unroll=4)
         def _(head):
             heads = at(head * p.lat, p.lat)
             cols, low_lane = window(head)
@@ -923,7 +923,7 @@
     def weight_grads(ref, grad, width, side):
         cols = at(side * width, width)
 
-        @pl.loop(0, p.din // 256)
+        @pl.loop(0, p.din // 256, unroll=True)
         def _(i):
             rows = at(i * 256, 256)
             ref[side, rows, :] = matmul(s.nin_t[rows, :], grad[:, cols]).astype(LOW)
@@ -1011,11 +1011,21 @@
 
     key_grads = Local(s.swk, s.rwk, s.cwk, s.pwk_in, s.pwk, s.zwk_in, s.fwk, gk)
     value_grads = Local(s.swv, s.rwv, s.cwv, s.pwv_in, s.pwv, s.zwv_in, s.fwv, gv)
+    def byte_matmul(seq):
+        rows = at(seq * p.slots, p.slots)
+        for tile in range(p.din // 256):
+            cols = slice(tile * 256, (tile + 1) * 256)
+            grad = matmul_nt(s.dkeys[rows, :], s.wk[cols, :]) + matmul_nt(s.dvalues[rows, :], s.wv[cols, :])
+            s.scores[at(tile * p.rows_in + seq * p.slots, p.slots), :] = grad
+
     def byte_part(part):
-        @pl.loop(part * 2, part * 2 + 2)
+        byte_matmul(part)
+
+        @pl.loop(part * p.slots // 64, (part + 1) * p.slots // 64, unroll=2)
         def _(i):
             rows = at(i * 64, 64)
-            grad = matmul_nt(s.dkeys[rows, :], s.wk[...]) + matmul_nt(s.dvalues[rows, :], s.wv[...])
+            tiles_in = [s.scores[at(k * p.rows_in + i * 64, 64), :] for k in range(p.din // 256)]
+            grad = jnp.concatenate(tiles_in, axis=1)
             normed, scale = ln_parts(s.feats[rows, :].astype(FULL))
             s.vs[2:3, 0 : p.din] += columns_sum(grad * normed)
             s.vs[3:4, 0 : p.din] += columns_sum(grad)
@@ -1101,7 +1111,7 @@
         cp.sent(vs_pairs[1], s.vs_in2.at[0:3])
 
     def make_result():
-        @pl.loop(0, tiles)
+        @pl.loop(0, tiles, unroll=True)
         def _(i):
             tile = at(i * 256, 256)
             s.res[:, tile] = (s.hid[:, tile] + matmul(s.act[own, :], s.wd[:, tile])).astype(LOW)
@@ -1135,7 +1145,7 @@
     def query_grads():
         cp.got(dq_pairs[3], s.dq_in1)
 
-        @pl.loop(0, tiles)
+        @pl.loop(0, tiles, unroll=True)
         def _(i):
             tile = at(i * 256, 256)
             s.gq[tile, :] = matmul_tn(s.nlat[:, tile], s.dq_all[...])
@@ -1152,7 +1162,7 @@
         s.vs_all[...] = total
         s.vs_all[4:6, :] = jnp.zeros((2, p.dl), FULL)
 
-        @pl.loop(0, p.lat // 64)
+        @pl.loop(0, p.lat // 64, unroll=2)
         def _(i):
             rows = at(i * 64, 64)
             normed, scale = ln_parts(s.lat[rows, :].astype(FULL))
@@ -1251,8 +1261,6 @@
     key_grads.middle(1)
     byte_part(0)
     byte_part(1)
-    byte_part(2)
-    byte_part(3)
     byte_store()
     key_grads.add(0)
     key_grads.add(1)

time: 156 us -> 146 us (0.936)
  Pallas kernels: 155 us -> 145 us
    pallas_call x1, Pallas kernels: 148 us -> 139 us  [fused(): pl.pallas_call(functools.partial(fused_kernel, p, tuple(table)), out_shap...]
where the time goes in v5:
time: 146 us
  Pallas kernels  145 us (99%)
    pallas_call x1, Pallas kernels, fused(): pl.pallas_call(functools.partial(fused_kernel, p, tuple(table)), out_shap...  139 us
    pallas_call x1, Pallas kernels, fused(): pl.pallas_call(functools.partial(finish_kernel, p), out_shape=tuple((stru...  6.43 us

profile of v5, /device:TPU:0, one launch (start us, length us, event | category | flops | bytes accessed | tf_op | source)
XLA Modules:
  0.0 146.1 jit_solution(1224726296917382919)
XLA Ops:
  0.7 139.0 %block.1 = (bf16[512,1280]{1,0:T(8,128)(2,1)}, bf16[512,768]{1,0:T(8,128)(2,1)}, bf16[320,1280]{1,0:T(8,128)(2,1)}, bf16[320,1280]{1,0:T(8,128)(2,1)}, bf16[320,...) custom-call(s32[2]{0:T(128)} %refs_0_.1, ...), custom_call_target="tpu_custom_call" | custom-call | tf_op jit(solution)/shard_map/block/pallas_call | solution.py:1325
  139.7 6.4 %finish.1 = (bf16[512,1280]{1,0:T(8,128)(2,1)}, bf16[512,768]{1,0:T(8,128)(2,1)}, f32[64,1280]{1,0:T(8,128)}, f32[320]{0:T(512)}, f32[320]{0:T(512)}, /*index=5*...) custom-call(bf16[512,1280]{1,0:T(8,128)(2,1)} %get-tuple-element.41., ...), custom_call_target="tpu_custom_call" | custom-call | tf_op jit(solution)/shard_map/finish/pallas_call | solution.py:1358

commit v6 on v5

--- a/solution.py
+++ b/solution.py
@@ -1174,61 +1174,61 @@
         stores.append(cp.local(s.slope.at[at(z * (p.lat // zs), p.lat // zs, 16), :], glat_out))
         stores.append(cp.local(s.vs_all, vec_out))
 
+    normed_bytes()
+    wk.first()
+    turned_bytes()
+    wk.second()
     wq.first()
-    wk.first()
-    normed_bytes()
+    wk.third()
+    wu.hop(0)
+    wq.second()
     lat.first()
     lat.second()
-    turned_bytes()
-    wk.second()
-    wq.second()
-    wk.third()
+    wo.hop(1)
+    wv.first()
     wq.third()
     wk.ready()
-    wv.first()
-    wo.hop(1)
-    make_keys()
     wq.ready()
     lat.third()
-    wu.hop(0)
     lat.ready()
     normed_latents()
+    make_keys()
+    wv.second()
     make_queries()
     wo.hop(2)
-    wv.second()
     make_scores()
     wd.hop(0)
     wo.first()
     wv.third()
-    get_max()
     wu.hop(1)
     wv.ready()
+    wo.second()
+    get_max()
     make_values()
-    wo.second()
+    partial_other()
     wu.hop(2)
-    partial_other()
     partial_own()
     chip_numer()
     wd.hop(1)
     wu.first()
     wo.third()
+    wd.hop(2)
     turned_weights()
     chip_pass()
+    make_scale()
+    wo.ready()
     wu.second()
-    wd.hop(2)
-    make_scale()
     make_att()
     att_pass()
     wu.third()
-    share_inverse()
-    wo.ready()
     wd.first()
     get_att()
     make_hidden()
+    wu.ready()
     make_mid()
-    wu.ready()
     make_act()
     wd.third()
+    share_inverse()
     down_grads()
     wd.ready()
     make_dup()
@@ -1239,50 +1239,50 @@
     values_own()
     values_other()
     value_weights()
+    upper_grads()
     down.add()
-    upper_grads()
     value_weights_own()
     value_chunks()
     scores_own()
     scores_other()
     value_grads.middle(0)
+    byte_part(0)
+    dq_chip()
     value_grads.middle(1)
-    dq_chip()
+    value_grads.add(0)
     key_weights()
-    value_grads.add(0)
     down.spread()
+    key_chunks()
     value_grads.add(1)
-    key_chunks()
     outer_grads()
     down.halve()
     key_grads.middle(0)
-    dq_pass()
     upper.add()
     key_grads.middle(1)
-    byte_part(0)
     byte_part(1)
-    byte_store()
+    dq_pass()
     key_grads.add(0)
+    upper.spread()
     key_grads.add(1)
     dq_plane()
-    upper.spread()
     value_grads.finish()
     value_grads.spread()
-    make_result()
+    byte_store()
+    value_grads.halve()
     vs_chip()
     outer.add()
+    key_grads.finish()
+    make_result()
+    latents.add()
     upper.halve()
-    key_grads.finish()
-    value_grads.halve()
-    latents.add()
-    vs_plane()
     outer.spread()
     key_grads.spread()
+    vs_plane()
+    latents.spread()
     dq_total()
-    latents.spread()
     query_grads()
+    outer.halve()
     key_grads.halve()
-    outer.halve()
     latents.halve()
     latent_grads()
     for part in (*reduces, *kv):
@@ -1293,20 +1293,47 @@
     cp.drain()
 
 
-def finish_kernel(p, res, byte, go, gu, gd, gv, gk, gl, gq, glat, vec, *outs):
+def finish_kernel(p, *refs):
+    ins, outs, scratch = refs[:11], refs[11:26], refs[26:]
+    held, wide, sems = scratch[:11], scratch[11:17], scratch[17]
     z = lax.axis_index("wshard")
-    outs[0][...] = res[...]
-    outs[1][...] = byte[...]
-    outs[2][...] = glat[...] + gl[...].astype(FULL)
+    order = (10, 2, 3, 4, 5, 0, 1, 7, 9, 8, 6)
+    loads = {n: pltpu.make_async_copy(ins[n], held[n], sems.at[n]) for n in order}
+    for load in loads.values():
+        load.start()
+    stores = []
+
+    def store(ref, out):
+        copy = pltpu.make_async_copy(ref, outs[out], sems.at[11 + out])
+        copy.start()
+        stores.append(copy)
+
+    loads[10].wait()
+    vec = held[10]
     for out, row in ((3, 4), (4, 5), (5, 2), (6, 3), (11, 0), (12, 1)):
         size = outs[out].shape[0]
         picked = vec[row : row + 1, 0:size]
         for zz in range(1, p.zs):
             picked = jnp.where(z == zz, vec[row : row + 1, zz * size : (zz + 1) * size], picked)
         outs[out][...] = picked.reshape(size)
-    outs[7][...] = gq[...]
-    for out, source in ((8, gk), (9, gv), (10, go), (13, gu), (14, gd)):
-        outs[out][...] = source[...].astype(FULL)
+    for n, out, slot in ((2, 10, 0), (3, 13, 1), (4, 14, 2), (5, 9, 3)):
+        loads[n].wait()
+        wide[slot][...] = held[n][...].astype(FULL)
+        store(wide[slot], out)
+    for n, out in ((0, 0), (1, 1)):
+        loads[n].wait()
+        store(held[n], out)
+    loads[7].wait()
+    loads[9].wait()
+    wide[5][...] = held[9][...] + held[7][...].astype(FULL)
+    store(wide[5], 2)
+    loads[8].wait()
+    store(held[8], 7)
+    loads[6].wait()
+    wide[4][...] = held[6][...].astype(FULL)
+    store(wide[4], 8)
+    for copy in stores:
+        copy.wait()
 
 
 def fused(*args):
@@ -1358,8 +1385,11 @@
     outs = pl.pallas_call(
         functools.partial(finish_kernel, p),
         out_shape=tuple(struct(shape, kind) for shape, kind in shapes),
-        in_specs=[in_vmem] * 11,
-        out_specs=(in_vmem,) * 15,
+        in_specs=[anywhere] * 11,
+        out_specs=tuple(in_vmem if len(shape) == 1 else anywhere for shape, _ in shapes),
+        scratch_shapes=[pltpu.VMEM(one.shape, one.dtype) for one in made]
+        + [pltpu.VMEM(shapes[n][0], FULL) for n in (10, 13, 14, 9, 8, 2)]
+        + [pltpu.SemaphoreType.DMA((26,))],
         compiler_params=pltpu.CompilerParams(vmem_limit_bytes=60 * 2**20),
         name="finish",
     )(*made)

time: 146 us -> 141 us (0.966)
  Pallas kernels: 145 us -> 140 us
    pallas_call x1, Pallas kernels: 139 us -> 134 us  [fused(): pl.pallas_call(functools.partial(fused_kernel, p, tuple(table)), out_shap...]
where the time goes in v6:
time: 141 us
  Pallas kernels  140 us (99%)
    pallas_call x1, Pallas kernels, fused(): pl.pallas_call(functools.partial(fused_kernel, p, tuple(table)), out_shap...  134 us
    pallas_call x1, Pallas kernels, fused(): pl.pallas_call(functools.partial(finish_kernel, p), out_shape=tuple((stru...  5.55 us

profile of v6, /device:TPU:0, one launch (start us, length us, event | category | flops | bytes accessed | tf_op | source)
XLA Modules:
  0.0 140.6 jit_solution(1886607012303212645)
XLA Ops:
  0.7 134.2 %block.1 = (bf16[512,1280]{1,0:T(8,128)(2,1)}, bf16[512,768]{1,0:T(8,128)(2,1)}, bf16[320,1280]{1,0:T(8,128)(2,1)}, bf16[320,1280]{1,0:T(8,128)(2,1)}, bf16[320,...) custom-call(s32[2]{0:T(128)} %refs_0_.1, ...), custom_call_target="tpu_custom_call" | custom-call | tf_op jit(solution)/shard_map/block/pallas_call | solution.py:1352
  134.9 5.5 %finish.1 = (bf16[512,1280]{1,0:T(8,128)(2,1)}, bf16[512,768]{1,0:T(8,128)(2,1)}, f32[64,1280]{1,0:T(8,128)}, f32[320]{0:T(512)}, f32[320]{0:T(512)}, /*index=5*...) custom-call(bf16[512,1280]{1,0:T(8,128)(2,1)} %get-tuple-element.41., ...), custom_call_target="tpu_custom_call" | custom-call | tf_op jit(solution)/shard_map/finish/pallas_call | solution.py:1385

commit v7 on v6

--- a/solution.py
+++ b/solution.py
@@ -383,11 +383,11 @@
         pl.semaphore_signal(barrier, inc=1, device_id=(peer, z), device_id_type=pl.DeviceIdType.MESH)
     for peer in zed:
         pl.semaphore_signal(barrier, inc=1, device_id=(c, peer), device_id_type=pl.DeviceIdType.MESH)
-    pl.semaphore_wait(barrier, ctx - 1 + zs - 1)
 
     load_feats = cp.local(feats_in, s.feats)
     for row, ref in enumerate(smalls):
         s.small_own[row : row + 1, 0 : ref.shape[0]] = ref[...].reshape(1, -1).astype(FULL)
+    pl.semaphore_wait(barrier, ctx - 1 + zs - 1)
     small_pair = cp.group()
     for peer in zed:
         cp.send(small_pair, s.small_own, s.small.at[z], c, peer)
@@ -551,7 +551,7 @@
             s.keys_t[:, rows] = low.T
 
     def normed_latents():
-        @pl.loop(0, p.lat // 64, unroll=2)
+        @pl.loop(0, p.lat // 64, unroll=True)
         def _(i):
             rows = at(i * 64, 64)
             normed, _ = ln_parts(s.lat[rows, :].astype(FULL))
@@ -725,7 +725,7 @@
             s.hid[:, tile] = s.lat[:, tile].astype(FULL) + matmul(s.att[own, :], s.wo[:, tile])
 
     def make_mid():
-        @pl.loop(0, p.lat // 64, unroll=2)
+        @pl.loop(0, p.lat // 64, unroll=True)
         def _(i):
             normed, _ = ln_parts(s.hid[at(i * 64, 64), :])
             s.mid[at(h * p.lat + i * 64, 64), :] = (normed * gain_mlp + bias_mlp).astype(LOW)
@@ -843,7 +843,7 @@
     def make_dhid():
         s.vs[...] = jnp.zeros_like(s.vs)
 
-        @pl.loop(0, p.lat // 64, unroll=2)
+        @pl.loop(0, p.lat // 64, unroll=True)
         def _(i):
             rows = at(i * 64, 64)
             full_rows = at(h * p.lat + i * 64, 64)
@@ -873,7 +873,7 @@
     def make_delta():
         s.stat[...] = jnp.zeros_like(s.stat)
 
-        @pl.loop(0, H, unroll=4)
+        @pl.loop(0, H, unroll=True)
         def _(head):
             cols, low_lane = window(head)
             product = s.datt[own, cols].astype(FULL) * s.att[own, cols].astype(FULL)
@@ -889,7 +889,7 @@
         latent_rows = at(seq * p.lat, p.lat)
         s.numer[...] = jnp.zeros_like(s.numer)
 
-        @pl.loop(0, H, unroll=4)
+        @pl.loop(0, H, unroll=True)
         def _(head):
             cols, low_lane = window(head)
             inverse = s.stats[seq, pl.ds(head, 1), :]
@@ -904,7 +904,7 @@
         latent_rows = at(seq * p.lat, p.lat)
         s.dk_sum[...] = jnp.zeros_like(s.dk_sum)
 
-        @pl.loop(0, H, unroll=4)
+        @pl.loop(0, H, unroll=True)
         def _(head):
             heads = at(head * p.lat, p.lat)
             cols, low_lane = window(head)
@@ -1162,7 +1162,7 @@
         s.vs_all[...] = total
         s.vs_all[4:6, :] = jnp.zeros((2, p.dl), FULL)
 
-        @pl.loop(0, p.lat // 64, unroll=2)
+        @pl.loop(0, p.lat // 64, unroll=True)
         def _(i):
             rows = at(i * 64, 64)
             normed, scale = ln_parts(s.lat[rows, :].astype(FULL))
@@ -1187,24 +1187,24 @@
     wo.hop(1)
     wv.first()
     wq.third()
-    wk.ready()
     wq.ready()
     lat.third()
+    wk.ready()
     lat.ready()
+    make_keys()
     normed_latents()
-    make_keys()
     wv.second()
     make_queries()
     wo.hop(2)
     make_scores()
+    wu.hop(1)
     wd.hop(0)
     wo.first()
     wv.third()
-    wu.hop(1)
     wv.ready()
     wo.second()
+    make_values()
     get_max()
-    make_values()
     partial_other()
     wu.hop(2)
     partial_own()
@@ -1216,19 +1216,19 @@
     turned_weights()
     chip_pass()
     make_scale()
-    wo.ready()
     wu.second()
     make_att()
+    wo.ready()
     att_pass()
     wu.third()
     wd.first()
     get_att()
+    wu.ready()
+    share_inverse()
     make_hidden()
-    wu.ready()
     make_mid()
     make_act()
     wd.third()
-    share_inverse()
     down_grads()
     wd.ready()
     make_dup()
@@ -1252,37 +1252,37 @@
     value_grads.add(0)
     key_weights()
     down.spread()
+    value_grads.add(1)
     key_chunks()
-    value_grads.add(1)
     outer_grads()
     down.halve()
+    upper.add()
     key_grads.middle(0)
-    upper.add()
+    dq_pass()
     key_grads.middle(1)
     byte_part(1)
-    dq_pass()
     key_grads.add(0)
+    key_grads.add(1)
+    value_grads.finish()
     upper.spread()
-    key_grads.add(1)
+    value_grads.spread()
     dq_plane()
-    value_grads.finish()
-    value_grads.spread()
     byte_store()
     value_grads.halve()
+    outer.add()
     vs_chip()
-    outer.add()
     key_grads.finish()
+    upper.halve()
     make_result()
     latents.add()
-    upper.halve()
     outer.spread()
     key_grads.spread()
     vs_plane()
+    dq_total()
     latents.spread()
-    dq_total()
-    query_grads()
     outer.halve()
     key_grads.halve()
+    query_grads()
     latents.halve()
     latent_grads()
     for part in (*reduces, *kv):

time: 141 us -> 140 us (level)
  no operation moved by 1% of the time
where the time goes in v7:
time: 140 us
  Pallas kernels  139 us (99%)
    pallas_call x1, Pallas kernels, fused(): pl.pallas_call(functools.partial(fused_kernel, p, tuple(table)), out_shap...  134 us
    pallas_call x1, Pallas kernels, fused(): pl.pallas_call(functools.partial(finish_kernel, p), out_shape=tuple((stru...  5.55 us

profile of v7, /device:TPU:0, one launch (start us, length us, event | category | flops | bytes accessed | tf_op | source)
XLA Modules:
  0.0 140.1 jit_solution(16787594160119765642)
XLA Ops:
  0.7 133.7 %block.1 = (bf16[512,1280]{1,0:T(8,128)(2,1)}, bf16[512,768]{1,0:T(8,128)(2,1)}, bf16[320,1280]{1,0:T(8,128)(2,1)}, bf16[320,1280]{1,0:T(8,128)(2,1)}, bf16[320,...) custom-call(s32[2]{0:T(128)} %refs_0_.1, ...), custom_call_target="tpu_custom_call" | custom-call | tf_op jit(solution)/shard_map/block/pallas_call | solution.py:1352
  134.4 5.5 %finish.1 = (bf16[512,1280]{1,0:T(8,128)(2,1)}, bf16[512,768]{1,0:T(8,128)(2,1)}, f32[64,1280]{1,0:T(8,128)}, f32[320]{0:T(512)}, f32[320]{0:T(512)}, /*index=5*...) custom-call(bf16[512,1280]{1,0:T(8,128)(2,1)} %get-tuple-element.41., ...), custom_call_target="tpu_custom_call" | custom-call | tf_op jit(solution)/shard_map/finish/pallas_call | solution.py:1385
